TPU v7x, 256 devices: a whole 4x4x8 slice. The times are simulated.
256 devices in a mesh: row: 16 (over z, core), col: 8 (over y, x_hi), pair: 2 (over x_lo).
Axes of the slice: x: 4 (x_hi: 2, x_lo: 2; x = x_hi * 2 + x_lo), y: 4, z: 8, core: 2. Of those that a mesh axis runs over, the one named last changes fastest.
Arguments:
- amplitudes: bfloat16 [320, 8, 320], P('row', 'pair', 'col'), may hold values from -6 to 6
- factors: bfloat16 [2048, 320, 320], P(('row', 'col', 'pair')), may hold values from -0.125 to 0.125
- vir_irrep: int32 [320], replicated, may hold values from 0 to 7, never falling along the last dimension, each value on 1 to 80 neighbouring positions
- pair_irrep: int32 [8], P('pair'), may hold values from 0 to 7
Outputs:
- ladder_term: float32 [320, 8, 320], P('row', 'pair', 'col')
Inputs may be any that keep to these rules, and one draw needn't show every extreme that they name: `vir_irrep`: labels never fall along the virtual index, so each label holds one contiguous block of virtuals.
All inputs are finite; a program needn't handle non-finite values.
Results may differ from a plain program's by a relative error of at most 0.0025.
Values may be sent and summed in bfloat16 or wider, within the bound.
No kernel may reach another device: no remote copies, remote signals or barrier semaphores. Data moves between devices by JAX's collectives and lax.ppermute only.
A program may use at most 64 MiB of HBM per device.

v0:
```python
import jax
import jax.numpy as jnp
from jax import lax
from jax.sharding import PartitionSpec as P


def ladder_step(amp_matrix, pairs_here, width):

    def one_factor(summed, factor):
        inner = jnp.dot(factor, amp_matrix, preferred_element_type=jnp.float32).astype(jnp.bfloat16)
        inner = inner.reshape(width * pairs_here, width)
        outer = lax.dot_general(
            inner, factor, (((1,), (1,)), ((), ())), preferred_element_type=jnp.float32
        )
        return (summed + outer.reshape(width, pairs_here, width), None)

    return one_factor


def reduce_blocks(stacked):
    first = lax.psum_scatter(stacked, "row", scatter_dimension=1, tiled=True)
    return lax.psum_scatter(first, "col", scatter_dimension=3, tiled=True)


def body(amplitudes, factors, vir_irrep, pair_irrep):
    row_block = amplitudes.shape[0]
    col_block = amplitudes.shape[2]
    pairs_here = amplitudes.shape[1]
    row_labels = lax.dynamic_slice_in_dim(vir_irrep, lax.axis_index("row") * row_block, row_block)
    col_labels = lax.dynamic_slice_in_dim(vir_irrep, lax.axis_index("col") * col_block, col_block)
    mixed = jnp.bitwise_xor(row_labels[:, None, None], col_labels[None, None, :])
    allowed = mixed == pair_irrep[None, :, None]
    sym_amp = jnp.where(allowed, amplitudes, jnp.zeros_like(amplitudes))
    across = lax.all_gather(sym_amp, "col", axis=2, tiled=True)
    whole = lax.all_gather(across, "row", axis=0, tiled=True)
    width = whole.shape[0]
    amp_matrix = whole.reshape(width, pairs_here * width)
    one_factor = ladder_step(amp_matrix, pairs_here, width)
    start_sum = jnp.zeros((width, pairs_here, width), jnp.float32)
    partial_value = lax.scan(
        one_factor, start_sum, lax.all_gather(factors, "pair", axis=0, tiled=True)
    )[0]
    flipped = jnp.transpose(partial_value, (2, 1, 0))
    stacked = jnp.stack([partial_value, flipped])
    reduced = reduce_blocks(stacked)
    ladder = jnp.sum(reduced, axis=0)
    return jnp.where(allowed, ladder, jnp.zeros_like(ladder))


def solution(mesh):
    placed = (P("row", "pair", "col"), P(("row", "col", "pair"), None, None), P(), P("pair"))
    return jax.shard_map(
        body, mesh=mesh, in_specs=placed, out_specs=P("row", "pair", "col"), check_vma=False
    )
```

profile of v0, /device:TPU:1, one launch (start us, length us, event | category | flops | bytes accessed | tf_op | source)
XLA Modules:
  0.0 413.0 jit_solution(4099211249512327469)
XLA Ops:
  7.8 31.3 %all_gather.10 = bf16[20,4,320]{0,1,2:T(4,128)(2,1)S(1)} all-gather(bf16[20,4,40]{0,1,2:T(4,128)(2,1)S(1)} %copy.10), channel_id=1, replica_groups=mesh['row'=16,'col'=8,'pair'=2] {'col'}, dimensions={2}, use_global_device_ids=true | all-gather | bytes 57600 | tf_op jit(solution)/shard_map/all_gather | solution.py:34
  39.4 29.9 %all_gather.11 = bf16[320,4,320]{2,1,0:T(4,128)(2,1)S(1)} all-gather(bf16[20,4,320]{2,1,0:T(4,128)(2,1)S(1)} %copy.11), channel_id=1, replica_groups=mesh['row'=16,'col'=8,'pair'=2] {'row'}, dimensions={0}, use_global_device_ids=true | all-gather | bytes 870400 | tf_op jit(solution)/shard_map/all_gather | solution.py:35
  70.9 3.3 all-gather.2.cloned.1.call-done
  74.3 122.1 %while.11 = (s32[]{:T(128)}, f32[320,4,320]{2,0,1:T(8,128)S(1)}, bf16[16,320,320]{2,1,0:T(8,128)(2,1)}, bf16[320,1280]{1,0:T(8,128)(2,1)}, s32[]{:T(128)}, /*index=5*/s32[]{:T(128)}) while((s32[]{:T(128)}, f32[320,4,320]{2,0,1:T(8,128)S(1)}, bf16[16,320,320]{2,1,0:T(8,128)(2,1)}, bf16[320,1280]{1,0:T(8,128)(2,1)}, s32[]{:T(128)}, ...), condition=%wide.region_1.2_spmd.clone, body=%wide.region_0.1_spmd.clone.sunk | while | flops 525516800 | bytes 7865423 | solution.py:40
  74.3 2.8 convolution_convert_fusion.2
  77.1 2.5 dot_general.12
  79.6 2.3 select_add_fusion.2
  81.9 2.8 convolution_convert_fusion.2
  84.7 2.5 dot_general.12
  87.2 2.3 select_add_fusion.2
  89.5 2.8 convolution_convert_fusion.2
  92.3 2.5 dot_general.12
  94.9 2.3 select_add_fusion.2
  97.1 2.8 convolution_convert_fusion.2
  99.9 2.5 dot_general.12
  102.5 2.3 select_add_fusion.2
  104.8 2.8 convolution_convert_fusion.2
  107.6 2.5 dot_general.12
  110.1 2.3 select_add_fusion.2
  112.4 2.8 convolution_convert_fusion.2
  115.2 2.5 dot_general.12
  117.8 2.3 select_add_fusion.2
  120.0 2.8 convolution_convert_fusion.2
  122.8 2.5 dot_general.12
  127.7 2.8 convolution_convert_fusion.2
  130.5 2.5 dot_general.12
  133.0 2.3 select_add_fusion.2
  135.3 2.8 convolution_convert_fusion.2
  138.1 2.5 dot_general.12
  142.9 2.8 convolution_convert_fusion.2
  145.7 2.5 dot_general.12
  150.6 2.8 convolution_convert_fusion.2
  153.4 2.5 dot_general.12
  155.9 2.3 select_add_fusion.2
  158.2 2.8 convolution_convert_fusion.2
  161.0 2.5 dot_general.12
  165.8 2.8 convolution_convert_fusion.2
  168.6 2.5 dot_general.12
  173.4 2.8 convolution_convert_fusion.2
  176.2 2.5 dot_general.12
  178.8 2.3 select_add_fusion.2
  181.1 2.8 convolution_convert_fusion.2
  183.9 2.5 dot_general.12
  188.7 2.8 convolution_convert_fusion.2
  191.5 2.5 dot_general.12
  200.1 4.4 %copy.13 = f32[2,320,4,320]{3,2,0,1:T(4,128)} copy(f32[2,320,4,320]{3,1,2,0:T(8,128)S(1)} %pad_maximum_fusion) | data formatting | bytes 6553600 | tf_op jit(solution)/shard_map/stack | solution.py:44
  206.4 119.8 %all-reduce.3.cloned.1.call-done = f32[2,320,4,320]{3,2,0,1:T(4,128)} async-done(((f32[2,320,4,320]{3,2,0,1:T(4,128)}), f32[2,320,4,320]{3,2,0,1:T(4,128)}) %all-reduce.3.cloned.1.call-update) | async-done | bytes 3276816
  329.4 75.2 %reduce-scatter.4.cloned.1.call-done = f32[40,160]{1,0:T(8,128)} async-done(((f32[320,160]{1,0:T(8,128)}), f32[40,160]{1,0:T(8,128)}) %reduce-scatter.4.cloned.1.call-update) | async-done | bytes 25616
  (40 shorter events, 29.0 us)
Async XLA Ops:
  6.5 0.8 copy-start.2
  6.5 1.0 copy-start
  6.5 1.0 copy-start.1
  6.5 67.7 %all-gather.2.cloned.1.call-start = ((), (), s32[]{:S(2)}) async-start(), calls=%async_computation.1 | async-start | bytes 5898240 | tf_op jit(solution)/shard_map/all_gather | solution.py:41
  7.3 318.9 %all-reduce.3.cloned.1.call-start = ((), (), s32[]{:S(2)}) async-start(), calls=%async_computation.3 | async-start | bytes 7864320
  204.5 0.7 copy-start.3
  204.5 200.1 %reduce-scatter.4.cloned.1.call-start = ((), (), s32[]{:S(2)}) async-start(), calls=%async_computation.2 | async-start | bytes 368640
Sparse Core Ops, SparseCore 0:
  9.1 65.0 all-gather.1
  204.7 121.4 all-reduce.2
  330.0 74.5 reduce-scatter.3
where the time goes:
time: 415 us; the launch traced here: 413 us
  waiting for transfers between devices  199 us (48%)
  matrix products  80.9 us (19%)
  blocking collectives  61.2 us (15%)
  local copies, waits for them, and re-layouts  55.1 us (13%)
  between operations  13.8 us (3%)
    unnamed x5, waiting for transfers between devices  196 us
    dot_general x16, matrix products, one_factor(): jnp.dot(factor, amp_matrix, preferred_element_type=jnp.float32)  44.8 us
    dot_general x16, local copies, waits for them, and re-layouts, one_factor(): lax.dot_general(inner, factor, (((1,), (1,)), ((), ())), preferred_elemen...  40.6 us
    dot_general x16, matrix products, one_factor(): lax.dot_general(inner, factor, (((1,), (1,)), ((), ())), preferred_elemen...  36.2 us
    all_gather x1, blocking collectives, body(): across = lax.all_gather(sym_amp, 'col', axis=2, tiled=True)  31.3 us
    all_gather x1, blocking collectives, body(): whole = lax.all_gather(across, 'row', axis=0, tiled=True)  29.9 us
  transfers between devices with their start and end apart: 3, of which 3 were waited for; matrix products, arithmetic and copies ran while one was open for 1% of the time, Pallas kernels for 0%

commit v1 on v0

v1 whole, which is shorter than its diff:
```python
import functools

import jax
import jax.numpy as jnp
from jax import lax
from jax.experimental import pallas as pl
from jax.experimental.pallas import tpu as pltpu
from jax.sharding import PartitionSpec as P

FOLD = 128


def fold_rows(x):
    total = x[:FOLD]
    for start in range(FOLD, x.shape[0], FOLD):
        piece = x[start : start + FOLD]
        total = total + jnp.pad(piece, ((0, FOLD - piece.shape[0]), (0, 0)))
    return total


def unfold_rows(x, width):
    pieces = [x[: min(FOLD, width - start)] for start in range(0, width, FOLD)]
    return jnp.concatenate(pieces, axis=0)


def both_halves(own):
    other = lax.ppermute(own, "pair", [(0, 1), (1, 0)])
    first = lax.axis_index("pair") == 0
    return jnp.concatenate([jnp.where(first, own, other), jnp.where(first, other, own)])


def ladder_kernel(
    cols, pairs_here, pair_ref, t_ref, stack_ref, side_ref, down_ref, across_ref, out_ref, inner
):
    p = pl.program_id(0)
    width = side_ref.shape[0]
    count = side_ref.shape[1] // width
    half, at = p // pairs_here, p % pairs_here
    groups = t_ref.shape[0] // cols
    want = pair_ref[p]
    allowed = jnp.bitwise_xor(down_ref[...], across_ref[...]) == want
    rows = jnp.concatenate(
        [t_ref[q * groups + half, at].astype(jnp.float32) for q in range(cols)], axis=0
    )
    tiles = -(-width // FOLD)
    spread = jnp.concatenate([rows] * tiles, axis=1)
    amp = jnp.where(allowed, spread, 0.0).astype(jnp.bfloat16)[:, :width]
    for k in range(count):
        part = lax.dot_general(
            amp,
            stack_ref[pl.ds(k * width, width), :],
            (((1,), (1,)), ((), ())),
            preferred_element_type=jnp.float32,
        )
        inner[pl.ds(k * width, width), :] = part.astype(jnp.bfloat16)
    ladder = jnp.dot(side_ref[...], inner[...], preferred_element_type=jnp.float32)
    both = ladder + ladder.T
    both = jnp.concatenate(
        [both, jnp.zeros((width, tiles * FOLD - width), jnp.float32)], axis=1
    )
    both = jnp.where(allowed, both, 0.0)
    folded = both[:, :FOLD]
    for k in range(1, tiles):
        folded = folded + both[:, k * FOLD : (k + 1) * FOLD]
    block = width // cols
    for q in range(cols):
        out_ref[q * groups + half, at] = folded[q * block : (q + 1) * block].astype(out_ref.dtype)


def ladder_call(gathered, factors, labels, pair_labels, cols, pairs_here):
    count, width, _ = factors.shape
    pairs = pair_labels.shape[0]
    tiles = -(-width // FOLD)
    stack = factors.reshape(count * width, width)
    side = jnp.transpose(factors, (1, 0, 2)).reshape(width, count * width)
    down = labels[:, None]
    across = jnp.pad(labels, (0, tiles * FOLD - width), constant_values=-1)[None, :]
    vmem = pl.BlockSpec(memory_space=pltpu.VMEM)
    return pl.pallas_call(
        functools.partial(ladder_kernel, cols, pairs_here),
        grid=(pairs,),
        out_shape=jax.ShapeDtypeStruct(gathered.shape, jnp.bfloat16),
        in_specs=[pl.BlockSpec(memory_space=pltpu.SMEM)] + [vmem] * 5,
        out_specs=vmem,
        scratch_shapes=[pltpu.VMEM((count * width, width), jnp.bfloat16)],
    )(pair_labels, gathered, stack, side, down, across)


def body(amplitudes, factors, vir_irrep, pair_irrep):
    row_block, pairs_here, col_block = amplitudes.shape
    width = vir_irrep.shape[0]
    rows, cols = width // row_block, width // col_block
    inner = pairs_here * col_block
    plane = ("col", "pair")
    row_labels = lax.dynamic_slice_in_dim(vir_irrep, lax.axis_index("row") * row_block, row_block)
    col_labels = lax.dynamic_slice_in_dim(vir_irrep, lax.axis_index("col") * col_block, col_block)
    pair_labels = both_halves(pair_irrep)
    partner = jnp.bitwise_xor(pair_irrep[:, None], col_labels[None, :]).reshape(1, inner)

    sent = jnp.broadcast_to(amplitudes.reshape(1, row_block, inner), (rows, row_block, inner))
    tall = lax.all_to_all(sent, "row", 0, 0, tiled=True).reshape(width, inner)
    tall = jnp.where(vir_irrep[:, None] == partner, tall, jnp.zeros_like(tall))
    block = fold_rows(tall).T.reshape(1, pairs_here, col_block, FOLD)
    groups = cols * lax.axis_size("pair")
    gathered = lax.all_to_all(
        jnp.broadcast_to(block, (groups, pairs_here, col_block, FOLD)), plane, 0, 0, tiled=True
    )

    partial_sums = ladder_call(gathered, factors, vir_irrep, pair_labels, cols, pairs_here)

    pieces = lax.all_to_all(partial_sums, plane, 0, 0, tiled=True)
    summed = jnp.sum(pieces.astype(jnp.float32), axis=0).reshape(inner, FOLD)
    tall_sum = unfold_rows(summed.T, width).reshape(rows, row_block, inner)
    finals = lax.all_to_all(tall_sum, "row", 0, 0, tiled=True)
    ladder = jnp.sum(finals, axis=0)
    ladder = jnp.where(row_labels[:, None] == partner, ladder, jnp.zeros_like(ladder))
    return ladder.reshape(row_block, pairs_here, col_block)


def solution(mesh):
    placed = (P("row", "pair", "col"), P(("row", "col", "pair"), None, None), P(), P("pair"))
    return jax.shard_map(
        body, mesh=mesh, in_specs=placed, out_specs=P("row", "pair", "col"), check_vma=False
    )
```

time: 415 us -> 104 us (0.25)
  waiting for transfers between devices: 199 us -> 27.4 us
  matrix products: 80.9 us -> 0 us
  blocking collectives: 61.2 us -> 15.1 us
  local copies, waits for them, and re-layouts: 55.1 us -> 11.7 us
  starting transfers between devices: 0.08 us -> 23.8 us
  Pallas kernels: 0 us -> 22.7 us
  between operations: 13.8 us -> 0.09 us
    unnamed x5 -> x0, waiting for transfers between devices: 196 us -> none
    dot_general x32 -> x0, matrix products: 80.9 us -> none  [the longest x16 44.8 us: one_factor(): jnp.dot(factor, amp_matrix, preferred_element_type=jnp.float32)]
    all_gather x2 -> x0, blocking collectives: 61.2 us -> none  [the longest x1 31.3 us: body(): across = lax.all_gather(sym_amp, 'col', axis=2, tiled=True)]
    dot_general x16 -> x0, local copies, waits for them, and re-layouts: 40.6 us -> none  [one_factor(): lax.dot_general(inner, factor, (((1,), (1,)), ((), ())), preferred_elemen...]
    all_to_all x0 -> x3, waiting for transfers between devices: none -> 25.8 us  [the longest x1 14.4 us: body(): finals = lax.all_to_all(tall_sum, 'row', 0, 0, tiled=True)]
    pallas_call x0 -> x1, Pallas kernels: none -> 22.7 us  [ladder_call(): pl.pallas_call(functools.partial(ladder_kernel, cols, pairs_here), grid=(...]
    all_to_all x0 -> x3, starting transfers between devices: none -> 22.4 us  [the longest x1 9.97 us: body(): tall = lax.all_to_all(sent, 'row', 0, 0, tiled=True).reshape(width, inner)]
    all_to_all x0 -> x1, blocking collectives: none -> 15.1 us  [body(): pieces = lax.all_to_all(partial_sums, plane, 0, 0, tiled=True)]
  transfers between devices with their start and end apart: 3 -> 4, of which waited for: 3 -> 4; matrix products, arithmetic and copies ran while one was open for 1% -> 8% of each run, Pallas kernels for 0% -> 0%
where the time goes in v1:
time: 104 us
  waiting for transfers between devices  27.4 us (26%)
  starting transfers between devices  23.8 us (23%)
  Pallas kernels  22.7 us (22%)
  blocking collectives  15.1 us (15%)
  local copies, waits for them, and re-layouts  11.7 us (11%)
  other arithmetic  2.96 us (3%)
    pallas_call x1, Pallas kernels, ladder_call(): pl.pallas_call(functools.partial(ladder_kernel, cols, pairs_here), grid=(...  22.7 us
    all_to_all x1, blocking collectives, body(): pieces = lax.all_to_all(partial_sums, plane, 0, 0, tiled=True)  15.1 us
    all_to_all x1, waiting for transfers between devices, body(): finals = lax.all_to_all(tall_sum, 'row', 0, 0, tiled=True)  14.4 us
    all_to_all x1, starting transfers between devices, body(): tall = lax.all_to_all(sent, 'row', 0, 0, tiled=True).reshape(width, inner)  9.97 us
    all_to_all x1, waiting for transfers between devices, body(): tall = lax.all_to_all(sent, 'row', 0, 0, tiled=True).reshape(width, inner)  8.64 us
    all_to_all x1, starting transfers between devices, body(): lax.all_to_all(jnp.broadcast_to(block, (groups, pairs_here, col_block, FO...  6.75 us
    all_to_all x1, starting transfers between devices, body(): finals = lax.all_to_all(tall_sum, 'row', 0, 0, tiled=True)  5.66 us
    all_to_all x1, waiting for transfers between devices, body(): lax.all_to_all(jnp.broadcast_to(block, (groups, pairs_here, col_block, FO...  2.75 us
  transfers between devices with their start and end apart: 4, of which 4 were waited for; matrix products, arithmetic and copies ran while one was open for 8% of the time, Pallas kernels for 0%

profile of v1, /device:TPU:1, one launch (start us, length us, event | category | flops | bytes accessed | tf_op | source)
XLA Modules:
  0.0 103.9 jit_solution(4605940661361947696)
XLA Ops:
  0.0 0.0 copy-start.1
  0.0 0.0 copy-start.2
  0.0 0.8 broadcast_in_dim.30
  0.8 0.7 broadcast_in_dim.31
  1.5 10.0 %all-to-all-start = ((bf16[16,20,160]{2,1,0:T(8,128)(2,1)}), bf16[16,20,160]{2,1,0:T(8,128)(2,1)S(1)}, u32[]{:S(2)}, u32[]{:S(2)}) async-start(bf16[16,20,160]{2,1,0:T(8,128)(2,1)} %broadcast_in_dim.31), calls=%async_computation | async-start | bytes 393216 | tf_op jit(solution)/shard_map/all_to_all | solution.py:101
  11.5 0.8 dynamic_slice.7
  12.3 0.7 broadcast_xor_fusion
  13.0 0.1 xor.24
  13.1 8.6 %all-to-all-done = bf16[16,20,160]{2,1,0:T(8,128)(2,1)S(1)} async-done(((bf16[16,20,160]{2,1,0:T(8,128)(2,1)}), bf16[16,20,160]{2,1,0:T(8,128)(2,1)S(1)}, u32[]{:S(2)}, u32[]{:S(2)}) %all-to-all-start) | async-done | bytes 102432 | tf_op jit(solution)/shard_map/all_to_all | solution.py:101
  21.7 0.1 reshape.50
  21.8 0.8 compare_select_fusion
  22.6 0.1 copy.10
  22.7 1.0 broadcast_in_dim.34
  23.7 6.8 %all-to-all-start.1 = ((bf16[16,4,40,128]{3,2,1,0:T(8,128)(2,1)}), bf16[16,4,40,128]{3,2,1,0:T(8,128)(2,1)S(1)}, u32[]{:S(2)}, u32[]{:S(2)}) async-start(bf16[16,4,40,128]{3,2,1,0:T(8,128)(2,1)} %broadcast_in_dim.34), calls=%async_computation.1 | async-start | bytes 1310720 | tf_op jit(solution)/shard_map/all_to_all | solution.py:105
  30.4 0.0 copy-done.2
  30.5 1.4 %collective-permute-start = (s32[4]{0:T(128)S(1)}, s32[4]{0:T(128)S(1)}, u32[]{:S(2)}, u32[]{:S(2)}) collective-permute-start(s32[4]{0:T(128)S(1)} %copy-done.2), channel_id=1, source_target_pairs={{0,1},{1,0},{2,3},{3,2},{4,5},{5,4},{6,7},{7,6},{8,9},{9,8},{10,11... | collective-permute-start | bytes 56 | tf_op jit(solution)/shard_map/ppermute | solution.py:27
  31.9 0.0 copy-done.1
  31.9 0.8 broadcast_in_dim.38.down_ref
  32.7 2.7 %copy.11 = bf16[320,8,320]{2,1,0:T(8,128)(2,1)S(1)} copy(bf16[320,8,320]{2,0,1:T(8,128)(2,1)} %bitcast.9) | data formatting | bytes 3276800 | tf_op jit(solution)/shard_map/transpose | solution.py:75
  35.4 2.3 %reshape.52.side_ref = bf16[320,2560]{1,0:T(8,128)(2,1)} reshape(bf16[320,8,320]{2,1,0:T(8,128)(2,1)S(1)} %copy.11) | data formatting | bytes 3276800 | tf_op jit(solution)/shard_map/reshape | solution.py:75
  37.7 0.6 broadcast_in_dim.36.across_ref
  38.2 1.6 %collective-permute-done = s32[4]{0:T(128)S(1)} collective-permute-done((s32[4]{0:T(128)S(1)}, s32[4]{0:T(128)S(1)}, u32[]{:S(2)}, u32[]{:S(2)}) %collective-permute-start) | collective-permute-done | bytes 48 | tf_op jit(solution)/shard_map/ppermute | solution.py:27
  39.8 0.6 pad_add_fusion.pair_ref
  40.4 2.7 %all-to-all-done.1.t_ref = bf16[16,4,40,128]{3,2,1,0:T(8,128)(2,1)S(1)} async-done(((bf16[16,4,40,128]{3,2,1,0:T(8,128)(2,1)}), bf16[16,4,40,128]{3,2,1,0:T(8,128)(2,1)S(1)}, u32[]{:S(2)}, u32[]{:S(2)}) %all-to-all-start.1) | async-done | bytes 655392 | tf_op jit(solution)/shard_map/all_to_all | solution.py:105
  43.1 0.0 copy-start
  43.1 0.9 copy-done
  44.0 22.7 %shard_map.46 = bf16[16,4,40,128]{3,2,1,0:T(8,128)(2,1)} custom-call(s32[8]{0:T(128)} %pad_add_fusion.pair_ref, bf16[16,4,40,128]{3,2,1,0:T(8,128)(2,1)} %copy-done, bf16[2560,320]{1,0:T(8,128)(2,1)} %bitcast.10, bf16[320,2560]{1,0:T(8,128)(2,1)} %reshape.52.side_ref, s32[320,1]{1,0:T(8,128)} %broadcast_in_dim.38.down_ref, s32[1,384]{1,0:T(1,128)} %broadcast_in_dim.36.across_ref), custom_call_target="tpu_custom_call" | custom-call | tf_op jit(solution)/shard_map/pallas_call | solution.py:79
  66.7 15.1 %all_to_all.20 = bf16[16,4,40,128]{3,2,1,0:T(8,128)(2,1)S(1)} all-to-all(bf16[16,4,40,128]{3,2,1,0:T(8,128)(2,1)} %shard_map.46), channel_id=1, replica_groups=mesh['row'=16,'col'=8,'pair'=2] {'col','pair'}, dimensions={0} | all-to-all | bytes 1310720 | tf_op jit(solution)/shard_map/all_to_all | solution.py:111
  81.8 0.1 convert_reduce_fusion
  81.9 0.1 copy.13
  82.1 0.8 reshape.54
  82.8 5.7 %all-to-all-start.3 = ((f32[16,20,160]{2,1,0:T(8,128)}), f32[16,20,160]{2,1,0:T(8,128)S(1)}, u32[]{:S(2)}, u32[]{:S(2)}) async-start(f32[16,20,160]{2,1,0:T(8,128)} %reshape.54), calls=%async_computation.3 | async-start | bytes 786432 | tf_op jit(solution)/shard_map/all_to_all | solution.py:114
  88.5 0.1 dynamic_slice.6
  88.6 14.4 %all-to-all-done.3 = f32[16,20,160]{2,1,0:T(8,128)S(1)} async-done(((f32[16,20,160]{2,1,0:T(8,128)}), f32[16,20,160]{2,1,0:T(8,128)S(1)}, u32[]{:S(2)}, u32[]{:S(2)}) %all-to-all-start.3) | async-done | bytes 204832 | tf_op jit(solution)/shard_map/all_to_all | solution.py:114
  103.1 0.1 reduce_sum.22
  103.2 0.7 compare_select_fusion.1
  (6 shorter events, 0.1 us)
Async XLA Ops:
  0.0 31.9 %copy-start.1 = (s32[320]{0:T(512)S(1)}, s32[320]{0:T(512)}, u32[]{:S(2)}) copy-start(s32[320]{0:T(512)} %param.6) | copy-start | bytes 3844
  0.0 30.4 %copy-start.2 = (s32[4]{0:T(128)S(1)}, s32[4]{0:T(128)}, u32[]{:S(2)}) copy-start(s32[4]{0:T(128)} %param.7) | copy-start | bytes 52
  1.5 20.2 %all-to-all-start = ((bf16[16,20,160]{2,1,0:T(8,128)(2,1)}), bf16[16,20,160]{2,1,0:T(8,128)(2,1)S(1)}, u32[]{:S(2)}, u32[]{:S(2)}) async-start(bf16[16,20,160]{2,1,0:T(8,128)(2,1)} %broadcast_in_dim.31), calls=%async_computation | async-start | bytes 393216 | tf_op jit(solution)/shard_map/all_to_all | solution.py:101
  23.7 19.4 %all-to-all-start.1 = ((bf16[16,4,40,128]{3,2,1,0:T(8,128)(2,1)}), bf16[16,4,40,128]{3,2,1,0:T(8,128)(2,1)S(1)}, u32[]{:S(2)}, u32[]{:S(2)}) async-start(bf16[16,4,40,128]{3,2,1,0:T(8,128)(2,1)} %broadcast_in_dim.34), calls=%async_computation.1 | async-start | bytes 1310720 | tf_op jit(solution)/shard_map/all_to_all | solution.py:105
  30.5 9.4 %collective-permute-start = (s32[4]{0:T(128)S(1)}, s32[4]{0:T(128)S(1)}, u32[]{:S(2)}, u32[]{:S(2)}) collective-permute-start(s32[4]{0:T(128)S(1)} %copy-done.2), channel_id=1, source_target_pairs={{0,1},{1,0},{2,3},{3,2},{4,5},{5,4},{6,7},{7,6},{8,9},{9,8},{10,11... | collective-permute-start | bytes 56 | tf_op jit(solution)/shard_map/ppermute | solution.py:27
  43.1 0.9 copy-start
  82.8 20.2 %all-to-all-start.3 = ((f32[16,20,160]{2,1,0:T(8,128)}), f32[16,20,160]{2,1,0:T(8,128)S(1)}, u32[]{:S(2)}, u32[]{:S(2)}) async-start(f32[16,20,160]{2,1,0:T(8,128)} %reshape.54), calls=%async_computation.3 | async-start | bytes 786432 | tf_op jit(solution)/shard_map/all_to_all | solution.py:114

commit v2 on v1

v2 whole, which is shorter than its diff:
```python
import functools

import jax
import jax.numpy as jnp
from jax import lax
from jax.experimental import pallas as pl
from jax.experimental.pallas import tpu as pltpu
from jax.sharding import PartitionSpec as P

FOLD = 128
CORES = 2


def fold_rows(x):
    total = x[:FOLD]
    for start in range(FOLD, x.shape[0], FOLD):
        piece = x[start : start + FOLD]
        total = total + jnp.pad(piece, ((0, FOLD - piece.shape[0]), (0, 0)))
    return total


def unfold_rows(x, width):
    pieces = [x[: min(FOLD, width - start)] for start in range(0, width, FOLD)]
    return jnp.concatenate(pieces, axis=0)


def ladder_kernel(
    cols,
    factor_group,
    lane_group,
    pair_ref,
    t_ref,
    own_ref,
    other_ref,
    own_side_ref,
    other_side_ref,
    down_ref,
    across_ref,
    out_ref,
    inner,
    amp,
    ladders,
):
    width = own_side_ref.shape[0]
    half_depth = own_ref.shape[0]
    count = half_depth // width
    groups, pairs_here = t_ref.shape[0] // cols, t_ref.shape[1]
    pairs = groups * pairs_here
    tiles = -(-width // FOLD)
    block = width // cols
    mixed = jnp.bitwise_xor(down_ref[...], across_ref[...])

    for p in range(pairs):
        half, at = p // pairs_here, p % pairs_here
        rows = jnp.concatenate(
            [t_ref[q * groups + half, at].astype(jnp.float32) for q in range(cols)], axis=0
        )
        spread = jnp.where(mixed == pair_ref[p], jnp.concatenate([rows] * tiles, axis=1), 0.0)
        amp[p * width : (p + 1) * width, :] = spread.astype(jnp.bfloat16)[:, :width]

    step = factor_group * width
    for source, base in ((own_ref, 0), (other_ref, half_depth)):

        @pl.loop(0, count // factor_group)
        def _(g, source=source, base=base):
            part = lax.dot_general(
                amp[...],
                source[pl.ds(pl.multiple_of(g * step, step), step), :],
                (((1,), (1,)), ((), ())),
                preferred_element_type=jnp.float32,
            ).astype(jnp.bfloat16)
            for p in range(pairs):
                for k in range(factor_group):
                    at = pl.multiple_of(base + g * step + k * width, width)
                    inner[pl.ds(at, width), p * width : (p + 1) * width] = part[
                        p * width : (p + 1) * width, k * width : (k + 1) * width
                    ]

    for start in range(0, pairs * width, lane_group):
        lanes = slice(start, start + lane_group)
        ladders[:, lanes] = jnp.dot(
            own_side_ref[...], inner[:half_depth, lanes], preferred_element_type=jnp.float32
        ) + jnp.dot(
            other_side_ref[...], inner[half_depth:, lanes], preferred_element_type=jnp.float32
        )

    for p in range(pairs):
        half, at = p // pairs_here, p % pairs_here
        ladder = ladders[:, p * width : (p + 1) * width]
        both = ladder + ladder.T
        both = jnp.concatenate(
            [both, jnp.zeros((width, tiles * FOLD - width), jnp.float32)], axis=1
        )
        both = jnp.where(mixed == pair_ref[p], both, 0.0)
        folded = both[:, :FOLD]
        for k in range(1, tiles):
            folded = folded + both[:, k * FOLD : (k + 1) * FOLD]
        for q in range(cols):
            out_ref[q * groups + half, at] = folded[q * block : (q + 1) * block].astype(
                out_ref.dtype
            )


def side_by_side(factors):
    count, width, _ = factors.shape
    return jnp.transpose(factors, (1, 0, 2)).reshape(width, count * width)


def ladder_call(gathered, own, other, labels, pair_labels, cols):
    count, width, _ = own.shape
    pairs = pair_labels.shape[0]
    tiles = -(-width // FOLD)
    down = labels[:, None]
    across = jnp.pad(labels, (0, tiles * FOLD - width), constant_values=-1)[None, :]
    vmem = pl.BlockSpec(memory_space=pltpu.VMEM)
    return pl.pallas_call(
        functools.partial(ladder_kernel, cols, 4, 2 * FOLD),
        out_shape=jax.ShapeDtypeStruct(gathered.shape, jnp.bfloat16),
        in_specs=[pl.BlockSpec(memory_space=pltpu.SMEM)] + [vmem] * 7,
        out_specs=vmem,
        scratch_shapes=[
            pltpu.VMEM((2 * count * width, pairs * width), jnp.bfloat16),
            pltpu.VMEM((pairs * width, width), jnp.bfloat16),
            pltpu.VMEM((width, pairs * width), jnp.float32),
        ],
    )(
        pair_labels,
        gathered,
        own.reshape(count * width, width),
        other.reshape(count * width, width),
        side_by_side(own),
        side_by_side(other),
        down,
        across,
    )


def body(amplitudes, factors, vir_irrep, pair_irrep):
    row_block, pairs_here, col_block = amplitudes.shape
    width = vir_irrep.shape[0]
    rows, cols = width // row_block, width // col_block
    held = pairs_here // CORES
    inner = held * col_block
    plane = ("col", "pair")
    core = lax.axis_index("row") % CORES
    swap = [(k, k ^ 1) for k in range(rows)]

    other_factors = lax.ppermute(factors, "row", swap)
    other_pairs = lax.ppermute(pair_irrep, "pair", [(0, 1), (1, 0)])
    first = lax.axis_index("pair") == 0
    pair_labels = jnp.stack(
        [jnp.where(first, pair_irrep, other_pairs), jnp.where(first, other_pairs, pair_irrep)]
    )
    pair_labels = lax.dynamic_slice_in_dim(pair_labels, core * held, held, axis=1).reshape(-1)

    row_labels = lax.dynamic_slice_in_dim(vir_irrep, lax.axis_index("row") * row_block, row_block)
    col_labels = lax.dynamic_slice_in_dim(vir_irrep, lax.axis_index("col") * col_block, col_block)
    partner = jnp.bitwise_xor(pair_irrep[:, None], col_labels[None, :])
    partner_held = lax.dynamic_slice_in_dim(partner, core * held, held, axis=0).reshape(1, inner)

    halves = amplitudes.reshape(row_block, CORES, inner).transpose(1, 0, 2)
    sent = jnp.broadcast_to(halves[None], (rows // CORES, CORES, row_block, inner))
    sent = sent.reshape(rows, row_block, inner)
    tall = lax.all_to_all(sent, "row", 0, 0, tiled=True).reshape(width, inner)
    tall = jnp.where(vir_irrep[:, None] == partner_held, tall, jnp.zeros_like(tall))
    block = fold_rows(tall).T.reshape(1, held, col_block, FOLD)
    groups = cols * lax.axis_size("pair")
    gathered = lax.all_to_all(
        jnp.broadcast_to(block, (groups, held, col_block, FOLD)), plane, 0, 0, tiled=True
    )

    partial_sums = ladder_call(gathered, factors, other_factors, vir_irrep, pair_labels, cols)

    pieces = lax.all_to_all(partial_sums, plane, 0, 0, tiled=True)
    summed = jnp.sum(pieces.astype(jnp.float32), axis=0).reshape(inner, FOLD)
    tall_sum = unfold_rows(summed.T, width).reshape(rows, row_block, inner)
    finals = lax.all_to_all(tall_sum, "row", 0, 0, tiled=True)
    ladder = jnp.sum(finals.reshape(rows // CORES, CORES, row_block, inner), axis=0)
    ladder = ladder.transpose(1, 0, 2).reshape(row_block, pairs_here, col_block)
    allowed = row_labels[:, None, None] == partner[None]
    return jnp.where(allowed, ladder, jnp.zeros_like(ladder))


def solution(mesh):
    placed = (P("row", "pair", "col"), P(("row", "col", "pair"), None, None), P(), P("pair"))
    return jax.shard_map(
        body, mesh=mesh, in_specs=placed, out_specs=P("row", "pair", "col"), check_vma=False
    )
```

time: 104 us -> 90.1 us (0.87)
  waiting for transfers between devices: 27.4 us -> 13.2 us
  local copies, waits for them, and re-layouts: 11.7 us -> 17.5 us
  Pallas kernels: 22.7 us -> 18.2 us
  blocking collectives: 15.1 us -> 11.6 us
  starting transfers between devices: 23.8 us -> 27.1 us
  other arithmetic: 2.96 us -> 1.66 us
    all_to_all x1, waiting for transfers between devices: 8.64 us -> 0.01 us  [body(): tall = lax.all_to_all(sent, 'row', 0, 0, tiled=True).reshape(width, inner)]
    pallas_call x1, Pallas kernels: 22.7 us -> 18.2 us  [ladder_call(): pl.pallas_call(functools.partial(ladder_kernel, cols, 4, 2 * FOLD), out_s...]
    all_to_all x1, waiting for transfers between devices: 14.4 us -> 10.1 us  [body(): finals = lax.all_to_all(tall_sum, 'row', 0, 0, tiled=True)]
    reshape x1 -> x5, local copies, waits for them, and re-layouts: 2.27 us -> 5.99 us  [the longest x2 4.47 us: side_by_side(): return jnp.transpose(factors, (1, 0, 2)).reshape(width, count * width)]
    all_to_all x1, starting transfers between devices: 5.66 us -> 9.35 us  [body(): finals = lax.all_to_all(tall_sum, 'row', 0, 0, tiled=True)]
    all_to_all x1, blocking collectives: 15.1 us -> 11.6 us  [body(): pieces = lax.all_to_all(partial_sums, plane, 0, 0, tiled=True)]
    all_to_all x1, starting transfers between devices: 9.97 us -> 6.88 us  [body(): tall = lax.all_to_all(sent, 'row', 0, 0, tiled=True).reshape(width, inner)]
    ppermute x1 -> x2, starting transfers between devices: 1.45 us -> 4.41 us  [the longest x1 3.2 us: body(): other_factors = lax.ppermute(factors, 'row', swap)]
  transfers between devices with their start and end apart: 4 -> 5, of which waited for: 4 -> 2; matrix products, arithmetic and copies ran while one was open for 8% -> 19% of each run, Pallas kernels for 0% -> 0%
where the time goes in v2:
time: 90.1 us; the launch traced here: 89.5 us
  starting transfers between devices  27.1 us (30%)
  Pallas kernels  18.2 us (20%)
  local copies, waits for them, and re-layouts  17.5 us (19%)
  waiting for transfers between devices  13.2 us (15%)
  blocking collectives  11.6 us (13%)
  other arithmetic  1.66 us (2%)
    pallas_call x1, Pallas kernels, ladder_call(): pl.pallas_call(functools.partial(ladder_kernel, cols, 4, 2 * FOLD), out_s...  18.2 us
    all_to_all x1, blocking collectives, body(): pieces = lax.all_to_all(partial_sums, plane, 0, 0, tiled=True)  11.6 us
    all_to_all x1, waiting for transfers between devices, body(): finals = lax.all_to_all(tall_sum, 'row', 0, 0, tiled=True)  10.1 us
    all_to_all x1, starting transfers between devices, body(): finals = lax.all_to_all(tall_sum, 'row', 0, 0, tiled=True)  9.35 us
    all_to_all x1, starting transfers between devices, body(): tall = lax.all_to_all(sent, 'row', 0, 0, tiled=True).reshape(width, inner)  6.88 us
    all_to_all x1, starting transfers between devices, body(): lax.all_to_all(jnp.broadcast_to(block, (groups, held, col_block, FOLD)),...  6.47 us
    transpose x2, local copies, waits for them, and re-layouts, side_by_side(): return jnp.transpose(factors, (1, 0, 2)).reshape(width, count * width)  5.39 us
    reshape x2, local copies, waits for them, and re-layouts, side_by_side(): return jnp.transpose(factors, (1, 0, 2)).reshape(width, count * width)  4.47 us
  transfers between devices with their start and end apart: 5, of which 2 were waited for; matrix products, arithmetic and copies ran while one was open for 19% of the time, Pallas kernels for 0%

profile of v2, /device:TPU:1, one launch (start us, length us, event | category | flops | bytes accessed | tf_op | source)
XLA Modules:
  0.0 89.5 jit_solution(3154709180194600819)
XLA Ops:
  0.0 3.2 %collective-permute-start.1 = (bf16[8,320,320]{2,1,0:T(8,128)(2,1)}, bf16[8,320,320]{2,1,0:T(8,128)(2,1)}, u32[]{:S(2)}, u32[]{:S(2)}) collective-permute-start(bf16[8,320,320]{2,1,0:T(8,128)(2,1)} %param.5), channel_id=1, source_target_pairs={{0,16},{16,0},{32,48},{48,32},{64,80},{80,64},{96,112},{112,96},{1... | collective-permute-start | bytes 4915208 | tf_op jit(solution)/shard_map/ppermute | solution.py:148
  3.2 0.8 reshape.71
  4.0 0.7 broadcast_in_dim.14
  4.7 6.9 %all-to-all-start = ((bf16[16,20,80]{2,1,0:T(8,128)(2,1)}), bf16[16,20,80]{2,1,0:T(8,128)(2,1)S(1)}, u32[]{:S(2)}, u32[]{:S(2)}) async-start(bf16[16,20,80]{2,1,0:T(8,128)(2,1)} %bitcast.3), calls=%async_computation | async-start | bytes 196608 | tf_op jit(solution)/shard_map/all_to_all | solution.py:164
  11.6 1.2 %collective-permute-start = (s32[4]{0:T(128)}, s32[4]{0:T(128)S(1)}, u32[]{:S(2)}, u32[]{:S(2)}) collective-permute-start(s32[4]{0:T(128)} %param.7), channel_id=1, source_target_pairs={{0,1},{1,0},{2,3},{3,2},{4,5},{5,4},{6,7},{7,6},{8,9},{9,8},{10,11... | collective-permute-start | bytes 56 | tf_op jit(solution)/shard_map/ppermute | solution.py:149
  12.8 1.4 %broadcast_in_dim.37.down_ref = s32[320,1]{1,0:T(8,128)} reshape(s32[320]{0:T(512)} %param.6) | data formatting | bytes 2560 | tf_op jit(solution)/shard_map/broadcast_in_dim | solution.py:165
  14.2 0.8 dynamic_slice.13
  15.0 0.7 broadcast_xor_fusion
  15.7 0.1 eq.38
  15.8 2.7 %copy.27 = bf16[320,8,320]{2,1,0:T(8,128)(2,1)S(1)} copy(bf16[320,8,320]{2,0,1:T(8,128)(2,1)} %bitcast.19) | data formatting | bytes 3276800 | tf_op jit(solution)/shard_map/transpose | solution.py:106
  18.5 0.0 copy-start.1
  18.5 0.0 copy-start.2
  18.5 2.2 %reshape.76.own_side_ref = bf16[320,2560]{1,0:T(8,128)(2,1)} reshape(bf16[320,8,320]{2,1,0:T(8,128)(2,1)S(1)} %copy.27) | data formatting | bytes 3276800 | tf_op jit(solution)/shard_map/reshape | solution.py:106
  20.8 0.0 copy-done.1
  20.8 0.6 broadcast_in_dim.35.across_ref
  21.3 0.0 all-to-all-done
  21.4 0.1 compare_select_fusion
  21.5 0.1 copy.26
  21.6 0.8 broadcast_in_dim.33
  22.4 6.5 %all-to-all-start.1 = ((bf16[16,2,40,128]{3,2,1,0:T(8,128)(2,1)}), bf16[16,2,40,128]{3,2,1,0:T(8,128)(2,1)S(1)}, u32[]{:S(2)}, u32[]{:S(2)}) async-start(bf16[16,2,40,128]{3,2,1,0:T(8,128)(2,1)} %broadcast_in_dim.33), calls=%async_computation.1 | async-start | bytes 655360 | tf_op jit(solution)/shard_map/all_to_all | solution.py:168
  28.9 0.0 collective-permute-done
  28.9 0.0 copy-done.2
  28.9 0.1 constant_dynamic-slice_fusion.1
  29.0 0.6 reshape.70.pair_ref
  29.6 0.0 collective-permute-done.1
  29.6 2.7 %copy.28 = bf16[320,8,320]{2,1,0:T(8,128)(2,1)S(1)} copy(bf16[320,8,320]{2,0,1:T(8,128)(2,1)} %bitcast.9) | data formatting | bytes 3276800 | tf_op jit(solution)/shard_map/transpose | solution.py:106
  32.3 2.2 %reshape.77.other_side_ref = bf16[320,2560]{1,0:T(8,128)(2,1)} reshape(bf16[320,8,320]{2,1,0:T(8,128)(2,1)S(1)} %copy.28) | data formatting | bytes 3276800 | tf_op jit(solution)/shard_map/reshape | solution.py:106
  34.6 3.1 %all-to-all-done.1.t_ref = bf16[16,2,40,128]{3,2,1,0:T(8,128)(2,1)S(1)} async-done(((bf16[16,2,40,128]{3,2,1,0:T(8,128)(2,1)}), bf16[16,2,40,128]{3,2,1,0:T(8,128)(2,1)S(1)}, u32[]{:S(2)}, u32[]{:S(2)}) %all-to-all-start.1) | async-done | bytes 327712 | tf_op jit(solution)/shard_map/all_to_all | solution.py:168
  37.6 0.0 copy-start
  37.6 0.7 copy-done
  38.4 18.2 %shard_map.46 = bf16[16,2,40,128]{3,2,1,0:T(8,128)(2,1)} custom-call(s32[4]{0:T(128)} %reshape.70.pair_ref, bf16[16,2,40,128]{3,2,1,0:T(8,128)(2,1)} %copy-done, bf16[2560,320]{1,0:T(8,128)(2,1)} %bitcast.20, bf16[2560,320]{1,0:T(8,128)(2,1)} %bitcast.7.other_ref, bf16[320,2560]{1,0:T(8,128)(2,1)} %reshape.76.own_side_ref, ...), custom_call_target="tpu_custom_call" | custom-call | tf_op jit(solution)/shard_map/pallas_call | solution.py:116
  56.6 11.6 %all_to_all.20 = bf16[16,2,40,128]{3,2,1,0:T(8,128)(2,1)S(1)} all-to-all(bf16[16,2,40,128]{3,2,1,0:T(8,128)(2,1)} %shard_map.46), channel_id=1, replica_groups=mesh['row'=16,'col'=8,'pair'=2] {'col','pair'}, dimensions={0} | all-to-all | bytes 655360 | tf_op jit(solution)/shard_map/all_to_all | solution.py:174
  68.2 0.1 convert_reduce_fusion
  68.3 0.1 copy.30
  68.4 0.7 reshape.79
  69.1 9.4 %all-to-all-start.3 = ((f32[16,20,80]{2,1,0:T(8,128)}), f32[16,20,80]{2,1,0:T(8,128)S(1)}, u32[]{:S(2)}, u32[]{:S(2)}) async-start(f32[16,20,80]{2,1,0:T(8,128)} %reshape.79), calls=%async_computation.3 | async-start | bytes 393216 | tf_op jit(solution)/shard_map/all_to_all | solution.py:177
  78.4 0.1 dynamic_slice.12
  78.5 10.1 %all-to-all-done.3 = f32[16,20,80]{2,1,0:T(8,128)S(1)} async-done(((f32[16,20,80]{2,1,0:T(8,128)}), f32[16,20,80]{2,1,0:T(8,128)S(1)}, u32[]{:S(2)}, u32[]{:S(2)}) %all-to-all-start.3) | async-done | bytes 102432 | tf_op jit(solution)/shard_map/all_to_all | solution.py:177
  88.7 0.1 reshape.81
  88.8 0.7 compare_select_fusion.1
  (11 shorter events, 0.1 us)
Async XLA Ops:
  0.0 29.6 %collective-permute-start.1 = (bf16[8,320,320]{2,1,0:T(8,128)(2,1)}, bf16[8,320,320]{2,1,0:T(8,128)(2,1)}, u32[]{:S(2)}, u32[]{:S(2)}) collective-permute-start(bf16[8,320,320]{2,1,0:T(8,128)(2,1)} %param.5), channel_id=1, source_target_pairs={{0,16},{16,0},{32,48},{48,32},{64,80},{80,64},{96,112},{112,96},{1... | collective-permute-start | bytes 4915208 | tf_op jit(solution)/shard_map/ppermute | solution.py:148
  4.7 16.7 %all-to-all-start = ((bf16[16,20,80]{2,1,0:T(8,128)(2,1)}), bf16[16,20,80]{2,1,0:T(8,128)(2,1)S(1)}, u32[]{:S(2)}, u32[]{:S(2)}) async-start(bf16[16,20,80]{2,1,0:T(8,128)(2,1)} %bitcast.3), calls=%async_computation | async-start | bytes 196608 | tf_op jit(solution)/shard_map/all_to_all | solution.py:164
  11.6 17.3 %collective-permute-start = (s32[4]{0:T(128)}, s32[4]{0:T(128)S(1)}, u32[]{:S(2)}, u32[]{:S(2)}) collective-permute-start(s32[4]{0:T(128)} %param.7), channel_id=1, source_target_pairs={{0,1},{1,0},{2,3},{3,2},{4,5},{5,4},{6,7},{7,6},{8,9},{9,8},{10,11... | collective-permute-start | bytes 56 | tf_op jit(solution)/shard_map/ppermute | solution.py:149
  18.5 2.3 %copy-start.1 = (s32[320]{0:T(512)S(1)}, s32[320]{0:T(512)}, u32[]{:S(2)}) copy-start(s32[320]{0:T(512)} %param.6) | copy-start | bytes 3844
  18.5 10.4 %copy-start.2 = (s32[4]{0:T(128)S(1)}, s32[4]{0:T(128)}, u32[]{:S(2)}) copy-start(s32[4]{0:T(128)} %param.7) | copy-start | bytes 52
  22.4 15.2 %all-to-all-start.1 = ((bf16[16,2,40,128]{3,2,1,0:T(8,128)(2,1)}), bf16[16,2,40,128]{3,2,1,0:T(8,128)(2,1)S(1)}, u32[]{:S(2)}, u32[]{:S(2)}) async-start(bf16[16,2,40,128]{3,2,1,0:T(8,128)(2,1)} %broadcast_in_dim.33), calls=%async_computation.1 | async-start | bytes 655360 | tf_op jit(solution)/shard_map/all_to_all | solution.py:168
  37.6 0.7 copy-start
  69.1 19.6 %all-to-all-start.3 = ((f32[16,20,80]{2,1,0:T(8,128)}), f32[16,20,80]{2,1,0:T(8,128)S(1)}, u32[]{:S(2)}, u32[]{:S(2)}) async-start(f32[16,20,80]{2,1,0:T(8,128)} %reshape.79), calls=%async_computation.3 | async-start | bytes 393216 | tf_op jit(solution)/shard_map/all_to_all | solution.py:177

commit v3 on v2

--- a/solution.py
+++ b/solution.py
@@ -7,6 +7,7 @@
 from jax.experimental.pallas import tpu as pltpu
 from jax.sharding import PartitionSpec as P
 
+
 FOLD = 128
 CORES = 2
 
@@ -26,30 +27,34 @@
 
 def ladder_kernel(
     cols,
-    factor_group,
+    group,
     lane_group,
     pair_ref,
     t_ref,
     own_ref,
     other_ref,
-    own_side_ref,
-    other_side_ref,
     down_ref,
     across_ref,
     out_ref,
     inner,
     amp,
     ladders,
+    side,
+    stack,
+    arrived,
 ):
-    width = own_side_ref.shape[0]
+    width = down_ref.shape[0]
     half_depth = own_ref.shape[0]
-    count = half_depth // width
     groups, pairs_here = t_ref.shape[0] // cols, t_ref.shape[1]
     pairs = groups * pairs_here
     tiles = -(-width // FOLD)
     block = width // cols
+    step = group * width
+    half_steps = half_depth // step
+
+    fetch = pltpu.make_async_copy(other_ref, stack, arrived)
+    fetch.start()
     mixed = jnp.bitwise_xor(down_ref[...], across_ref[...])
-
     for p in range(pairs):
         half, at = p // pairs_here, p % pairs_here
         rows = jnp.concatenate(
@@ -58,31 +63,40 @@
         spread = jnp.where(mixed == pair_ref[p], jnp.concatenate([rows] * tiles, axis=1), 0.0)
         amp[p * width : (p + 1) * width, :] = spread.astype(jnp.bfloat16)[:, :width]
 
-    step = factor_group * width
-    for source, base in ((own_ref, 0), (other_ref, half_depth)):
-
-        @pl.loop(0, count // factor_group)
+    for source, base in ((own_ref, 0), (stack, half_steps)):
+        if base:
+            fetch.wait()
+
+        @pl.loop(0, half_steps)
         def _(g, source=source, base=base):
+            here = pl.multiple_of(g * step, step)
+            there = pl.multiple_of((base + g) * step, step)
+            for k in range(group):
+                side[base + g, :, k * width : (k + 1) * width] = source[
+                    pl.ds(pl.multiple_of(here + k * width, width), width), :
+                ]
             part = lax.dot_general(
                 amp[...],
-                source[pl.ds(pl.multiple_of(g * step, step), step), :],
+                source[pl.ds(here, step), :],
                 (((1,), (1,)), ((), ())),
                 preferred_element_type=jnp.float32,
             ).astype(jnp.bfloat16)
             for p in range(pairs):
-                for k in range(factor_group):
-                    at = pl.multiple_of(base + g * step + k * width, width)
-                    inner[pl.ds(at, width), p * width : (p + 1) * width] = part[
-                        p * width : (p + 1) * width, k * width : (k + 1) * width
-                    ]
+                for k in range(group):
+                    inner[
+                        pl.ds(pl.multiple_of(there + k * width, width), width),
+                        p * width : (p + 1) * width,
+                    ] = part[p * width : (p + 1) * width, k * width : (k + 1) * width]
 
     for start in range(0, pairs * width, lane_group):
         lanes = slice(start, start + lane_group)
-        ladders[:, lanes] = jnp.dot(
-            own_side_ref[...], inner[:half_depth, lanes], preferred_element_type=jnp.float32
-        ) + jnp.dot(
-            other_side_ref[...], inner[half_depth:, lanes], preferred_element_type=jnp.float32
-        )
+        total = None
+        for g in range(2 * half_steps):
+            term = jnp.dot(
+                side[g], inner[g * step : (g + 1) * step, lanes], preferred_element_type=jnp.float32
+            )
+            total = term if total is None else total + term
+        ladders[:, lanes] = total
 
     for p in range(pairs):
         half, at = p // pairs_here, p % pairs_here
@@ -101,37 +115,38 @@
             )
 
 
-def side_by_side(factors):
-    count, width, _ = factors.shape
-    return jnp.transpose(factors, (1, 0, 2)).reshape(width, count * width)
-
-
 def ladder_call(gathered, own, other, labels, pair_labels, cols):
     count, width, _ = own.shape
     pairs = pair_labels.shape[0]
     tiles = -(-width // FOLD)
+    group = 4
+    depth, lanes = 2 * count * width, pairs * width
     down = labels[:, None]
     across = jnp.pad(labels, (0, tiles * FOLD - width), constant_values=-1)[None, :]
     vmem = pl.BlockSpec(memory_space=pltpu.VMEM)
+    anywhere = pl.BlockSpec(memory_space=pl.ANY)
+    close = functools.partial(pltpu.with_memory_space_constraint, memory_space=pltpu.VMEM)
     return pl.pallas_call(
-        functools.partial(ladder_kernel, cols, 4, 2 * FOLD),
+        functools.partial(ladder_kernel, cols, group, 2 * FOLD),
         out_shape=jax.ShapeDtypeStruct(gathered.shape, jnp.bfloat16),
-        in_specs=[pl.BlockSpec(memory_space=pltpu.SMEM)] + [vmem] * 7,
+        in_specs=[pl.BlockSpec(memory_space=pltpu.SMEM), vmem, vmem, anywhere, vmem, vmem],
         out_specs=vmem,
         scratch_shapes=[
-            pltpu.VMEM((2 * count * width, pairs * width), jnp.bfloat16),
-            pltpu.VMEM((pairs * width, width), jnp.bfloat16),
-            pltpu.VMEM((width, pairs * width), jnp.float32),
+            pltpu.VMEM((depth, lanes), jnp.bfloat16),
+            pltpu.VMEM((lanes, width), jnp.bfloat16),
+            pltpu.VMEM((width, lanes), jnp.float32),
+            pltpu.VMEM((2 * count // group, width, group * width), jnp.bfloat16),
+            pltpu.VMEM((count * width, width), jnp.bfloat16),
+            pltpu.SemaphoreType.DMA(()),
         ],
+        compiler_params=pltpu.CompilerParams(vmem_limit_bytes=48 * 2**20),
     )(
         pair_labels,
-        gathered,
-        own.reshape(count * width, width),
+        close(gathered),
+        close(own.reshape(count * width, width)),
         other.reshape(count * width, width),
-        side_by_side(own),
-        side_by_side(other),
-        down,
-        across,
+        close(down),
+        close(across),
     )
 
 
@@ -174,6 +189,7 @@
     pieces = lax.all_to_all(partial_sums, plane, 0, 0, tiled=True)
     summed = jnp.sum(pieces.astype(jnp.float32), axis=0).reshape(inner, FOLD)
     tall_sum = unfold_rows(summed.T, width).reshape(rows, row_block, inner)
+    tall_sum, row_labels = lax.optimization_barrier((tall_sum, row_labels))
     finals = lax.all_to_all(tall_sum, "row", 0, 0, tiled=True)
     ladder = jnp.sum(finals.reshape(rows // CORES, CORES, row_block, inner), axis=0)
     ladder = ladder.transpose(1, 0, 2).reshape(row_block, pairs_here, col_block)

time: 90.1 us -> 82.5 us (0.916)
  local copies, waits for them, and re-layouts: 17.5 us -> 5.89 us
  waiting for transfers between devices: 13.2 us -> 21.4 us
  starting transfers between devices: 27.1 us -> 21.6 us
  blocking collectives: 11.6 us -> 15 us
  Pallas kernels: 18.2 us -> 15.6 us
    all_to_all x1, starting transfers between devices: 9.35 us -> 3.55 us  [body(): pieces = lax.all_to_all(partial_sums, plane, 0, 0, tiled=True)]
    all_to_all x1, waiting for transfers between devices: 3.06 us -> 8.8 us  [body(): lax.all_to_all(jnp.broadcast_to(block, (groups, held, col_block, FOLD)),...]
    all_to_all x1, waiting for transfers between devices: 0.01 us -> 5.4 us  [body(): tall = lax.all_to_all(sent, 'row', 0, 0, tiled=True).reshape(width, inner)]
    transpose x2 -> x0, local copies, waits for them, and re-layouts: 5.39 us -> none  [side_by_side(): return jnp.transpose(factors, (1, 0, 2)).reshape(width, count * width)]
    reshape x2 -> x0, local copies, waits for them, and re-layouts: 4.47 us -> none  [side_by_side(): return jnp.transpose(factors, (1, 0, 2)).reshape(width, count * width)]
    all_to_all x1, blocking collectives: 11.6 us -> 15 us  [body(): finals = lax.all_to_all(tall_sum, 'row', 0, 0, tiled=True)]
    all_to_all x1, waiting for transfers between devices: 10.1 us -> 7.23 us  [body(): pieces = lax.all_to_all(partial_sums, plane, 0, 0, tiled=True)]
    pallas_call x1, Pallas kernels: 18.2 us -> 15.6 us  [ladder_call(): pl.pallas_call(functools.partial(ladder_kernel, cols, group, 2 * FOLD), o...]
  transfers between devices with their start and end apart: 5 -> 5, of which waited for: 2 -> 3; matrix products, arithmetic and copies ran while one was open for 19% -> 9% of each run, Pallas kernels for 0% -> 0%
where the time goes in v3:
time: 82.5 us; the launch traced here: 82 us
  starting transfers between devices  21.6 us (26%)
  waiting for transfers between devices  21.4 us (26%)
  Pallas kernels  15.6 us (19%)
  blocking collectives  15 us (18%)
  local copies, waits for them, and re-layouts  5.89 us (7%)
  other arithmetic  2.34 us (3%)
    pallas_call x1, Pallas kernels, ladder_call(): pl.pallas_call(functools.partial(ladder_kernel, cols, group, 2 * FOLD), o...  15.6 us
    all_to_all x1, blocking collectives, body(): finals = lax.all_to_all(tall_sum, 'row', 0, 0, tiled=True)  15 us
    all_to_all x1, waiting for transfers between devices, body(): lax.all_to_all(jnp.broadcast_to(block, (groups, held, col_block, FOLD)),...  8.8 us
    all_to_all x1, starting transfers between devices, body(): tall = lax.all_to_all(sent, 'row', 0, 0, tiled=True).reshape(width, inner)  8.35 us
    all_to_all x1, waiting for transfers between devices, body(): pieces = lax.all_to_all(partial_sums, plane, 0, 0, tiled=True)  7.23 us
    all_to_all x1, starting transfers between devices, body(): lax.all_to_all(jnp.broadcast_to(block, (groups, held, col_block, FOLD)),...  6.46 us
    all_to_all x1, waiting for transfers between devices, body(): tall = lax.all_to_all(sent, 'row', 0, 0, tiled=True).reshape(width, inner)  5.4 us
    all_to_all x1, starting transfers between devices, body(): pieces = lax.all_to_all(partial_sums, plane, 0, 0, tiled=True)  3.55 us
  transfers between devices with their start and end apart: 5, of which 3 were waited for; matrix products, arithmetic and copies ran while one was open for 9% of the time, Pallas kernels for 0%

profile of v3, /device:TPU:1, one launch (start us, length us, event | category | flops | bytes accessed | tf_op | source)
XLA Modules:
  0.0 82.0 jit_solution(1724295965627638566)
XLA Ops:
  0.0 0.0 copy-start
  0.0 0.0 copy-start.1
  0.0 3.2 %collective-permute-start.1 = (bf16[8,320,320]{2,1,0:T(8,128)(2,1)}, bf16[8,320,320]{2,1,0:T(8,128)(2,1)}, u32[]{:S(2)}, u32[]{:S(2)}) collective-permute-start(bf16[8,320,320]{2,1,0:T(8,128)(2,1)} %param.5), channel_id=1, source_target_pairs={{0,16},{16,0},{32,48},{48,32},{64,80},{80,64},{96,112},{112,96},{1... | collective-permute-start | bytes 4915208 | tf_op jit(solution)/shard_map/ppermute | solution.py:163
  3.2 0.0 collective-permute-start
  3.2 0.8 reshape.63
  4.0 0.7 broadcast_in_dim.14
  4.7 8.4 %all-to-all-start = ((bf16[16,20,80]{2,1,0:T(8,128)(2,1)}), bf16[16,20,80]{2,1,0:T(8,128)(2,1)S(1)}, u32[]{:S(2)}, u32[]{:S(2)}) async-start(bf16[16,20,80]{2,1,0:T(8,128)(2,1)} %bitcast.3), calls=%async_computation | async-start | bytes 196608 | tf_op jit(solution)/shard_map/all_to_all | solution.py:179
  13.0 0.8 broadcast_in_dim.37.down_ref
  13.8 0.8 dynamic_slice.13
  14.6 0.7 broadcast_xor_fusion
  15.3 0.1 eq.35
  15.4 0.7 pad.9
  16.1 5.4 %all-to-all-done = bf16[16,20,80]{2,1,0:T(8,128)(2,1)S(1)} async-done(((bf16[16,20,80]{2,1,0:T(8,128)(2,1)}), bf16[16,20,80]{2,1,0:T(8,128)(2,1)S(1)}, u32[]{:S(2)}, u32[]{:S(2)}) %all-to-all-start) | async-done | bytes 51232 | tf_op jit(solution)/shard_map/all_to_all | solution.py:179
  21.5 0.8 compare_select_fusion
  22.4 0.1 copy.18
  22.5 0.8 broadcast_in_dim.33
  23.3 6.5 %all-to-all-start.1 = ((bf16[16,2,40,128]{3,2,1,0:T(8,128)(2,1)}), bf16[16,2,40,128]{3,2,1,0:T(8,128)(2,1)S(1)}, u32[]{:S(2)}, u32[]{:S(2)}) async-start(bf16[16,2,40,128]{3,2,1,0:T(8,128)(2,1)} %broadcast_in_dim.33), calls=%async_computation.1 | async-start | bytes 655360 | tf_op jit(solution)/shard_map/all_to_all | solution.py:183
  29.7 0.0 collective-permute-done
  29.8 0.0 copy-done.1
  29.8 0.1 constant_dynamic-slice_fusion.1
  29.9 0.1 reshape.62.pair_ref
  30.0 8.8 %all-to-all-done.1.t_ref = bf16[16,2,40,128]{3,2,1,0:T(8,128)(2,1)S(1)} async-done(((bf16[16,2,40,128]{3,2,1,0:T(8,128)(2,1)}), bf16[16,2,40,128]{3,2,1,0:T(8,128)(2,1)S(1)}, u32[]{:S(2)}, u32[]{:S(2)}) %all-to-all-start.1) | async-done | bytes 327712 | tf_op jit(solution)/shard_map/all_to_all | solution.py:183
  38.8 0.0 collective-permute-done.1
  38.8 0.0 copy-done
  38.8 15.6 %shard_map.46 = bf16[16,2,40,128]{3,2,1,0:T(8,128)(2,1)} custom-call(s32[4]{0:T(128)S(1)} %reshape.62.pair_ref, bf16[16,2,40,128]{3,2,1,0:T(8,128)(2,1)S(1)} %all-to-all-done.1.t_ref, bf16[2560,320]{1,0:T(8,128)(2,1)S(1)} %bitcast.17, bf16[2560,320]{1,0:T(8,128)(2,1)} %bitcast.7.other_ref, s32[320,1]{1,0:T(8,128)S(1)} %broadcast_in_dim.37.down_ref, ...), custom_call_target="tpu_custom_call" | custom-call | tf_op jit(solution)/shard_map/pallas_call | solution.py:129
  54.4 3.6 %all-to-all-start.2 = ((bf16[16,2,40,128]{3,2,1,0:T(8,128)(2,1)}), bf16[16,2,40,128]{3,2,1,0:T(8,128)(2,1)S(1)}, u32[]{:S(2)}, u32[]{:S(2)}) async-start(bf16[16,2,40,128]{3,2,1,0:T(8,128)(2,1)} %shard_map.46), calls=%async_computation.2 | async-start | bytes 655360 | tf_op jit(solution)/shard_map/all_to_all | solution.py:189
  57.9 0.8 dynamic_slice.15
  58.7 7.2 %all-to-all-done.2 = bf16[16,2,40,128]{3,2,1,0:T(8,128)(2,1)S(1)} async-done(((bf16[16,2,40,128]{3,2,1,0:T(8,128)(2,1)}), bf16[16,2,40,128]{3,2,1,0:T(8,128)(2,1)S(1)}, u32[]{:S(2)}, u32[]{:S(2)}) %all-to-all-start.2) | async-done | bytes 327712 | tf_op jit(solution)/shard_map/all_to_all | solution.py:189
  65.9 0.1 convert_reduce_fusion
  66.0 0.1 copy.20
  66.1 15.0 %all_to_all.20 = f32[16,20,80]{2,1,0:T(8,128)S(1)} all-to-all(f32[16,20,80]{2,1,0:T(8,128)S(1)} %reshape.69), channel_id=1, replica_groups=mesh['row'=16,'col'=8,'pair'=2] {'row'}, dimensions={0} | all-to-all | bytes 204800 | tf_op jit(solution)/shard_map/all_to_all | solution.py:193
  81.2 0.1 reshape.71
  81.3 0.7 compare_select_fusion.1
  (12 shorter events, 0.2 us)
Async XLA Ops:
  0.0 38.8 %copy-start = (bf16[8,320,320]{2,1,0:T(8,128)(2,1)S(1)}, bf16[8,320,320]{2,1,0:T(8,128)(2,1)}, u32[]{:S(2)}) copy-start(bf16[8,320,320]{2,1,0:T(8,128)(2,1)} %param.5) | copy-start | bytes 4915204
  0.0 29.8 %copy-start.1 = (s32[4]{0:T(128)S(1)}, s32[4]{0:T(128)}, u32[]{:S(2)}) copy-start(s32[4]{0:T(128)} %param.7) | copy-start | bytes 52
  0.0 38.8 %collective-permute-start.1 = (bf16[8,320,320]{2,1,0:T(8,128)(2,1)}, bf16[8,320,320]{2,1,0:T(8,128)(2,1)}, u32[]{:S(2)}, u32[]{:S(2)}) collective-permute-start(bf16[8,320,320]{2,1,0:T(8,128)(2,1)} %param.5), channel_id=1, source_target_pairs={{0,16},{16,0},{32,48},{48,32},{64,80},{80,64},{96,112},{112,96},{1... | collective-permute-start | bytes 4915208 | tf_op jit(solution)/shard_map/ppermute | solution.py:163
  3.2 26.5 %collective-permute-start = (s32[4]{0:T(128)}, s32[4]{0:T(128)S(1)}, u32[]{:S(2)}, u32[]{:S(2)}) collective-permute-start(s32[4]{0:T(128)} %param.7), channel_id=1, source_target_pairs={{0,1},{1,0},{2,3},{3,2},{4,5},{5,4},{6,7},{7,6},{8,9},{9,8},{10,11... | collective-permute-start | bytes 56 | tf_op jit(solution)/shard_map/ppermute | solution.py:164
  4.7 16.8 %all-to-all-start = ((bf16[16,20,80]{2,1,0:T(8,128)(2,1)}), bf16[16,20,80]{2,1,0:T(8,128)(2,1)S(1)}, u32[]{:S(2)}, u32[]{:S(2)}) async-start(bf16[16,20,80]{2,1,0:T(8,128)(2,1)} %bitcast.3), calls=%async_computation | async-start | bytes 196608 | tf_op jit(solution)/shard_map/all_to_all | solution.py:179
  23.3 15.5 %all-to-all-start.1 = ((bf16[16,2,40,128]{3,2,1,0:T(8,128)(2,1)}), bf16[16,2,40,128]{3,2,1,0:T(8,128)(2,1)S(1)}, u32[]{:S(2)}, u32[]{:S(2)}) async-start(bf16[16,2,40,128]{3,2,1,0:T(8,128)(2,1)} %broadcast_in_dim.33), calls=%async_computation.1 | async-start | bytes 655360 | tf_op jit(solution)/shard_map/all_to_all | solution.py:183
  54.4 11.6 %all-to-all-start.2 = ((bf16[16,2,40,128]{3,2,1,0:T(8,128)(2,1)}), bf16[16,2,40,128]{3,2,1,0:T(8,128)(2,1)S(1)}, u32[]{:S(2)}, u32[]{:S(2)}) async-start(bf16[16,2,40,128]{3,2,1,0:T(8,128)(2,1)} %shard_map.46), calls=%async_computation.2 | async-start | bytes 655360 | tf_op jit(solution)/shard_map/all_to_all | solution.py:189

commit v4 on v3

--- a/solution.py
+++ b/solution.py
@@ -12,12 +12,36 @@
 CORES = 2
 
 
-def fold_rows(x):
-    total = x[:FOLD]
-    for start in range(FOLD, x.shape[0], FOLD):
-        piece = x[start : start + FOLD]
-        total = total + jnp.pad(piece, ((0, FOLD - piece.shape[0]), (0, 0)))
-    return total
+def fold_kernel(tall_ref, down_ref, partner_ref, out_ref):
+    groups, held, col_block, _ = out_ref.shape
+    tall = jnp.concatenate(
+        [tall_ref[r].astype(jnp.float32) for r in range(tall_ref.shape[0])], axis=0
+    )
+    tall = jnp.where(down_ref[...] == partner_ref[...], tall, 0.0)
+    folded = tall[:FOLD]
+    for start in range(FOLD, tall.shape[0], FOLD):
+        piece = tall[start : start + FOLD]
+        short = FOLD - piece.shape[0]
+        if short:
+            piece = jnp.concatenate([piece, jnp.zeros((short, piece.shape[1]), jnp.float32)], axis=0)
+        folded = folded + piece
+    block = folded.T.astype(out_ref.dtype)
+    for j in range(held):
+        part = block[j * col_block : (j + 1) * col_block]
+        for m in range(groups):
+            out_ref[m, j] = part
+
+
+def fold_call(tall, down, partner, shape):
+    vmem = pl.BlockSpec(memory_space=pltpu.VMEM)
+    close = functools.partial(pltpu.with_memory_space_constraint, memory_space=pltpu.VMEM)
+    return pl.pallas_call(
+        fold_kernel,
+        out_shape=pltpu.VMEM(shape, tall.dtype),
+        in_specs=[vmem] * 3,
+        out_specs=vmem,
+        compiler_params=pltpu.CompilerParams(vmem_limit_bytes=8 * 2**20),
+    )(close(tall), close(down), close(partner))
 
 
 def unfold_rows(x, width):
@@ -31,8 +55,8 @@
     lane_group,
     pair_ref,
     t_ref,
-    own_ref,
-    other_ref,
+    near_ref,
+    far_ref,
     down_ref,
     across_ref,
     out_ref,
@@ -44,7 +68,7 @@
     arrived,
 ):
     width = down_ref.shape[0]
-    half_depth = own_ref.shape[0]
+    half_depth = near_ref.shape[0]
     groups, pairs_here = t_ref.shape[0] // cols, t_ref.shape[1]
     pairs = groups * pairs_here
     tiles = -(-width // FOLD)
@@ -52,18 +76,21 @@
     step = group * width
     half_steps = half_depth // step
 
-    fetch = pltpu.make_async_copy(other_ref, stack, arrived)
+    fetch = pltpu.make_async_copy(far_ref, stack, arrived)
     fetch.start()
-    mixed = jnp.bitwise_xor(down_ref[...], across_ref[...])
+    filler = jnp.full((1, tiles * FOLD - width), -1, jnp.int32)
+    mixed = jnp.bitwise_xor(
+        down_ref[...], jnp.concatenate([across_ref[...], filler], axis=1)
+    )
     for p in range(pairs):
         half, at = p // pairs_here, p % pairs_here
         rows = jnp.concatenate(
             [t_ref[q * groups + half, at].astype(jnp.float32) for q in range(cols)], axis=0
         )
-        spread = jnp.where(mixed == pair_ref[p], jnp.concatenate([rows] * tiles, axis=1), 0.0)
+        spread = jnp.where(mixed == pair_ref[p : p + 1, :1], jnp.concatenate([rows] * tiles, axis=1), 0.0)
         amp[p * width : (p + 1) * width, :] = spread.astype(jnp.bfloat16)[:, :width]
 
-    for source, base in ((own_ref, 0), (stack, half_steps)):
+    for source, base in ((near_ref, 0), (stack, half_steps)):
         if base:
             fetch.wait()
 
@@ -105,7 +132,7 @@
         both = jnp.concatenate(
             [both, jnp.zeros((width, tiles * FOLD - width), jnp.float32)], axis=1
         )
-        both = jnp.where(mixed == pair_ref[p], both, 0.0)
+        both = jnp.where(mixed == pair_ref[p : p + 1, :1], both, 0.0)
         folded = both[:, :FOLD]
         for k in range(1, tiles):
             folded = folded + both[:, k * FOLD : (k + 1) * FOLD]
@@ -115,21 +142,18 @@
             )
 
 
-def ladder_call(gathered, own, other, labels, pair_labels, cols):
-    count, width, _ = own.shape
+def ladder_call(gathered, near, far, down, across, pair_labels, cols):
+    count, width, _ = near.shape
     pairs = pair_labels.shape[0]
-    tiles = -(-width // FOLD)
     group = 4
     depth, lanes = 2 * count * width, pairs * width
-    down = labels[:, None]
-    across = jnp.pad(labels, (0, tiles * FOLD - width), constant_values=-1)[None, :]
     vmem = pl.BlockSpec(memory_space=pltpu.VMEM)
     anywhere = pl.BlockSpec(memory_space=pl.ANY)
     close = functools.partial(pltpu.with_memory_space_constraint, memory_space=pltpu.VMEM)
     return pl.pallas_call(
         functools.partial(ladder_kernel, cols, group, 2 * FOLD),
-        out_shape=jax.ShapeDtypeStruct(gathered.shape, jnp.bfloat16),
-        in_specs=[pl.BlockSpec(memory_space=pltpu.SMEM), vmem, vmem, anywhere, vmem, vmem],
+        out_shape=pltpu.VMEM(gathered.shape, jnp.bfloat16),
+        in_specs=[vmem, vmem, vmem, anywhere, vmem, vmem],
         out_specs=vmem,
         scratch_shapes=[
             pltpu.VMEM((depth, lanes), jnp.bfloat16),
@@ -139,12 +163,12 @@
             pltpu.VMEM((count * width, width), jnp.bfloat16),
             pltpu.SemaphoreType.DMA(()),
         ],
-        compiler_params=pltpu.CompilerParams(vmem_limit_bytes=48 * 2**20),
+        compiler_params=pltpu.CompilerParams(vmem_limit_bytes=40 * 2**20),
     )(
-        pair_labels,
+        close(jnp.broadcast_to(pair_labels[:, None], (pairs, FOLD))),
         close(gathered),
-        close(own.reshape(count * width, width)),
-        other.reshape(count * width, width),
+        close(near.reshape(count * width, width)),
+        pltpu.with_memory_space_constraint(far.reshape(count * width, width), pltpu.HBM),
         close(down),
         close(across),
     )
@@ -170,30 +194,29 @@
 
     row_labels = lax.dynamic_slice_in_dim(vir_irrep, lax.axis_index("row") * row_block, row_block)
     col_labels = lax.dynamic_slice_in_dim(vir_irrep, lax.axis_index("col") * col_block, col_block)
-    partner = jnp.bitwise_xor(pair_irrep[:, None], col_labels[None, :])
-    partner_held = lax.dynamic_slice_in_dim(partner, core * held, held, axis=0).reshape(1, inner)
+    pairs_held = lax.dynamic_slice_in_dim(pair_irrep, core * held, held)
+    partner = jnp.bitwise_xor(pairs_held[:, None], col_labels[None, :]).reshape(1, inner)
+    down, across = vir_irrep[:, None], vir_irrep[None, :]
 
     halves = amplitudes.reshape(row_block, CORES, inner).transpose(1, 0, 2)
     sent = jnp.broadcast_to(halves[None], (rows // CORES, CORES, row_block, inner))
     sent = sent.reshape(rows, row_block, inner)
-    tall = lax.all_to_all(sent, "row", 0, 0, tiled=True).reshape(width, inner)
-    tall = jnp.where(vir_irrep[:, None] == partner_held, tall, jnp.zeros_like(tall))
-    block = fold_rows(tall).T.reshape(1, held, col_block, FOLD)
+    tall = lax.all_to_all(sent, "row", 0, 0, tiled=True)
     groups = cols * lax.axis_size("pair")
-    gathered = lax.all_to_all(
-        jnp.broadcast_to(block, (groups, held, col_block, FOLD)), plane, 0, 0, tiled=True
-    )
-
-    partial_sums = ladder_call(gathered, factors, other_factors, vir_irrep, pair_labels, cols)
+    block = fold_call(tall, down, partner, (groups, held, col_block, FOLD))
+    gathered = lax.all_to_all(block, plane, 0, 0, tiled=True)
+
+    partial_sums = ladder_call(gathered, other_factors, factors, down, across, pair_labels, cols)
 
     pieces = lax.all_to_all(partial_sums, plane, 0, 0, tiled=True)
     summed = jnp.sum(pieces.astype(jnp.float32), axis=0).reshape(inner, FOLD)
     tall_sum = unfold_rows(summed.T, width).reshape(rows, row_block, inner)
-    tall_sum, row_labels = lax.optimization_barrier((tall_sum, row_labels))
+    mixed = jnp.bitwise_xor(row_labels[:, None, None], col_labels[None, None, :])
+    allowed = mixed == pair_irrep[None, :, None]
+    tall_sum, allowed = lax.optimization_barrier((tall_sum, allowed))
     finals = lax.all_to_all(tall_sum, "row", 0, 0, tiled=True)
     ladder = jnp.sum(finals.reshape(rows // CORES, CORES, row_block, inner), axis=0)
     ladder = ladder.transpose(1, 0, 2).reshape(row_block, pairs_here, col_block)
-    allowed = row_labels[:, None, None] == partner[None]
     return jnp.where(allowed, ladder, jnp.zeros_like(ladder))
 
 

time: 82.5 us -> 80.4 us (0.975)
  waiting for transfers between devices: 21.4 us -> 19.3 us
    all_to_all x2, waiting for transfers between devices: 14.2 us -> 11.5 us  [the longest x1 8.16 us: body(): gathered = lax.all_to_all(block, plane, 0, 0, tiled=True)]
    ppermute x1, starting transfers between devices: 0.01 us -> 1.21 us  [body(): other_pairs = lax.ppermute(pair_irrep, 'pair', [(0, 1), (1, 0)])]
    all_to_all x2, starting transfers between devices: 14.8 us -> 13.6 us  [the longest x1 6.88 us: body(): tall = lax.all_to_all(sent, 'row', 0, 0, tiled=True)]
    pallas_call x0 -> x1, Pallas kernels: none -> 0.89 us  [fold_call(): pl.pallas_call(fold_kernel, out_shape=pltpu.VMEM(shape, tall.dtype), in_s...]
  transfers between devices with their start and end apart: 5 -> 5, of which waited for: 3 -> 3; matrix products, arithmetic and copies ran while one was open for 9% -> 8% of each run, Pallas kernels for 0% -> 1%
where the time goes in v4:
time: 80.4 us; the launch traced here: 79.9 us
  starting transfers between devices  21.6 us (27%)
  waiting for transfers between devices  19.3 us (24%)
  Pallas kernels  15.9 us (20%)
  blocking collectives  15.5 us (19%)
  local copies, waits for them, and re-layouts  5.75 us (7%)
  other arithmetic  1.62 us (2%)
    all_to_all x1, blocking collectives, body(): finals = lax.all_to_all(tall_sum, 'row', 0, 0, tiled=True)  15.5 us
    pallas_call x1, Pallas kernels, ladder_call(): pl.pallas_call(functools.partial(ladder_kernel, cols, group, 2 * FOLD), o...  15 us
    all_to_all x1, waiting for transfers between devices, body(): gathered = lax.all_to_all(block, plane, 0, 0, tiled=True)  8.16 us
    all_to_all x1, waiting for transfers between devices, body(): pieces = lax.all_to_all(partial_sums, plane, 0, 0, tiled=True)  7.83 us
    all_to_all x1, starting transfers between devices, body(): tall = lax.all_to_all(sent, 'row', 0, 0, tiled=True)  6.88 us
    all_to_all x1, starting transfers between devices, body(): gathered = lax.all_to_all(block, plane, 0, 0, tiled=True)  6.75 us
    all_to_all x1, starting transfers between devices, body(): pieces = lax.all_to_all(partial_sums, plane, 0, 0, tiled=True)  3.55 us
    all_to_all x1, waiting for transfers between devices, body(): tall = lax.all_to_all(sent, 'row', 0, 0, tiled=True)  3.34 us
  transfers between devices with their start and end apart: 5, of which 3 were waited for; matrix products, arithmetic and copies ran while one was open for 8% of the time, Pallas kernels for 1%

profile of v4, /device:TPU:1, one launch (start us, length us, event | category | flops | bytes accessed | tf_op | source)
XLA Modules:
  0.0 79.9 jit_solution(13693748202183255480)
XLA Ops:
  0.0 3.2 %collective-permute-start.1 = (bf16[8,320,320]{2,1,0:T(8,128)(2,1)}, bf16[8,320,320]{2,1,0:T(8,128)(2,1)S(1)}, u32[]{:S(2)}, u32[]{:S(2)}) collective-permute-start(bf16[8,320,320]{2,1,0:T(8,128)(2,1)} %param.5), channel_id=1, source_target_pairs={{0,16},{16,0},{32,48},{48,32},{64,80},{80,64},{96,112},{112,96},{1... | collective-permute-start | bytes 4915208 | tf_op jit(solution)/shard_map/ppermute | solution.py:187
  3.2 0.8 %reshape.80 = bf16[20,2,80]{2,1,0:T(2,128)(2,1)S(1)} reshape(bf16[20,4,40]{2,1,0:T(4,128)(2,1)} %param.4) | data formatting | bytes 12800 | tf_op jit(solution)/shard_map/reshape | solution.py:201
  4.0 0.7 broadcast_in_dim.14
  4.7 6.9 %all-to-all-start = ((bf16[16,20,80]{2,1,0:T(8,128)(2,1)}), bf16[16,20,80]{2,1,0:T(8,128)(2,1)S(1)}, u32[]{:S(2)}, u32[]{:S(2)}) async-start(bf16[16,20,80]{2,1,0:T(8,128)(2,1)} %bitcast.3), calls=%async_computation | async-start | bytes 196608 | tf_op jit(solution)/shard_map/all_to_all | solution.py:204
  11.6 1.2 %collective-permute-start = (s32[4]{0:T(128)}, s32[4]{0:T(128)S(1)}, u32[]{:S(2)}, u32[]{:S(2)}) collective-permute-start(s32[4]{0:T(128)} %param.7), channel_id=1, source_target_pairs={{0,1},{1,0},{2,3},{3,2},{4,5},{5,4},{6,7},{7,6},{8,9},{9,8},{10,11... | collective-permute-start | bytes 56 | tf_op jit(solution)/shard_map/ppermute | solution.py:188
  12.8 0.8 dynamic_slice.13
  13.5 0.8 dynamic_slice.14
  14.3 0.1 broadcast_xor_fusion.1
  14.4 0.8 broadcast_in_dim.33.down_ref
  15.1 0.7 broadcast_in_dim.31.across_ref
  15.8 0.1 xor.44.partner_ref
  15.9 0.8 dynamic_slice.15
  16.7 3.3 %all-to-all-done.tall_ref = bf16[16,20,80]{2,1,0:T(8,128)(2,1)S(1)} async-done(((bf16[16,20,80]{2,1,0:T(8,128)(2,1)}), bf16[16,20,80]{2,1,0:T(8,128)(2,1)S(1)}, u32[]{:S(2)}, u32[]{:S(2)}) %all-to-all-start) | async-done | bytes 51232 | tf_op jit(solution)/shard_map/all_to_all | solution.py:204
  20.0 0.9 %shard_map.46 = bf16[16,2,40,128]{3,2,1,0:T(8,128)(2,1)} custom-call(bf16[16,20,80]{2,1,0:T(8,128)(2,1)S(1)} %all-to-all-done.tall_ref, s32[320,1]{1,0:T(8,128)S(1)} %broadcast_in_dim.33.down_ref, s32[1,80]{1,0:T(1,128)S(1)} %xor.44.partner_ref), custom_call_target="tpu_custom_call" | custom-call | tf_op jit(solution)/shard_map/pallas_call | solution.py:38
  20.9 6.8 %all-to-all-start.1 = ((bf16[16,2,40,128]{3,2,1,0:T(8,128)(2,1)}), bf16[16,2,40,128]{3,2,1,0:T(8,128)(2,1)S(1)}, u32[]{:S(2)}, u32[]{:S(2)}) async-start(bf16[16,2,40,128]{3,2,1,0:T(8,128)(2,1)} %shard_map.46), calls=%async_computation.1 | async-start | bytes 655360 | tf_op jit(solution)/shard_map/all_to_all | solution.py:207
  27.7 0.0 collective-permute-done
  27.7 0.7 fusion
  28.4 0.1 constant_dynamic-slice_fusion
  28.4 0.1 broadcast_in_dim.12
  28.5 8.2 %all-to-all-done.1.t_ref = bf16[16,2,40,128]{3,2,1,0:T(8,128)(2,1)S(1)} async-done(((bf16[16,2,40,128]{3,2,1,0:T(8,128)(2,1)}), bf16[16,2,40,128]{3,2,1,0:T(8,128)(2,1)S(1)}, u32[]{:S(2)}, u32[]{:S(2)}) %all-to-all-start.1) | async-done | bytes 327712 | tf_op jit(solution)/shard_map/all_to_all | solution.py:207
  36.7 0.0 collective-permute-done.1
  36.7 0.1 broadcast_in_dim.13.pair_ref
  36.8 0.0 copy-start
  36.8 15.0 %shard_map.47 = bf16[16,2,40,128]{3,2,1,0:T(8,128)(2,1)} custom-call(s32[4,128]{1,0:T(4,128)S(1)} %broadcast_in_dim.13.pair_ref, bf16[16,2,40,128]{3,2,1,0:T(8,128)(2,1)S(1)} %all-to-all-done.1.t_ref, bf16[2560,320]{1,0:T(8,128)(2,1)S(1)} %bitcast.14, bf16[2560,320]{1,0:T(8,128)(2,1)} %bitcast.15, s32[320,1]{1,0:T(8,128)S(1)} %broadcast_in_dim.33.down_ref, ...), custom_call_target="tpu_custom_call" | custom-call | tf_op jit(solution)/shard_map/pallas_call | solution.py:153
  51.8 3.6 %all-to-all-start.2 = ((bf16[16,2,40,128]{3,2,1,0:T(8,128)(2,1)}), bf16[16,2,40,128]{3,2,1,0:T(8,128)(2,1)S(1)}, u32[]{:S(2)}, u32[]{:S(2)}) async-start(bf16[16,2,40,128]{3,2,1,0:T(8,128)(2,1)} %shard_map.47), calls=%async_computation.2 | async-start | bytes 655360 | tf_op jit(solution)/shard_map/all_to_all | solution.py:211
  55.4 0.1 broadcast_xor_fusion
  55.4 0.0 copy-done
  55.4 0.1 broadcast_compare_fusion
  55.5 7.8 %all-to-all-done.2 = bf16[16,2,40,128]{3,2,1,0:T(8,128)(2,1)S(1)} async-done(((bf16[16,2,40,128]{3,2,1,0:T(8,128)(2,1)}), bf16[16,2,40,128]{3,2,1,0:T(8,128)(2,1)S(1)}, u32[]{:S(2)}, u32[]{:S(2)}) %all-to-all-start.2) | async-done | bytes 327712 | tf_op jit(solution)/shard_map/all_to_all | solution.py:211
  63.4 0.1 convert_reduce_fusion
  63.4 0.1 copy.20
  63.6 15.5 %all_to_all.20 = f32[16,20,80]{2,1,0:T(8,128)S(1)} all-to-all(f32[16,20,80]{2,1,0:T(8,128)S(1)} %reshape.85), channel_id=1, replica_groups=mesh['row'=16,'col'=8,'pair'=2] {'row'}, dimensions={0} | all-to-all | bytes 204800 | tf_op jit(solution)/shard_map/all_to_all | solution.py:217
  79.1 0.1 reshape.87
  79.2 0.6 broadcast_select_fusion
  (6 shorter events, 0.1 us)
Async XLA Ops:
  0.0 36.7 %collective-permute-start.1 = (bf16[8,320,320]{2,1,0:T(8,128)(2,1)}, bf16[8,320,320]{2,1,0:T(8,128)(2,1)S(1)}, u32[]{:S(2)}, u32[]{:S(2)}) collective-permute-start(bf16[8,320,320]{2,1,0:T(8,128)(2,1)} %param.5), channel_id=1, source_target_pairs={{0,16},{16,0},{32,48},{48,32},{64,80},{80,64},{96,112},{112,96},{1... | collective-permute-start | bytes 4915208 | tf_op jit(solution)/shard_map/ppermute | solution.py:187
  4.7 15.3 %all-to-all-start = ((bf16[16,20,80]{2,1,0:T(8,128)(2,1)}), bf16[16,20,80]{2,1,0:T(8,128)(2,1)S(1)}, u32[]{:S(2)}, u32[]{:S(2)}) async-start(bf16[16,20,80]{2,1,0:T(8,128)(2,1)} %bitcast.3), calls=%async_computation | async-start | bytes 196608 | tf_op jit(solution)/shard_map/all_to_all | solution.py:204
  11.6 16.1 %collective-permute-start = (s32[4]{0:T(128)}, s32[4]{0:T(128)S(1)}, u32[]{:S(2)}, u32[]{:S(2)}) collective-permute-start(s32[4]{0:T(128)} %param.7), channel_id=1, source_target_pairs={{0,1},{1,0},{2,3},{3,2},{4,5},{5,4},{6,7},{7,6},{8,9},{9,8},{10,11... | collective-permute-start | bytes 56 | tf_op jit(solution)/shard_map/ppermute | solution.py:188
  20.9 15.8 %all-to-all-start.1 = ((bf16[16,2,40,128]{3,2,1,0:T(8,128)(2,1)}), bf16[16,2,40,128]{3,2,1,0:T(8,128)(2,1)S(1)}, u32[]{:S(2)}, u32[]{:S(2)}) async-start(bf16[16,2,40,128]{3,2,1,0:T(8,128)(2,1)} %shard_map.46), calls=%async_computation.1 | async-start | bytes 655360 | tf_op jit(solution)/shard_map/all_to_all | solution.py:207
  36.8 18.7 %copy-start = (s32[4]{0:T(128)S(1)}, s32[4]{0:T(128)}, u32[]{:S(2)}) copy-start(s32[4]{0:T(128)} %param.7) | copy-start | bytes 52
  51.8 11.6 %all-to-all-start.2 = ((bf16[16,2,40,128]{3,2,1,0:T(8,128)(2,1)}), bf16[16,2,40,128]{3,2,1,0:T(8,128)(2,1)S(1)}, u32[]{:S(2)}, u32[]{:S(2)}) async-start(bf16[16,2,40,128]{3,2,1,0:T(8,128)(2,1)} %shard_map.47), calls=%async_computation.2 | async-start | bytes 655360 | tf_op jit(solution)/shard_map/all_to_all | solution.py:211

commit v5 on v4

--- a/solution.py
+++ b/solution.py
@@ -185,18 +185,11 @@
     swap = [(k, k ^ 1) for k in range(rows)]
 
     other_factors = lax.ppermute(factors, "row", swap)
-    other_pairs = lax.ppermute(pair_irrep, "pair", [(0, 1), (1, 0)])
-    first = lax.axis_index("pair") == 0
-    pair_labels = jnp.stack(
-        [jnp.where(first, pair_irrep, other_pairs), jnp.where(first, other_pairs, pair_irrep)]
-    )
-    pair_labels = lax.dynamic_slice_in_dim(pair_labels, core * held, held, axis=1).reshape(-1)
-
-    row_labels = lax.dynamic_slice_in_dim(vir_irrep, lax.axis_index("row") * row_block, row_block)
+
     col_labels = lax.dynamic_slice_in_dim(vir_irrep, lax.axis_index("col") * col_block, col_block)
     pairs_held = lax.dynamic_slice_in_dim(pair_irrep, core * held, held)
     partner = jnp.bitwise_xor(pairs_held[:, None], col_labels[None, :]).reshape(1, inner)
-    down, across = vir_irrep[:, None], vir_irrep[None, :]
+    down = vir_irrep[:, None]
 
     halves = amplitudes.reshape(row_block, CORES, inner).transpose(1, 0, 2)
     sent = jnp.broadcast_to(halves[None], (rows // CORES, CORES, row_block, inner))
@@ -204,7 +197,17 @@
     tall = lax.all_to_all(sent, "row", 0, 0, tiled=True)
     groups = cols * lax.axis_size("pair")
     block = fold_call(tall, down, partner, (groups, held, col_block, FOLD))
+    block, late_vir, late_pair = lax.optimization_barrier((block, vir_irrep, pair_irrep))
     gathered = lax.all_to_all(block, plane, 0, 0, tiled=True)
+
+    other_pairs = lax.ppermute(late_pair, "pair", [(0, 1), (1, 0)])
+    first = lax.axis_index("pair") == 0
+    pair_labels = jnp.stack(
+        [jnp.where(first, late_pair, other_pairs), jnp.where(first, other_pairs, late_pair)]
+    )
+    pair_labels = lax.dynamic_slice_in_dim(pair_labels, core * held, held, axis=1).reshape(-1)
+    across = late_vir[None, :]
+    row_labels = lax.dynamic_slice_in_dim(late_vir, lax.axis_index("row") * row_block, row_block)
 
     partial_sums = ladder_call(gathered, other_factors, factors, down, across, pair_labels, cols)
 

time: 80.4 us -> 80.8 us (level)
  waiting for transfers between devices: 19.3 us -> 20.6 us
    all_to_all x1, waiting for transfers between devices: 3.34 us -> 6.03 us  [body(): tall = lax.all_to_all(sent, 'row', 0, 0, tiled=True)]
    all_to_all x1, waiting for transfers between devices: 8.16 us -> 6.69 us  [body(): gathered = lax.all_to_all(block, plane, 0, 0, tiled=True)]
where the time goes in v5:
time: 80.8 us; the launch traced here: 80.3 us
  starting transfers between devices  21.3 us (26%)
  waiting for transfers between devices  20.6 us (25%)
  Pallas kernels  15.9 us (20%)
  blocking collectives  15.1 us (19%)
  local copies, waits for them, and re-layouts  5.71 us (7%)
  other arithmetic  1.62 us (2%)
    all_to_all x1, blocking collectives, body(): finals = lax.all_to_all(tall_sum, 'row', 0, 0, tiled=True)  15.1 us
    pallas_call x1, Pallas kernels, ladder_call(): pl.pallas_call(functools.partial(ladder_kernel, cols, group, 2 * FOLD), o...  15 us
    all_to_all x1, waiting for transfers between devices, body(): pieces = lax.all_to_all(partial_sums, plane, 0, 0, tiled=True)  7.84 us
    all_to_all x1, starting transfers between devices, body(): tall = lax.all_to_all(sent, 'row', 0, 0, tiled=True)  6.88 us
    all_to_all x1, waiting for transfers between devices, body(): gathered = lax.all_to_all(block, plane, 0, 0, tiled=True)  6.69 us
    all_to_all x1, starting transfers between devices, body(): gathered = lax.all_to_all(block, plane, 0, 0, tiled=True)  6.46 us
    all_to_all x1, waiting for transfers between devices, body(): tall = lax.all_to_all(sent, 'row', 0, 0, tiled=True)  6.03 us
    all_to_all x1, starting transfers between devices, body(): pieces = lax.all_to_all(partial_sums, plane, 0, 0, tiled=True)  3.55 us
  transfers between devices with their start and end apart: 5, of which 3 were waited for; matrix products, arithmetic and copies ran while one was open for 8% of the time, Pallas kernels for 1%

profile of v5, /device:TPU:1, one launch (start us, length us, event | category | flops | bytes accessed | tf_op | source)
XLA Modules:
  0.0 80.3 jit_solution(7420603523507617408)
XLA Ops:
  0.0 3.2 %collective-permute-start.1 = (bf16[8,320,320]{2,1,0:T(8,128)(2,1)}, bf16[8,320,320]{2,1,0:T(8,128)(2,1)S(1)}, u32[]{:S(2)}, u32[]{:S(2)}) collective-permute-start(bf16[8,320,320]{2,1,0:T(8,128)(2,1)} %param.5), channel_id=1, source_target_pairs={{0,16},{16,0},{32,48},{48,32},{64,80},{80,64},{96,112},{112,96},{1... | collective-permute-start | bytes 4915208 | tf_op jit(solution)/shard_map/ppermute | solution.py:187
  3.2 0.8 %reshape.80 = bf16[20,2,80]{2,1,0:T(2,128)(2,1)S(1)} reshape(bf16[20,4,40]{2,1,0:T(4,128)(2,1)} %param.4) | data formatting | bytes 12800 | tf_op jit(solution)/shard_map/reshape | solution.py:194
  4.0 0.7 broadcast_in_dim.12
  4.7 6.9 %all-to-all-start = ((bf16[16,20,80]{2,1,0:T(8,128)(2,1)}), bf16[16,20,80]{2,1,0:T(8,128)(2,1)S(1)}, u32[]{:S(2)}, u32[]{:S(2)}) async-start(bf16[16,20,80]{2,1,0:T(8,128)(2,1)} %bitcast.1), calls=%async_computation | async-start | bytes 196608 | tf_op jit(solution)/shard_map/all_to_all | solution.py:197
  11.6 0.7 dynamic_slice.12
  12.3 0.8 dynamic_slice.13
  13.0 0.1 broadcast_xor_fusion.1
  13.1 0.8 broadcast_in_dim.33.down_ref
  13.9 0.1 xor.44.partner_ref
  14.0 6.0 %all-to-all-done.tall_ref = bf16[16,20,80]{2,1,0:T(8,128)(2,1)S(1)} async-done(((bf16[16,20,80]{2,1,0:T(8,128)(2,1)}), bf16[16,20,80]{2,1,0:T(8,128)(2,1)S(1)}, u32[]{:S(2)}, u32[]{:S(2)}) %all-to-all-start) | async-done | bytes 51232 | tf_op jit(solution)/shard_map/all_to_all | solution.py:197
  20.0 0.9 %shard_map.46 = bf16[16,2,40,128]{3,2,1,0:T(8,128)(2,1)} custom-call(bf16[16,20,80]{2,1,0:T(8,128)(2,1)S(1)} %all-to-all-done.tall_ref, s32[320,1]{1,0:T(8,128)S(1)} %broadcast_in_dim.33.down_ref, s32[1,80]{1,0:T(1,128)S(1)} %xor.44.partner_ref), custom_call_target="tpu_custom_call" | custom-call | tf_op jit(solution)/shard_map/pallas_call | solution.py:38
  20.9 1.2 %collective-permute-start = (s32[4]{0:T(128)}, s32[4]{0:T(128)S(1)}, u32[]{:S(2)}, u32[]{:S(2)}) collective-permute-start(s32[4]{0:T(128)} %param.7), channel_id=1, source_target_pairs={{0,1},{1,0},{2,3},{3,2},{4,5},{5,4},{6,7},{7,6},{8,9},{9,8},{10,11... | collective-permute-start | bytes 56 | tf_op jit(solution)/shard_map/ppermute | solution.py:203
  22.1 6.5 %all-to-all-start.1 = ((bf16[16,2,40,128]{3,2,1,0:T(8,128)(2,1)}), bf16[16,2,40,128]{3,2,1,0:T(8,128)(2,1)S(1)}, u32[]{:S(2)}, u32[]{:S(2)}) async-start(bf16[16,2,40,128]{3,2,1,0:T(8,128)(2,1)} %shard_map.46), calls=%async_computation.1 | async-start | bytes 655360 | tf_op jit(solution)/shard_map/all_to_all | solution.py:201
  28.6 0.7 broadcast_in_dim.31.across_ref
  29.3 0.8 dynamic_slice.15
  30.0 0.0 collective-permute-done
  30.0 0.7 fusion
  30.7 0.1 constant_dynamic-slice_fusion
  30.8 0.1 broadcast_in_dim.14
  30.9 6.7 %all-to-all-done.1.t_ref = bf16[16,2,40,128]{3,2,1,0:T(8,128)(2,1)S(1)} async-done(((bf16[16,2,40,128]{3,2,1,0:T(8,128)(2,1)}), bf16[16,2,40,128]{3,2,1,0:T(8,128)(2,1)S(1)}, u32[]{:S(2)}, u32[]{:S(2)}) %all-to-all-start.1) | async-done | bytes 327712 | tf_op jit(solution)/shard_map/all_to_all | solution.py:201
  37.6 0.0 collective-permute-done.1
  37.6 0.1 broadcast_in_dim.30.pair_ref
  37.6 0.0 copy-start
  37.6 15.0 %shard_map.47 = bf16[16,2,40,128]{3,2,1,0:T(8,128)(2,1)} custom-call(s32[4,128]{1,0:T(4,128)S(1)} %broadcast_in_dim.30.pair_ref, bf16[16,2,40,128]{3,2,1,0:T(8,128)(2,1)S(1)} %all-to-all-done.1.t_ref, bf16[2560,320]{1,0:T(8,128)(2,1)S(1)} %bitcast.14, bf16[2560,320]{1,0:T(8,128)(2,1)} %bitcast.15, s32[320,1]{1,0:T(8,128)S(1)} %broadcast_in_dim.33.down_ref, ...), custom_call_target="tpu_custom_call" | custom-call | tf_op jit(solution)/shard_map/pallas_call | solution.py:153
  52.7 3.6 %all-to-all-start.2 = ((bf16[16,2,40,128]{3,2,1,0:T(8,128)(2,1)}), bf16[16,2,40,128]{3,2,1,0:T(8,128)(2,1)S(1)}, u32[]{:S(2)}, u32[]{:S(2)}) async-start(bf16[16,2,40,128]{3,2,1,0:T(8,128)(2,1)} %shard_map.47), calls=%async_computation.2 | async-start | bytes 655360 | tf_op jit(solution)/shard_map/all_to_all | solution.py:214
  56.2 0.1 broadcast_xor_fusion
  56.3 0.0 copy-done
  56.3 0.1 broadcast_compare_fusion
  56.4 7.8 %all-to-all-done.2 = bf16[16,2,40,128]{3,2,1,0:T(8,128)(2,1)S(1)} async-done(((bf16[16,2,40,128]{3,2,1,0:T(8,128)(2,1)}), bf16[16,2,40,128]{3,2,1,0:T(8,128)(2,1)S(1)}, u32[]{:S(2)}, u32[]{:S(2)}) %all-to-all-start.2) | async-done | bytes 327712 | tf_op jit(solution)/shard_map/all_to_all | solution.py:214
  64.2 0.1 convert_reduce_fusion
  64.3 0.1 copy.20
  64.5 15.1 %all_to_all.20 = f32[16,20,80]{2,1,0:T(8,128)S(1)} all-to-all(f32[16,20,80]{2,1,0:T(8,128)S(1)} %reshape.85), channel_id=1, replica_groups=mesh['row'=16,'col'=8,'pair'=2] {'row'}, dimensions={0} | all-to-all | bytes 204800 | tf_op jit(solution)/shard_map/all_to_all | solution.py:220
  79.6 0.1 reshape.87
  79.7 0.6 broadcast_select_fusion
  (6 shorter events, 0.1 us)
Async XLA Ops:
  0.0 37.6 %collective-permute-start.1 = (bf16[8,320,320]{2,1,0:T(8,128)(2,1)}, bf16[8,320,320]{2,1,0:T(8,128)(2,1)S(1)}, u32[]{:S(2)}, u32[]{:S(2)}) collective-permute-start(bf16[8,320,320]{2,1,0:T(8,128)(2,1)} %param.5), channel_id=1, source_target_pairs={{0,16},{16,0},{32,48},{48,32},{64,80},{80,64},{96,112},{112,96},{1... | collective-permute-start | bytes 4915208 | tf_op jit(solution)/shard_map/ppermute | solution.py:187
  4.7 15.3 %all-to-all-start = ((bf16[16,20,80]{2,1,0:T(8,128)(2,1)}), bf16[16,20,80]{2,1,0:T(8,128)(2,1)S(1)}, u32[]{:S(2)}, u32[]{:S(2)}) async-start(bf16[16,20,80]{2,1,0:T(8,128)(2,1)} %bitcast.1), calls=%async_computation | async-start | bytes 196608 | tf_op jit(solution)/shard_map/all_to_all | solution.py:197
  20.9 9.1 %collective-permute-start = (s32[4]{0:T(128)}, s32[4]{0:T(128)S(1)}, u32[]{:S(2)}, u32[]{:S(2)}) collective-permute-start(s32[4]{0:T(128)} %param.7), channel_id=1, source_target_pairs={{0,1},{1,0},{2,3},{3,2},{4,5},{5,4},{6,7},{7,6},{8,9},{9,8},{10,11... | collective-permute-start | bytes 56 | tf_op jit(solution)/shard_map/ppermute | solution.py:203
  22.1 15.4 %all-to-all-start.1 = ((bf16[16,2,40,128]{3,2,1,0:T(8,128)(2,1)}), bf16[16,2,40,128]{3,2,1,0:T(8,128)(2,1)S(1)}, u32[]{:S(2)}, u32[]{:S(2)}) async-start(bf16[16,2,40,128]{3,2,1,0:T(8,128)(2,1)} %shard_map.46), calls=%async_computation.1 | async-start | bytes 655360 | tf_op jit(solution)/shard_map/all_to_all | solution.py:201
  37.6 18.7 %copy-start = (s32[4]{0:T(128)S(1)}, s32[4]{0:T(128)}, u32[]{:S(2)}) copy-start(s32[4]{0:T(128)} %param.7) | copy-start | bytes 52
  52.7 11.6 %all-to-all-start.2 = ((bf16[16,2,40,128]{3,2,1,0:T(8,128)(2,1)}), bf16[16,2,40,128]{3,2,1,0:T(8,128)(2,1)S(1)}, u32[]{:S(2)}, u32[]{:S(2)}) async-start(bf16[16,2,40,128]{3,2,1,0:T(8,128)(2,1)} %shard_map.47), calls=%async_computation.2 | async-start | bytes 655360 | tf_op jit(solution)/shard_map/all_to_all | solution.py:214

commit v6 on v5

--- a/solution.py
+++ b/solution.py
@@ -44,9 +44,72 @@
     )(close(tall), close(down), close(partner))
 
 
-def unfold_rows(x, width):
-    pieces = [x[: min(FOLD, width - start)] for start in range(0, width, FOLD)]
-    return jnp.concatenate(pieces, axis=0)
+PACK = 16
+
+
+def pack_kernel(row_block, pieces_ref, out_ref):
+    total = pieces_ref[0].astype(jnp.float32)
+    for m in range(1, pieces_ref.shape[0]):
+        total = total + pieces_ref[m].astype(jnp.float32)
+    total = total.reshape(-1, FOLD)
+    lane = lax.broadcasted_iota(jnp.int32, (PACK, FOLD), 1)
+    for r in range(out_ref.shape[0]):
+        packed = jnp.zeros((PACK, FOLD), jnp.float32)
+        for g in range(total.shape[0] // PACK):
+            shift = (g - r) * row_block % FOLD
+            moved = total[g * PACK : (g + 1) * PACK]
+            if shift:
+                moved = pltpu.roll(moved, shift, 1)
+            packed = jnp.where(
+                (lane >= g * row_block) & (lane < (g + 1) * row_block), moved, packed
+            )
+        out_ref[r] = packed
+
+
+def unpack_kernel(finals_ref, down_ref, across_ref, out_ref):
+    row_block, pairs_here, col_block = out_ref.shape
+    held = pairs_here // CORES
+    lines = held * col_block
+    for c in range(CORES):
+        total = finals_ref[c]
+        for z in range(CORES + c, finals_ref.shape[0], CORES):
+            total = total + finals_ref[z]
+        spread = jnp.concatenate(
+            [
+                total if g == 0 else pltpu.roll(total, -g * row_block % FOLD, 1)
+                for g in range(lines // PACK)
+            ],
+            axis=0,
+        )
+        spread = jnp.where(
+            down_ref[:, :1] == across_ref[c : c + 1, :lines], spread.T[:row_block], 0.0
+        )
+        for j in range(held):
+            out_ref[:, c * held + j, :] = spread[:, j * col_block : (j + 1) * col_block]
+
+
+def pack_call(pieces, rows, row_block):
+    close = functools.partial(pltpu.with_memory_space_constraint, memory_space=pltpu.VMEM)
+    vmem = pl.BlockSpec(memory_space=pltpu.VMEM)
+    return pl.pallas_call(
+        functools.partial(pack_kernel, row_block),
+        out_shape=jax.ShapeDtypeStruct((rows, PACK, FOLD), jnp.float32),
+        in_specs=[vmem],
+        out_specs=vmem,
+        compiler_params=pltpu.CompilerParams(vmem_limit_bytes=8 * 2**20),
+    )(close(pieces))
+
+
+def unpack_call(finals, down, across, shape):
+    close = functools.partial(pltpu.with_memory_space_constraint, memory_space=pltpu.VMEM)
+    vmem = pl.BlockSpec(memory_space=pltpu.VMEM)
+    return pl.pallas_call(
+        unpack_kernel,
+        out_shape=jax.ShapeDtypeStruct(shape, jnp.float32),
+        in_specs=[vmem] * 3,
+        out_specs=vmem,
+        compiler_params=pltpu.CompilerParams(vmem_limit_bytes=8 * 2**20),
+    )(close(finals), close(down), close(across))
 
 
 def ladder_kernel(
@@ -127,15 +190,24 @@
 
     for p in range(pairs):
         half, at = p // pairs_here, p % pairs_here
-        ladder = ladders[:, p * width : (p + 1) * width]
-        both = ladder + ladder.T
-        both = jnp.concatenate(
-            [both, jnp.zeros((width, tiles * FOLD - width), jnp.float32)], axis=1
+        ladder = jnp.concatenate(
+            [
+                ladders[:, p * width : (p + 1) * width],
+                jnp.zeros((width, tiles * FOLD - width), jnp.float32),
+            ],
+            axis=1,
         )
-        both = jnp.where(mixed == pair_ref[p : p + 1, :1], both, 0.0)
-        folded = both[:, :FOLD]
-        for k in range(1, tiles):
-            folded = folded + both[:, k * FOLD : (k + 1) * FOLD]
+        ladder = jnp.where(mixed == pair_ref[p : p + 1, :1], ladder, 0.0)
+        folded = ladder[:, :FOLD]
+        tall = ladder[:FOLD]
+        for start in range(FOLD, tiles * FOLD, FOLD):
+            folded = folded + ladder[:, start : start + FOLD]
+            piece = ladder[start : start + FOLD]
+            if piece.shape[0] < FOLD:
+                blank = jnp.zeros((FOLD - piece.shape[0], tiles * FOLD), jnp.float32)
+                piece = jnp.concatenate([piece, blank], axis=0)
+            tall = tall + piece
+        folded = folded + tall.T[:width]
         for q in range(cols):
             out_ref[q * groups + half, at] = folded[q * block : (q + 1) * block].astype(
                 out_ref.dtype
@@ -212,15 +284,13 @@
     partial_sums = ladder_call(gathered, other_factors, factors, down, across, pair_labels, cols)
 
     pieces = lax.all_to_all(partial_sums, plane, 0, 0, tiled=True)
-    summed = jnp.sum(pieces.astype(jnp.float32), axis=0).reshape(inner, FOLD)
-    tall_sum = unfold_rows(summed.T, width).reshape(rows, row_block, inner)
-    mixed = jnp.bitwise_xor(row_labels[:, None, None], col_labels[None, None, :])
-    allowed = mixed == pair_irrep[None, :, None]
-    tall_sum, allowed = lax.optimization_barrier((tall_sum, allowed))
-    finals = lax.all_to_all(tall_sum, "row", 0, 0, tiled=True)
-    ladder = jnp.sum(finals.reshape(rows // CORES, CORES, row_block, inner), axis=0)
-    ladder = ladder.transpose(1, 0, 2).reshape(row_block, pairs_here, col_block)
-    return jnp.where(allowed, ladder, jnp.zeros_like(ladder))
+    packed = pack_call(pieces, rows, row_block)
+    need = jnp.bitwise_xor(pair_irrep[:, None], col_labels[None, :]).reshape(CORES, inner)
+    packed, row_labels, need = lax.optimization_barrier(
+        (packed, jnp.broadcast_to(row_labels[:, None], (row_block, FOLD)), need)
+    )
+    finals = lax.all_to_all(packed, "row", 0, 0, tiled=True)
+    return unpack_call(finals, row_labels, need, amplitudes.shape)
 
 
 def solution(mesh):

time: 80.8 us -> 79.4 us (0.983)
  blocking collectives: 15.1 us -> 14 us
  other arithmetic: 1.62 us -> 0.75 us
    pallas_call x0 -> x2, Pallas kernels: none -> 1.15 us  [the longest x1 0.89 us: unpack_call(): pl.pallas_call(unpack_kernel, out_shape=jax.ShapeDtypeStruct(shape, jnp.f...]
    all_to_all x1, blocking collectives: 15.1 us -> 14 us  [body(): finals = lax.all_to_all(packed, 'row', 0, 0, tiled=True)]
    all_to_all x1, waiting for transfers between devices: 7.84 us -> 6.91 us  [body(): pieces = lax.all_to_all(partial_sums, plane, 0, 0, tiled=True)]
where the time goes in v6:
time: 79.4 us; the launch traced here: 78.9 us
  starting transfers between devices  21.3 us (27%)
  waiting for transfers between devices  20.4 us (26%)
  Pallas kernels  16.5 us (21%)
  blocking collectives  14 us (18%)
  local copies, waits for them, and re-layouts  5.88 us (7%)
    pallas_call x1, Pallas kernels, ladder_call(): pl.pallas_call(functools.partial(ladder_kernel, cols, group, 2 * FOLD), o...  14.5 us
    all_to_all x1, blocking collectives, body(): finals = lax.all_to_all(packed, 'row', 0, 0, tiled=True)  14 us
    all_to_all x1, waiting for transfers between devices, body(): gathered = lax.all_to_all(block, plane, 0, 0, tiled=True)  7.45 us
    all_to_all x1, waiting for transfers between devices, body(): pieces = lax.all_to_all(partial_sums, plane, 0, 0, tiled=True)  6.91 us
    all_to_all x1, starting transfers between devices, body(): tall = lax.all_to_all(sent, 'row', 0, 0, tiled=True)  6.88 us
    all_to_all x1, starting transfers between devices, body(): gathered = lax.all_to_all(block, plane, 0, 0, tiled=True)  6.46 us
    all_to_all x1, waiting for transfers between devices, body(): tall = lax.all_to_all(sent, 'row', 0, 0, tiled=True)  6.03 us
    all_to_all x1, starting transfers between devices, body(): pieces = lax.all_to_all(partial_sums, plane, 0, 0, tiled=True)  3.55 us
  transfers between devices with their start and end apart: 5, of which 3 were waited for; matrix products, arithmetic and copies ran while one was open for 8% of the time, Pallas kernels for 1%

profile of v6, /device:TPU:1, one launch (start us, length us, event | category | flops | bytes accessed | tf_op | source)
XLA Modules:
  0.0 78.9 jit_solution(3281710836972410996)
XLA Ops:
  0.0 3.2 %collective-permute-start.1 = (bf16[8,320,320]{2,1,0:T(8,128)(2,1)}, bf16[8,320,320]{2,1,0:T(8,128)(2,1)S(1)}, u32[]{:S(2)}, u32[]{:S(2)}) collective-permute-start(bf16[8,320,320]{2,1,0:T(8,128)(2,1)} %param.5), channel_id=1, source_target_pairs={{0,16},{16,0},{32,48},{48,32},{64,80},{80,64},{96,112},{112,96},{1... | collective-permute-start | bytes 4915208 | tf_op jit(solution)/shard_map/ppermute | solution.py:259
  3.2 0.8 %reshape.46 = bf16[20,2,80]{2,1,0:T(2,128)(2,1)S(1)} reshape(bf16[20,4,40]{2,1,0:T(4,128)(2,1)} %param.4) | data formatting | bytes 12800 | tf_op jit(solution)/shard_map/reshape | solution.py:266
  4.0 0.7 broadcast_in_dim.12
  4.7 6.9 %all-to-all-start = ((bf16[16,20,80]{2,1,0:T(8,128)(2,1)}), bf16[16,20,80]{2,1,0:T(8,128)(2,1)S(1)}, u32[]{:S(2)}, u32[]{:S(2)}) async-start(bf16[16,20,80]{2,1,0:T(8,128)(2,1)} %bitcast.1), calls=%async_computation | async-start | bytes 196608 | tf_op jit(solution)/shard_map/all_to_all | solution.py:269
  11.6 0.7 dynamic_slice.12
  12.3 0.8 dynamic_slice.13
  13.0 0.1 broadcast_xor_fusion.1
  13.1 0.8 broadcast_in_dim.35.down_ref
  13.9 0.1 xor.46.partner_ref
  14.0 6.0 %all-to-all-done.tall_ref = bf16[16,20,80]{2,1,0:T(8,128)(2,1)S(1)} async-done(((bf16[16,20,80]{2,1,0:T(8,128)(2,1)}), bf16[16,20,80]{2,1,0:T(8,128)(2,1)S(1)}, u32[]{:S(2)}, u32[]{:S(2)}) %all-to-all-start) | async-done | bytes 51232 | tf_op jit(solution)/shard_map/all_to_all | solution.py:269
  20.0 0.9 %shard_map.46 = bf16[16,2,40,128]{3,2,1,0:T(8,128)(2,1)} custom-call(bf16[16,20,80]{2,1,0:T(8,128)(2,1)S(1)} %all-to-all-done.tall_ref, s32[320,1]{1,0:T(8,128)S(1)} %broadcast_in_dim.35.down_ref, s32[1,80]{1,0:T(1,128)S(1)} %xor.46.partner_ref), custom_call_target="tpu_custom_call" | custom-call | tf_op jit(solution)/shard_map/pallas_call | solution.py:38
  20.9 1.2 %collective-permute-start = (s32[4]{0:T(128)}, s32[4]{0:T(128)S(1)}, u32[]{:S(2)}, u32[]{:S(2)}) collective-permute-start(s32[4]{0:T(128)} %param.7), channel_id=1, source_target_pairs={{0,1},{1,0},{2,3},{3,2},{4,5},{5,4},{6,7},{7,6},{8,9},{9,8},{10,11... | collective-permute-start | bytes 56 | tf_op jit(solution)/shard_map/ppermute | solution.py:275
  22.1 6.5 %all-to-all-start.1 = ((bf16[16,2,40,128]{3,2,1,0:T(8,128)(2,1)}), bf16[16,2,40,128]{3,2,1,0:T(8,128)(2,1)S(1)}, u32[]{:S(2)}, u32[]{:S(2)}) async-start(bf16[16,2,40,128]{3,2,1,0:T(8,128)(2,1)} %shard_map.46), calls=%async_computation.1 | async-start | bytes 655360 | tf_op jit(solution)/shard_map/all_to_all | solution.py:273
  28.6 0.7 broadcast_in_dim.16.across_ref
  29.3 0.0 collective-permute-done
  29.3 0.7 fusion
  30.0 0.1 constant_dynamic-slice_fusion
  30.0 0.1 broadcast_in_dim.14
  30.1 7.4 %all-to-all-done.1.t_ref = bf16[16,2,40,128]{3,2,1,0:T(8,128)(2,1)S(1)} async-done(((bf16[16,2,40,128]{3,2,1,0:T(8,128)(2,1)}), bf16[16,2,40,128]{3,2,1,0:T(8,128)(2,1)S(1)}, u32[]{:S(2)}, u32[]{:S(2)}) %all-to-all-start.1) | async-done | bytes 327712 | tf_op jit(solution)/shard_map/all_to_all | solution.py:273
  37.6 0.0 collective-permute-done.1
  37.6 0.1 broadcast_in_dim.15.pair_ref
  37.6 0.0 copy-start
  37.6 14.5 %shard_map.47 = bf16[16,2,40,128]{3,2,1,0:T(8,128)(2,1)} custom-call(s32[4,128]{1,0:T(4,128)S(1)} %broadcast_in_dim.15.pair_ref, bf16[16,2,40,128]{3,2,1,0:T(8,128)(2,1)S(1)} %all-to-all-done.1.t_ref, bf16[2560,320]{1,0:T(8,128)(2,1)S(1)} %bitcast.8, bf16[2560,320]{1,0:T(8,128)(2,1)} %bitcast.9, s32[320,1]{1,0:T(8,128)S(1)} %broadcast_in_dim.35.down_ref, ...), custom_call_target="tpu_custom_call" | custom-call | tf_op jit(solution)/shard_map/pallas_call | solution.py:225
  52.1 3.6 %all-to-all-start.2 = ((bf16[16,2,40,128]{3,2,1,0:T(8,128)(2,1)}), bf16[16,2,40,128]{3,2,1,0:T(8,128)(2,1)S(1)}, u32[]{:S(2)}, u32[]{:S(2)}) async-start(bf16[16,2,40,128]{3,2,1,0:T(8,128)(2,1)} %shard_map.47), calls=%async_computation.2 | async-start | bytes 655360 | tf_op jit(solution)/shard_map/all_to_all | solution.py:286
  55.7 0.0 copy-done
  55.7 0.1 xor.47
  55.8 0.1 xor.50
  55.9 0.1 xor.48
  55.9 0.1 xor.49
  56.0 0.8 dynamic_slice.15
  56.8 6.9 %all-to-all-done.2.pieces_ref = bf16[16,2,40,128]{3,2,1,0:T(8,128)(2,1)S(1)} async-done(((bf16[16,2,40,128]{3,2,1,0:T(8,128)(2,1)}), bf16[16,2,40,128]{3,2,1,0:T(8,128)(2,1)S(1)}, u32[]{:S(2)}, u32[]{:S(2)}) %all-to-all-start.2) | async-done | bytes 327712 | tf_op jit(solution)/shard_map/all_to_all | solution.py:286
  63.7 0.3 shard_map.48
  64.0 0.1 broadcast_in_dim.34.down_ref
  64.0 14.0 %all_to_all.20.finals_ref = f32[16,16,128]{2,1,0:T(8,128)S(1)} all-to-all(f32[16,16,128]{2,1,0:T(8,128)S(1)} %shard_map.48), channel_id=1, replica_groups=mesh['row'=16,'col'=8,'pair'=2] {'row'}, dimensions={0} | all-to-all | bytes 262144 | tf_op jit(solution)/shard_map/all_to_all | solution.py:292
  78.0 0.9 %shard_map.49 = f32[20,4,40]{2,1,0:T(4,128)} custom-call(f32[16,16,128]{2,1,0:T(8,128)S(1)} %all_to_all.20.finals_ref, s32[20,128]{1,0:T(8,128)S(1)} %broadcast_in_dim.34.down_ref, s32[2,80]{1,0:T(2,128)S(1)} %broadcast_xor_fusion.across_ref), custom_call_target="tpu_custom_call" | custom-call | tf_op jit(solution)/shard_map/pallas_call | solution.py:106
  (4 shorter events, 0.0 us)
Async XLA Ops:
  0.0 37.6 %collective-permute-start.1 = (bf16[8,320,320]{2,1,0:T(8,128)(2,1)}, bf16[8,320,320]{2,1,0:T(8,128)(2,1)S(1)}, u32[]{:S(2)}, u32[]{:S(2)}) collective-permute-start(bf16[8,320,320]{2,1,0:T(8,128)(2,1)} %param.5), channel_id=1, source_target_pairs={{0,16},{16,0},{32,48},{48,32},{64,80},{80,64},{96,112},{112,96},{1... | collective-permute-start | bytes 4915208 | tf_op jit(solution)/shard_map/ppermute | solution.py:259
  4.7 15.3 %all-to-all-start = ((bf16[16,20,80]{2,1,0:T(8,128)(2,1)}), bf16[16,20,80]{2,1,0:T(8,128)(2,1)S(1)}, u32[]{:S(2)}, u32[]{:S(2)}) async-start(bf16[16,20,80]{2,1,0:T(8,128)(2,1)} %bitcast.1), calls=%async_computation | async-start | bytes 196608 | tf_op jit(solution)/shard_map/all_to_all | solution.py:269
  20.9 8.4 %collective-permute-start = (s32[4]{0:T(128)}, s32[4]{0:T(128)S(1)}, u32[]{:S(2)}, u32[]{:S(2)}) collective-permute-start(s32[4]{0:T(128)} %param.7), channel_id=1, source_target_pairs={{0,1},{1,0},{2,3},{3,2},{4,5},{5,4},{6,7},{7,6},{8,9},{9,8},{10,11... | collective-permute-start | bytes 56 | tf_op jit(solution)/shard_map/ppermute | solution.py:275
  22.1 15.4 %all-to-all-start.1 = ((bf16[16,2,40,128]{3,2,1,0:T(8,128)(2,1)}), bf16[16,2,40,128]{3,2,1,0:T(8,128)(2,1)S(1)}, u32[]{:S(2)}, u32[]{:S(2)}) async-start(bf16[16,2,40,128]{3,2,1,0:T(8,128)(2,1)} %shard_map.46), calls=%async_computation.1 | async-start | bytes 655360 | tf_op jit(solution)/shard_map/all_to_all | solution.py:273
  37.6 18.1 %copy-start = (s32[4]{0:T(128)S(1)}, s32[4]{0:T(128)}, u32[]{:S(2)}) copy-start(s32[4]{0:T(128)} %param.7) | copy-start | bytes 52
  52.1 11.6 %all-to-all-start.2 = ((bf16[16,2,40,128]{3,2,1,0:T(8,128)(2,1)}), bf16[16,2,40,128]{3,2,1,0:T(8,128)(2,1)S(1)}, u32[]{:S(2)}, u32[]{:S(2)}) async-start(bf16[16,2,40,128]{3,2,1,0:T(8,128)(2,1)} %shard_map.47), calls=%async_computation.2 | async-start | bytes 655360 | tf_op jit(solution)/shard_map/all_to_all | solution.py:286

commit v7 on v6

--- a/solution.py
+++ b/solution.py
@@ -12,39 +12,78 @@
 CORES = 2
 
 
-def fold_kernel(tall_ref, down_ref, partner_ref, out_ref):
+PACK = 16
+
+
+def spread_kernel(amp_ref, out_ref):
+    row_block, pairs_here, col_block = amp_ref.shape
+    held = pairs_here // CORES
+    lines = held * col_block
+    amp = amp_ref[...].astype(jnp.float32)
+    for c in range(CORES):
+        lane_side = jnp.concatenate([amp[:, c * held + j, :] for j in range(held)], axis=1)
+        column = lane_side.T
+        groups = [column[g * PACK : (g + 1) * PACK] for g in range(lines // PACK)]
+        rest = FOLD - row_block * len(groups)
+        groups.append(jnp.zeros((PACK, rest), jnp.float32))
+        packed = jnp.concatenate(groups, axis=1).astype(out_ref.dtype)
+        for m in range(c, out_ref.shape[0], CORES):
+            out_ref[m] = packed
+
+
+def fold_kernel(row_block, tall_ref, across_ref, partner_ref, out_ref):
     groups, held, col_block, _ = out_ref.shape
-    tall = jnp.concatenate(
-        [tall_ref[r].astype(jnp.float32) for r in range(tall_ref.shape[0])], axis=0
-    )
-    tall = jnp.where(down_ref[...] == partner_ref[...], tall, 0.0)
-    folded = tall[:FOLD]
-    for start in range(FOLD, tall.shape[0], FOLD):
-        piece = tall[start : start + FOLD]
-        short = FOLD - piece.shape[0]
-        if short:
-            piece = jnp.concatenate([piece, jnp.zeros((short, piece.shape[1]), jnp.float32)], axis=0)
-        folded = folded + piece
-    block = folded.T.astype(out_ref.dtype)
+    width = across_ref.shape[1]
+    lines = held * col_block
+    tiles = -(-width // FOLD)
+    filler = jnp.full((1, tiles * FOLD - width), -1, jnp.int32)
+    labels = jnp.concatenate([across_ref[...], filler], axis=1)
+    partner = jnp.broadcast_to(partner_ref[...], (8, lines)).T[:, :1]
+    lane = lax.broadcasted_iota(jnp.int32, (1, FOLD), 1)
+    folded = [jnp.zeros((PACK, FOLD), jnp.float32) for _ in range(lines // PACK)]
+    for r in range(tall_ref.shape[0]):
+        tile, low = r * row_block // FOLD, r * row_block % FOLD
+        here = jnp.where(
+            (lane >= low) & (lane < low + row_block), labels[:, tile * FOLD : (tile + 1) * FOLD], -1
+        )
+        over = low + row_block - FOLD
+        if over > 0:
+            following = labels[:, (tile + 1) * FOLD : (tile + 2) * FOLD]
+            here = jnp.where(lane < over, following, here)
+        piece = tall_ref[r].astype(jnp.float32)
+        for g in range(lines // PACK):
+            shift = (r - g) * row_block % FOLD
+            moved = pltpu.roll(piece, shift, 1) if shift else piece
+            fits = partner[g * PACK : (g + 1) * PACK] == here
+            folded[g] = folded[g] + jnp.where(fits, moved, 0.0)
+    block = jnp.concatenate(folded, axis=0)
     for j in range(held):
-        part = block[j * col_block : (j + 1) * col_block]
+        part = block[j * col_block : (j + 1) * col_block].astype(out_ref.dtype)
         for m in range(groups):
             out_ref[m, j] = part
 
 
-def fold_call(tall, down, partner, shape):
+def spread_call(amplitudes, rows):
+    vmem = pl.BlockSpec(memory_space=pltpu.VMEM)
+    return pl.pallas_call(
+        spread_kernel,
+        out_shape=jax.ShapeDtypeStruct((rows, PACK, FOLD), amplitudes.dtype),
+        in_specs=[vmem],
+        out_specs=vmem,
+        compiler_params=pltpu.CompilerParams(vmem_limit_bytes=8 * 2**20),
+    )(amplitudes)
+
+
+def fold_call(tall, across, partner, row_block, shape):
     vmem = pl.BlockSpec(memory_space=pltpu.VMEM)
     close = functools.partial(pltpu.with_memory_space_constraint, memory_space=pltpu.VMEM)
     return pl.pallas_call(
-        fold_kernel,
-        out_shape=pltpu.VMEM(shape, tall.dtype),
+        functools.partial(fold_kernel, row_block),
+        out_shape=jax.ShapeDtypeStruct(shape, tall.dtype),
         in_specs=[vmem] * 3,
         out_specs=vmem,
         compiler_params=pltpu.CompilerParams(vmem_limit_bytes=8 * 2**20),
-    )(close(tall), close(down), close(partner))
-
-
-PACK = 16
+    )(close(tall), close(across), close(partner))
 
 
 def pack_kernel(row_block, pieces_ref, out_ref):
@@ -120,7 +159,6 @@
     t_ref,
     near_ref,
     far_ref,
-    down_ref,
     across_ref,
     out_ref,
     inner,
@@ -130,7 +168,7 @@
     stack,
     arrived,
 ):
-    width = down_ref.shape[0]
+    width = across_ref.shape[1]
     half_depth = near_ref.shape[0]
     groups, pairs_here = t_ref.shape[0] // cols, t_ref.shape[1]
     pairs = groups * pairs_here
@@ -142,9 +180,8 @@
     fetch = pltpu.make_async_copy(far_ref, stack, arrived)
     fetch.start()
     filler = jnp.full((1, tiles * FOLD - width), -1, jnp.int32)
-    mixed = jnp.bitwise_xor(
-        down_ref[...], jnp.concatenate([across_ref[...], filler], axis=1)
-    )
+    down = jnp.broadcast_to(across_ref[...], (8, width)).T[:, :1]
+    mixed = jnp.bitwise_xor(down, jnp.concatenate([across_ref[...], filler], axis=1))
     for p in range(pairs):
         half, at = p // pairs_here, p % pairs_here
         rows = jnp.concatenate(
@@ -214,7 +251,7 @@
             )
 
 
-def ladder_call(gathered, near, far, down, across, pair_labels, cols):
+def ladder_call(gathered, near, far, across, pair_labels, cols):
     count, width, _ = near.shape
     pairs = pair_labels.shape[0]
     group = 4
@@ -225,7 +262,7 @@
     return pl.pallas_call(
         functools.partial(ladder_kernel, cols, group, 2 * FOLD),
         out_shape=pltpu.VMEM(gathered.shape, jnp.bfloat16),
-        in_specs=[vmem, vmem, vmem, anywhere, vmem, vmem],
+        in_specs=[vmem, vmem, vmem, anywhere, vmem],
         out_specs=vmem,
         scratch_shapes=[
             pltpu.VMEM((depth, lanes), jnp.bfloat16),
@@ -241,7 +278,6 @@
         close(gathered),
         close(near.reshape(count * width, width)),
         pltpu.with_memory_space_constraint(far.reshape(count * width, width), pltpu.HBM),
-        close(down),
         close(across),
     )
 
@@ -261,14 +297,12 @@
     col_labels = lax.dynamic_slice_in_dim(vir_irrep, lax.axis_index("col") * col_block, col_block)
     pairs_held = lax.dynamic_slice_in_dim(pair_irrep, core * held, held)
     partner = jnp.bitwise_xor(pairs_held[:, None], col_labels[None, :]).reshape(1, inner)
-    down = vir_irrep[:, None]
-
-    halves = amplitudes.reshape(row_block, CORES, inner).transpose(1, 0, 2)
-    sent = jnp.broadcast_to(halves[None], (rows // CORES, CORES, row_block, inner))
-    sent = sent.reshape(rows, row_block, inner)
+    across = vir_irrep[None, :]
+
+    sent = spread_call(amplitudes, rows)
     tall = lax.all_to_all(sent, "row", 0, 0, tiled=True)
     groups = cols * lax.axis_size("pair")
-    block = fold_call(tall, down, partner, (groups, held, col_block, FOLD))
+    block = fold_call(tall, across, partner, row_block, (groups, held, col_block, FOLD))
     block, late_vir, late_pair = lax.optimization_barrier((block, vir_irrep, pair_irrep))
     gathered = lax.all_to_all(block, plane, 0, 0, tiled=True)
 
@@ -278,10 +312,9 @@
         [jnp.where(first, late_pair, other_pairs), jnp.where(first, other_pairs, late_pair)]
     )
     pair_labels = lax.dynamic_slice_in_dim(pair_labels, core * held, held, axis=1).reshape(-1)
-    across = late_vir[None, :]
     row_labels = lax.dynamic_slice_in_dim(late_vir, lax.axis_index("row") * row_block, row_block)
 
-    partial_sums = ladder_call(gathered, other_factors, factors, down, across, pair_labels, cols)
+    partial_sums = ladder_call(gathered, other_factors, factors, across, pair_labels, cols)
 
     pieces = lax.all_to_all(partial_sums, plane, 0, 0, tiled=True)
     packed = pack_call(pieces, rows, row_block)

time: 79.4 us -> 79.1 us (level)
  local copies, waits for them, and re-layouts: 5.88 us -> 4.35 us
  Pallas kernels: 16.5 us -> 17.6 us
    broadcast_in_dim x3 -> x1, local copies, waits for them, and re-layouts: 2.11 us -> 0.68 us  [body(): across = vir_irrep[None, :]]
    pallas_call x1 -> x2, Pallas kernels: 0.9 us -> 1.86 us  [the longest x1 0.99 us: fold_call(): pl.pallas_call(functools.partial(fold_kernel, row_block), out_shape=jax.S...]
    reshape x1 -> x0, local copies, waits for them, and re-layouts: 0.81 us -> none  [body(): halves = amplitudes.reshape(row_block, CORES, inner).transpose(1, 0, 2)]
  transfers between devices with their start and end apart: 5 -> 5, of which waited for: 3 -> 3; matrix products, arithmetic and copies ran while one was open for 8% -> 5% of each run, Pallas kernels for 1% -> 2%
where the time goes in v7:
time: 79.1 us; the launch traced here: 78.5 us
  starting transfers between devices  21.3 us (27%)
  waiting for transfers between devices  20.3 us (26%)
  Pallas kernels  17.6 us (22%)
  blocking collectives  14.1 us (18%)
  local copies, waits for them, and re-layouts  4.35 us (5%)
    pallas_call x1, Pallas kernels, ladder_call(): pl.pallas_call(functools.partial(ladder_kernel, cols, group, 2 * FOLD), o...  14.6 us
    all_to_all x1, blocking collectives, body(): finals = lax.all_to_all(packed, 'row', 0, 0, tiled=True)  14.1 us
    all_to_all x1, waiting for transfers between devices, body(): gathered = lax.all_to_all(block, plane, 0, 0, tiled=True)  7.96 us
    all_to_all x1, starting transfers between devices, body(): tall = lax.all_to_all(sent, 'row', 0, 0, tiled=True)  6.88 us
    all_to_all x1, waiting for transfers between devices, body(): pieces = lax.all_to_all(partial_sums, plane, 0, 0, tiled=True)  6.88 us
    all_to_all x1, starting transfers between devices, body(): gathered = lax.all_to_all(block, plane, 0, 0, tiled=True)  6.46 us
    all_to_all x1, waiting for transfers between devices, body(): tall = lax.all_to_all(sent, 'row', 0, 0, tiled=True)  5.45 us
    all_to_all x1, starting transfers between devices, body(): pieces = lax.all_to_all(partial_sums, plane, 0, 0, tiled=True)  3.55 us
  transfers between devices with their start and end apart: 5, of which 3 were waited for; matrix products, arithmetic and copies ran while one was open for 5% of the time, Pallas kernels for 2%

profile of v7, /device:TPU:1, one launch (start us, length us, event | category | flops | bytes accessed | tf_op | source)
XLA Modules:
  0.0 78.5 jit_solution(15990444625856763783)
XLA Ops:
  0.0 3.2 %collective-permute-start.1 = (bf16[8,320,320]{2,1,0:T(8,128)(2,1)}, bf16[8,320,320]{2,1,0:T(8,128)(2,1)S(1)}, u32[]{:S(2)}, u32[]{:S(2)}) collective-permute-start(bf16[8,320,320]{2,1,0:T(8,128)(2,1)} %param.5), channel_id=1, source_target_pairs={{0,16},{16,0},{32,48},{48,32},{64,80},{80,64},{96,112},{112,96},{1... | collective-permute-start | bytes 4915208 | tf_op jit(solution)/shard_map/ppermute | solution.py:295
  3.2 0.0 copy-start
  3.2 0.7 copy-done
  3.9 0.9 %shard_map.46 = bf16[16,16,128]{2,1,0:T(8,128)(2,1)} custom-call(bf16[20,4,40]{2,1,0:T(4,128)(2,1)S(1)} %copy-done), custom_call_target="tpu_custom_call" | custom-call | tf_op jit(solution)/shard_map/pallas_call | solution.py:68
  4.8 6.9 %all-to-all-start = ((bf16[16,16,128]{2,1,0:T(8,128)(2,1)}), bf16[16,16,128]{2,1,0:T(8,128)(2,1)S(1)}, u32[]{:S(2)}, u32[]{:S(2)}) async-start(bf16[16,16,128]{2,1,0:T(8,128)(2,1)} %shard_map.46), calls=%async_computation | async-start | bytes 131072 | tf_op jit(solution)/shard_map/all_to_all | solution.py:303
  11.7 0.7 broadcast_in_dim.8.across_ref
  12.4 0.8 dynamic_slice.13
  13.1 0.7 dynamic_slice.12
  13.9 0.1 broadcast_xor_fusion.1
  13.9 0.1 xor.46.partner_ref
  14.0 5.4 %all-to-all-done.tall_ref = bf16[16,16,128]{2,1,0:T(8,128)(2,1)S(1)} async-done(((bf16[16,16,128]{2,1,0:T(8,128)(2,1)}), bf16[16,16,128]{2,1,0:T(8,128)(2,1)S(1)}, u32[]{:S(2)}, u32[]{:S(2)}) %all-to-all-start) | async-done | bytes 65568 | tf_op jit(solution)/shard_map/all_to_all | solution.py:303
  19.5 1.0 %shard_map.47 = bf16[16,2,40,128]{3,2,1,0:T(8,128)(2,1)} custom-call(bf16[16,16,128]{2,1,0:T(8,128)(2,1)S(1)} %all-to-all-done.tall_ref, s32[1,320]{1,0:T(1,128)S(1)} %broadcast_in_dim.8.across_ref, s32[1,80]{1,0:T(1,128)S(1)} %xor.46.partner_ref), custom_call_target="tpu_custom_call" | custom-call | tf_op jit(solution)/shard_map/pallas_call | solution.py:80
  20.5 1.2 %collective-permute-start = (s32[4]{0:T(128)}, s32[4]{0:T(128)S(1)}, u32[]{:S(2)}, u32[]{:S(2)}) collective-permute-start(s32[4]{0:T(128)} %param.7), channel_id=1, source_target_pairs={{0,1},{1,0},{2,3},{3,2},{4,5},{5,4},{6,7},{7,6},{8,9},{9,8},{10,11... | collective-permute-start | bytes 56 | tf_op jit(solution)/shard_map/ppermute | solution.py:309
  21.7 6.5 %all-to-all-start.1 = ((bf16[16,2,40,128]{3,2,1,0:T(8,128)(2,1)}), bf16[16,2,40,128]{3,2,1,0:T(8,128)(2,1)S(1)}, u32[]{:S(2)}, u32[]{:S(2)}) async-start(bf16[16,2,40,128]{3,2,1,0:T(8,128)(2,1)} %shard_map.47), calls=%async_computation.1 | async-start | bytes 655360 | tf_op jit(solution)/shard_map/all_to_all | solution.py:307
  28.1 0.0 collective-permute-done
  28.1 0.7 fusion
  28.8 0.1 constant_dynamic-slice_fusion
  28.9 0.1 broadcast_in_dim.9
  29.0 8.0 %all-to-all-done.1.t_ref = bf16[16,2,40,128]{3,2,1,0:T(8,128)(2,1)S(1)} async-done(((bf16[16,2,40,128]{3,2,1,0:T(8,128)(2,1)}), bf16[16,2,40,128]{3,2,1,0:T(8,128)(2,1)S(1)}, u32[]{:S(2)}, u32[]{:S(2)}) %all-to-all-start.1) | async-done | bytes 327712 | tf_op jit(solution)/shard_map/all_to_all | solution.py:307
  36.9 0.0 collective-permute-done.1
  36.9 0.1 broadcast_in_dim.10.pair_ref
  37.0 0.0 copy-start.1
  37.0 14.6 %shard_map.48 = bf16[16,2,40,128]{3,2,1,0:T(8,128)(2,1)} custom-call(s32[4,128]{1,0:T(4,128)S(1)} %broadcast_in_dim.10.pair_ref, bf16[16,2,40,128]{3,2,1,0:T(8,128)(2,1)S(1)} %all-to-all-done.1.t_ref, bf16[2560,320]{1,0:T(8,128)(2,1)S(1)} %bitcast.6, bf16[2560,320]{1,0:T(8,128)(2,1)} %bitcast.7, s32[1,320]{1,0:T(1,128)S(1)} %broadcast_in_dim.8.across_ref), custom_call_target="tpu_custom_call" | custom-call | tf_op jit(solution)/shard_map/pallas_call | solution.py:262
  51.6 3.6 %all-to-all-start.2 = ((bf16[16,2,40,128]{3,2,1,0:T(8,128)(2,1)}), bf16[16,2,40,128]{3,2,1,0:T(8,128)(2,1)S(1)}, u32[]{:S(2)}, u32[]{:S(2)}) async-start(bf16[16,2,40,128]{3,2,1,0:T(8,128)(2,1)} %shard_map.48), calls=%async_computation.2 | async-start | bytes 655360 | tf_op jit(solution)/shard_map/all_to_all | solution.py:319
  55.2 0.0 copy-done.1
  55.2 0.1 xor.47
  55.3 0.1 xor.50
  55.4 0.1 xor.48
  55.5 0.1 xor.49
  55.5 0.8 dynamic_slice.15
  56.3 6.9 %all-to-all-done.2.pieces_ref = bf16[16,2,40,128]{3,2,1,0:T(8,128)(2,1)S(1)} async-done(((bf16[16,2,40,128]{3,2,1,0:T(8,128)(2,1)}), bf16[16,2,40,128]{3,2,1,0:T(8,128)(2,1)S(1)}, u32[]{:S(2)}, u32[]{:S(2)}) %all-to-all-start.2) | async-done | bytes 327712 | tf_op jit(solution)/shard_map/all_to_all | solution.py:319
  63.2 0.3 shard_map.49
  63.4 0.1 broadcast_in_dim.11.down_ref
  63.5 14.1 %all_to_all.20.finals_ref = f32[16,16,128]{2,1,0:T(8,128)S(1)} all-to-all(f32[16,16,128]{2,1,0:T(8,128)S(1)} %shard_map.49), channel_id=1, replica_groups=mesh['row'=16,'col'=8,'pair'=2] {'row'}, dimensions={0} | all-to-all | bytes 262144 | tf_op jit(solution)/shard_map/all_to_all | solution.py:325
  77.7 0.9 %shard_map.50 = f32[20,4,40]{2,1,0:T(4,128)} custom-call(f32[16,16,128]{2,1,0:T(8,128)S(1)} %all_to_all.20.finals_ref, s32[20,128]{1,0:T(8,128)S(1)} %broadcast_in_dim.11.down_ref, s32[2,80]{1,0:T(2,128)S(1)} %broadcast_xor_fusion.across_ref), custom_call_target="tpu_custom_call" | custom-call | tf_op jit(solution)/shard_map/pallas_call | solution.py:145
  (3 shorter events, 0.0 us)
Async XLA Ops:
  0.0 36.9 %collective-permute-start.1 = (bf16[8,320,320]{2,1,0:T(8,128)(2,1)}, bf16[8,320,320]{2,1,0:T(8,128)(2,1)S(1)}, u32[]{:S(2)}, u32[]{:S(2)}) collective-permute-start(bf16[8,320,320]{2,1,0:T(8,128)(2,1)} %param.5), channel_id=1, source_target_pairs={{0,16},{16,0},{32,48},{48,32},{64,80},{80,64},{96,112},{112,96},{1... | collective-permute-start | bytes 4915208 | tf_op jit(solution)/shard_map/ppermute | solution.py:295
  3.2 0.7 copy-start
  4.8 14.7 %all-to-all-start = ((bf16[16,16,128]{2,1,0:T(8,128)(2,1)}), bf16[16,16,128]{2,1,0:T(8,128)(2,1)S(1)}, u32[]{:S(2)}, u32[]{:S(2)}) async-start(bf16[16,16,128]{2,1,0:T(8,128)(2,1)} %shard_map.46), calls=%async_computation | async-start | bytes 131072 | tf_op jit(solution)/shard_map/all_to_all | solution.py:303
  20.5 7.7 %collective-permute-start = (s32[4]{0:T(128)}, s32[4]{0:T(128)S(1)}, u32[]{:S(2)}, u32[]{:S(2)}) collective-permute-start(s32[4]{0:T(128)} %param.7), channel_id=1, source_target_pairs={{0,1},{1,0},{2,3},{3,2},{4,5},{5,4},{6,7},{7,6},{8,9},{9,8},{10,11... | collective-permute-start | bytes 56 | tf_op jit(solution)/shard_map/ppermute | solution.py:309
  21.7 15.3 %all-to-all-start.1 = ((bf16[16,2,40,128]{3,2,1,0:T(8,128)(2,1)}), bf16[16,2,40,128]{3,2,1,0:T(8,128)(2,1)S(1)}, u32[]{:S(2)}, u32[]{:S(2)}) async-start(bf16[16,2,40,128]{3,2,1,0:T(8,128)(2,1)} %shard_map.47), calls=%async_computation.1 | async-start | bytes 655360 | tf_op jit(solution)/shard_map/all_to_all | solution.py:307
  37.0 18.2 %copy-start.1 = (s32[4]{0:T(128)S(1)}, s32[4]{0:T(128)}, u32[]{:S(2)}) copy-start(s32[4]{0:T(128)} %param.7) | copy-start | bytes 52
  51.6 11.5 %all-to-all-start.2 = ((bf16[16,2,40,128]{3,2,1,0:T(8,128)(2,1)}), bf16[16,2,40,128]{3,2,1,0:T(8,128)(2,1)S(1)}, u32[]{:S(2)}, u32[]{:S(2)}) async-start(bf16[16,2,40,128]{3,2,1,0:T(8,128)(2,1)} %shard_map.48), calls=%async_computation.2 | async-start | bytes 655360 | tf_op jit(solution)/shard_map/all_to_all | solution.py:319

commit v8 on v7

v8 whole, which is shorter than its diff:
```python
import functools

import jax
import jax.numpy as jnp
from jax import lax
from jax.experimental import pallas as pl
from jax.experimental.pallas import tpu as pltpu
from jax.sharding import PartitionSpec as P


LANES = 128
FOLD = 80
LEFT = LANES - FOLD
REST = FOLD - LEFT
SUB = 8
CORES = 2


def lanes():
    return lax.broadcasted_iota(jnp.int32, (1, LANES), 1)


def turn(x, shift):
    shift = shift % LANES
    return pltpu.roll(x, shift, 1) if shift else x


def join(first, second):
    lane = lanes()
    block = second.shape[0]
    main = jnp.where(lane < FOLD, first, turn(second, FOLD))
    rows, per_row = [], LANES // REST
    for start in range(0, block // SUB, per_row):
        row = jnp.zeros((SUB, LANES), jnp.float32)
        for k in range(min(per_row, block // SUB - start)):
            at = (start + k) * SUB
            moved = turn(second[at : at + SUB], k * REST - LEFT)
            row = jnp.where((lane >= k * REST) & (lane < (k + 1) * REST), moved, row)
        rows.append(row)
    return jnp.concatenate([main] + rows, axis=0)


def joined_rows(block):
    return block + -(-(block // SUB) // (LANES // REST)) * SUB


def part(x, block):
    lane = lanes()
    per_row = LANES // REST
    first = x[:block]
    tail = [
        turn(
            x[block + g // per_row * SUB : block + (g // per_row + 1) * SUB],
            LEFT - g % per_row * REST,
        )
        for g in range(block // SUB)
    ]
    second = jnp.where(lane < LEFT, turn(first, -FOLD), jnp.concatenate(tail, axis=0))
    return first, second


def unfold(x, tiles):
    lane = lanes()
    out = []
    for t in range(tiles):
        base = t * LANES
        tile = None
        for m in range(base // FOLD, -(-(base + LANES) // FOLD)):
            moved = turn(x, m * FOLD - base)
            tile = moved if tile is None else jnp.where(lane >= m * FOLD - base, moved, tile)
        out.append(tile)
    return out


def fold(pieces):
    lane = lanes()
    total, by_shift = None, {}
    for t, piece in enumerate(pieces):
        base = t * LANES
        for m in range(base // FOLD, -(-(base + LANES) // FOLD)):
            low, high = max(m * FOLD - base, 0), min((m + 1) * FOLD - base, LANES)
            inside = jnp.where((lane >= low) & (lane < high), piece, 0.0)
            shift = (base - m * FOLD) % LANES
            by_shift[shift] = inside if shift not in by_shift else by_shift[shift] + inside
    for shift, piece in by_shift.items():
        moved = turn(piece, shift)
        total = moved if total is None else total + moved
    return total


PACK = 16


def spread_kernel(amp_ref, out_ref):
    row_block, pairs_here, col_block = amp_ref.shape
    held = pairs_here // CORES
    lines = held * col_block
    amp = amp_ref[...].astype(jnp.float32)
    for c in range(CORES):
        lane_side = jnp.concatenate([amp[:, c * held + j, :] for j in range(held)], axis=1)
        column = lane_side.T
        groups = [column[g * PACK : (g + 1) * PACK] for g in range(lines // PACK)]
        rest = LANES - row_block * len(groups)
        groups.append(jnp.zeros((PACK, rest), jnp.float32))
        packed = jnp.concatenate(groups, axis=1).astype(out_ref.dtype)
        for m in range(c, out_ref.shape[0], CORES):
            out_ref[m] = packed


def fold_kernel(row_block, col_block, tall_ref, across_ref, partner_ref, out_ref):
    width = across_ref.shape[1]
    lines = partner_ref.shape[1]
    partner = jnp.broadcast_to(partner_ref[...], (SUB, lines)).T[:, :1]
    lane = lanes()
    filler = jnp.full((1, LANES - FOLD), -1, jnp.int32)
    folded = [jnp.zeros((PACK, LANES), jnp.float32) for _ in range(lines // PACK)]
    for m in range(width // FOLD):
        labels = jnp.concatenate([across_ref[:, m * FOLD : (m + 1) * FOLD], filler], axis=1)
        for k in range(FOLD // row_block):
            low = k * row_block
            here = jnp.where((lane >= low) & (lane < low + row_block), labels, -1)
            piece = tall_ref[m * (FOLD // row_block) + k].astype(jnp.float32)
            for g in range(lines // PACK):
                fits = partner[g * PACK : (g + 1) * PACK] == here
                folded[g] = folded[g] + jnp.where(fits, turn(piece, (k - g) * row_block), 0.0)
    block = jnp.concatenate(folded, axis=0)
    block = join(block[:col_block], block[col_block:]).astype(out_ref.dtype)
    for m in range(out_ref.shape[0]):
        out_ref[m] = block


def spread_call(amplitudes, rows):
    vmem = pl.BlockSpec(memory_space=pltpu.VMEM)
    return pl.pallas_call(
        spread_kernel,
        out_shape=jax.ShapeDtypeStruct((rows, PACK, LANES), amplitudes.dtype),
        in_specs=[vmem],
        out_specs=vmem,
        compiler_params=pltpu.CompilerParams(vmem_limit_bytes=8 * 2**20),
    )(amplitudes)


def fold_call(tall, across, partner, row_block, col_block, groups):
    vmem = pl.BlockSpec(memory_space=pltpu.VMEM)
    close = functools.partial(pltpu.with_memory_space_constraint, memory_space=pltpu.VMEM)
    return pl.pallas_call(
        functools.partial(fold_kernel, row_block, col_block),
        out_shape=jax.ShapeDtypeStruct((groups, joined_rows(col_block), LANES), tall.dtype),
        in_specs=[vmem] * 3,
        out_specs=vmem,
        compiler_params=pltpu.CompilerParams(vmem_limit_bytes=8 * 2**20),
    )(close(tall), close(across), close(partner))


def pack_kernel(row_block, col_block, pieces_ref, out_ref):
    total = pieces_ref[0].astype(jnp.float32)
    for m in range(1, pieces_ref.shape[0]):
        total = total + pieces_ref[m].astype(jnp.float32)
    total = jnp.concatenate(part(total, col_block), axis=0)
    lane = lanes()
    period = FOLD // row_block
    for k in range(period):
        packed = jnp.zeros((PACK, LANES), jnp.float32)
        for g in range(total.shape[0] // PACK):
            moved = turn(total[g * PACK : (g + 1) * PACK], (g - k) * row_block)
            packed = jnp.where(
                (lane >= g * row_block) & (lane < (g + 1) * row_block), moved, packed
            )
        for r in range(k, out_ref.shape[0], period):
            out_ref[r] = packed


def unpack_kernel(finals_ref, down_ref, across_ref, out_ref):
    row_block, pairs_here, col_block = out_ref.shape
    held = pairs_here // CORES
    lines = held * col_block
    for c in range(CORES):
        total = finals_ref[c]
        for z in range(CORES + c, finals_ref.shape[0], CORES):
            total = total + finals_ref[z]
        spread = jnp.concatenate(
            [
                turn(total, -g * row_block)
                for g in range(lines // PACK)
            ],
            axis=0,
        )
        spread = jnp.where(
            down_ref[:, :1] == across_ref[c : c + 1, :lines], spread.T[:row_block], 0.0
        )
        for j in range(held):
            out_ref[:, c * held + j, :] = spread[:, j * col_block : (j + 1) * col_block]


def pack_call(pieces, rows, row_block, col_block):
    close = functools.partial(pltpu.with_memory_space_constraint, memory_space=pltpu.VMEM)
    vmem = pl.BlockSpec(memory_space=pltpu.VMEM)
    return pl.pallas_call(
        functools.partial(pack_kernel, row_block, col_block),
        out_shape=jax.ShapeDtypeStruct((rows, PACK, LANES), jnp.float32),
        in_specs=[vmem],
        out_specs=vmem,
        compiler_params=pltpu.CompilerParams(vmem_limit_bytes=8 * 2**20),
    )(close(pieces))


def unpack_call(finals, down, across, shape):
    close = functools.partial(pltpu.with_memory_space_constraint, memory_space=pltpu.VMEM)
    vmem = pl.BlockSpec(memory_space=pltpu.VMEM)
    return pl.pallas_call(
        unpack_kernel,
        out_shape=jax.ShapeDtypeStruct(shape, jnp.float32),
        in_specs=[vmem] * 3,
        out_specs=vmem,
        compiler_params=pltpu.CompilerParams(vmem_limit_bytes=8 * 2**20),
    )(close(finals), close(down), close(across))


def ladder_kernel(
    cols,
    group,
    lane_group,
    pair_ref,
    t_ref,
    near_ref,
    far_ref,
    across_ref,
    out_ref,
    inner,
    amp,
    ladders,
    side,
    stack,
    arrived,
):
    width = across_ref.shape[1]
    half_depth = near_ref.shape[0]
    groups, pairs = t_ref.shape[0] // cols, pair_ref.shape[0]
    tiles = -(-width // LANES)
    block = width // cols
    step = group * width
    half_steps = half_depth // step

    fetch = pltpu.make_async_copy(far_ref, stack, arrived)
    fetch.start()
    filler = jnp.full((1, tiles * LANES - width), -1, jnp.int32)
    down = jnp.broadcast_to(across_ref[...], (8, width)).T[:, :1]
    mixed = jnp.bitwise_xor(down, jnp.concatenate([across_ref[...], filler], axis=1))
    for half in range(groups):
        both = [part(t_ref[q * groups + half].astype(jnp.float32), block) for q in range(cols)]
        for at in range(CORES):
            p = half * CORES + at
            rows = jnp.concatenate([pieces[at] for pieces in both], axis=0)
            spread = jnp.concatenate(unfold(rows, tiles), axis=1)
            spread = jnp.where(mixed == pair_ref[p : p + 1, :1], spread, 0.0)
            amp[p * width : (p + 1) * width, :] = spread.astype(jnp.bfloat16)[:, :width]

    for source, base in ((near_ref, 0), (stack, half_steps)):
        if base:
            fetch.wait()

        @pl.loop(0, half_steps)
        def _(g, source=source, base=base):
            here = pl.multiple_of(g * step, step)
            there = pl.multiple_of((base + g) * step, step)
            for k in range(group):
                side[base + g, :, k * width : (k + 1) * width] = source[
                    pl.ds(pl.multiple_of(here + k * width, width), width), :
                ]
            part = lax.dot_general(
                amp[...],
                source[pl.ds(here, step), :],
                (((1,), (1,)), ((), ())),
                preferred_element_type=jnp.float32,
            ).astype(jnp.bfloat16)
            for p in range(pairs):
                for k in range(group):
                    inner[
                        pl.ds(pl.multiple_of(there + k * width, width), width),
                        p * width : (p + 1) * width,
                    ] = part[p * width : (p + 1) * width, k * width : (k + 1) * width]

    for start in range(0, pairs * width, lane_group):
        lanes = slice(start, start + lane_group)
        total = None
        for g in range(2 * half_steps):
            term = jnp.dot(
                side[g], inner[g * step : (g + 1) * step, lanes], preferred_element_type=jnp.float32
            )
            total = term if total is None else total + term
        ladders[:, lanes] = total

    blank = jnp.zeros((width, tiles * LANES - width), jnp.float32)
    for half in range(groups):
        both = []
        for at in range(CORES):
            p = half * CORES + at
            ladder = jnp.concatenate([ladders[:, p * width : (p + 1) * width], blank], axis=1)
            ladder = jnp.where(mixed == pair_ref[p : p + 1, :1], ladder, 0.0)
            tall = ladder[:FOLD]
            for start in range(FOLD, width, FOLD):
                tall = tall + ladder[start : start + FOLD]
            tall = jnp.concatenate(
                [tall, jnp.zeros((LANES - FOLD, tiles * LANES), jnp.float32)], axis=0
            )
            flat = fold([ladder[:, t * LANES : (t + 1) * LANES] for t in range(tiles)])
            both.append(flat + tall.T[:width])
        for q in range(cols):
            span = slice(q * block, (q + 1) * block)
            out_ref[q * groups + half] = join(both[0][span], both[1][span]).astype(out_ref.dtype)


def ladder_call(gathered, near, far, across, pair_labels, cols):
    count, width, _ = near.shape
    pairs = pair_labels.shape[0]
    group = 4
    depth, lanes = 2 * count * width, pairs * width
    vmem = pl.BlockSpec(memory_space=pltpu.VMEM)
    anywhere = pl.BlockSpec(memory_space=pl.ANY)
    close = functools.partial(pltpu.with_memory_space_constraint, memory_space=pltpu.VMEM)
    return pl.pallas_call(
        functools.partial(ladder_kernel, cols, group, 2 * LANES),
        out_shape=pltpu.VMEM(gathered.shape, jnp.bfloat16),
        in_specs=[vmem, vmem, vmem, anywhere, vmem],
        out_specs=vmem,
        scratch_shapes=[
            pltpu.VMEM((depth, lanes), jnp.bfloat16),
            pltpu.VMEM((lanes, width), jnp.bfloat16),
            pltpu.VMEM((width, lanes), jnp.float32),
            pltpu.VMEM((2 * count // group, width, group * width), jnp.bfloat16),
            pltpu.VMEM((count * width, width), jnp.bfloat16),
            pltpu.SemaphoreType.DMA(()),
        ],
        compiler_params=pltpu.CompilerParams(vmem_limit_bytes=40 * 2**20),
    )(
        close(jnp.broadcast_to(pair_labels[:, None], (pairs, LANES))),
        close(gathered),
        close(near.reshape(count * width, width)),
        pltpu.with_memory_space_constraint(far.reshape(count * width, width), pltpu.HBM),
        close(across),
    )


def body(amplitudes, factors, vir_irrep, pair_irrep):
    row_block, pairs_here, col_block = amplitudes.shape
    width = vir_irrep.shape[0]
    rows, cols = width // row_block, width // col_block
    held = pairs_here // CORES
    inner = held * col_block
    plane = ("col", "pair")
    core = lax.axis_index("row") % CORES
    swap = [(k, k ^ 1) for k in range(rows)]

    other_factors = lax.ppermute(factors, "row", swap)

    col_labels = lax.dynamic_slice_in_dim(vir_irrep, lax.axis_index("col") * col_block, col_block)
    pairs_held = lax.dynamic_slice_in_dim(pair_irrep, core * held, held)
    partner = jnp.bitwise_xor(pairs_held[:, None], col_labels[None, :]).reshape(1, inner)
    across = vir_irrep[None, :]

    sent = spread_call(amplitudes, rows)
    tall = lax.all_to_all(sent, "row", 0, 0, tiled=True)
    groups = cols * lax.axis_size("pair")
    block = fold_call(tall, across, partner, row_block, col_block, groups)
    block, late_vir, late_pair = lax.optimization_barrier((block, vir_irrep, pair_irrep))
    gathered = lax.all_to_all(block, plane, 0, 0, tiled=True)

    other_pairs = lax.ppermute(late_pair, "pair", [(0, 1), (1, 0)])
    first = lax.axis_index("pair") == 0
    pair_labels = jnp.stack(
        [jnp.where(first, late_pair, other_pairs), jnp.where(first, other_pairs, late_pair)]
    )
    pair_labels = lax.dynamic_slice_in_dim(pair_labels, core * held, held, axis=1).reshape(-1)
    row_labels = lax.dynamic_slice_in_dim(late_vir, lax.axis_index("row") * row_block, row_block)

    partial_sums = ladder_call(gathered, other_factors, factors, across, pair_labels, cols)

    pieces = lax.all_to_all(partial_sums, plane, 0, 0, tiled=True)
    packed = pack_call(pieces, rows, row_block, col_block)
    need = jnp.bitwise_xor(pair_irrep[:, None], col_labels[None, :]).reshape(CORES, inner)
    packed, row_labels, need = lax.optimization_barrier(
        (packed, jnp.broadcast_to(row_labels[:, None], (row_block, LANES)), need)
    )
    finals = lax.all_to_all(packed, "row", 0, 0, tiled=True)
    return unpack_call(finals, row_labels, need, amplitudes.shape)


def solution(mesh):
    placed = (P("row", "pair", "col"), P(("row", "col", "pair"), None, None), P(), P("pair"))
    return jax.shard_map(
        body, mesh=mesh, in_specs=placed, out_specs=P("row", "pair", "col"), check_vma=False
    )
```

time: 79.1 us -> 78.8 us (level)
  waiting for transfers between devices: 20.3 us -> 18 us
  Pallas kernels: 17.6 us -> 19 us
    pallas_call x3, Pallas kernels: 15.9 us -> 17.2 us  [the longest x1 16 us: ladder_call(): pl.pallas_call(functools.partial(ladder_kernel, cols, group, 2 * LANES),...]
    all_to_all x1, waiting for transfers between devices: 7.96 us -> 6.91 us  [body(): gathered = lax.all_to_all(block, plane, 0, 0, tiled=True)]
    all_to_all x1, waiting for transfers between devices: 5.45 us -> 4.47 us  [body(): tall = lax.all_to_all(sent, 'row', 0, 0, tiled=True)]
  transfers between devices with their start and end apart: 5 -> 5, of which waited for: 3 -> 3; matrix products, arithmetic and copies ran while one was open for 5% -> 6% of each run, Pallas kernels for 2% -> 2%
where the time goes in v8:
time: 78.8 us; the launch traced here: 78.3 us
  starting transfers between devices  21.3 us (27%)
  Pallas kernels  19 us (24%)
  waiting for transfers between devices  18 us (23%)
  blocking collectives  14.2 us (18%)
  local copies, waits for them, and re-layouts  5.01 us (6%)
    pallas_call x1, Pallas kernels, ladder_call(): pl.pallas_call(functools.partial(ladder_kernel, cols, group, 2 * LANES),...  16 us
    all_to_all x1, blocking collectives, body(): finals = lax.all_to_all(packed, 'row', 0, 0, tiled=True)  14.2 us
    all_to_all x1, waiting for transfers between devices, body(): gathered = lax.all_to_all(block, plane, 0, 0, tiled=True)  6.91 us
    all_to_all x1, starting transfers between devices, body(): tall = lax.all_to_all(sent, 'row', 0, 0, tiled=True)  6.88 us
    all_to_all x1, waiting for transfers between devices, body(): pieces = lax.all_to_all(partial_sums, plane, 0, 0, tiled=True)  6.58 us
    all_to_all x1, starting transfers between devices, body(): gathered = lax.all_to_all(block, plane, 0, 0, tiled=True)  6.46 us
    all_to_all x1, waiting for transfers between devices, body(): tall = lax.all_to_all(sent, 'row', 0, 0, tiled=True)  4.47 us
    all_to_all x1, starting transfers between devices, body(): pieces = lax.all_to_all(partial_sums, plane, 0, 0, tiled=True)  3.54 us
  transfers between devices with their start and end apart: 5, of which 3 were waited for; matrix products, arithmetic and copies ran while one was open for 6% of the time, Pallas kernels for 2%

profile of v8, /device:TPU:1, one launch (start us, length us, event | category | flops | bytes accessed | tf_op | source)
XLA Modules:
  0.0 78.3 jit_solution(618137275639338405)
XLA Ops:
  0.0 3.2 %collective-permute-start.1 = (bf16[8,320,320]{2,1,0:T(8,128)(2,1)}, bf16[8,320,320]{2,1,0:T(8,128)(2,1)S(1)}, u32[]{:S(2)}, u32[]{:S(2)}) collective-permute-start(bf16[8,320,320]{2,1,0:T(8,128)(2,1)} %param.5), channel_id=1, source_target_pairs={{0,16},{16,0},{32,48},{48,32},{64,80},{80,64},{96,112},{112,96},{1... | collective-permute-start | bytes 4915208 | tf_op jit(solution)/shard_map/ppermute | solution.py:354
  3.2 0.0 copy-start
  3.2 0.7 copy-done
  3.9 0.9 %shard_map.46 = bf16[16,16,128]{2,1,0:T(8,128)(2,1)} custom-call(bf16[20,4,40]{2,1,0:T(4,128)(2,1)S(1)} %copy-done), custom_call_target="tpu_custom_call" | custom-call | tf_op jit(solution)/shard_map/pallas_call | solution.py:134
  4.8 6.9 %all-to-all-start = ((bf16[16,16,128]{2,1,0:T(8,128)(2,1)}), bf16[16,16,128]{2,1,0:T(8,128)(2,1)S(1)}, u32[]{:S(2)}, u32[]{:S(2)}) async-start(bf16[16,16,128]{2,1,0:T(8,128)(2,1)} %shard_map.46), calls=%async_computation | async-start | bytes 131072 | tf_op jit(solution)/shard_map/all_to_all | solution.py:362
  11.7 0.7 xor.47
  12.4 0.7 dynamic_slice.12
  13.1 0.7 broadcast_in_dim.8.across_ref
  13.8 0.8 dynamic_slice.13
  14.6 0.1 broadcast_xor_fusion.1
  14.7 0.1 xor.46.partner_ref
  14.7 0.1 xor.50
  14.8 0.1 xor.48
  14.9 0.1 xor.49
  15.0 4.5 %all-to-all-done.tall_ref = bf16[16,16,128]{2,1,0:T(8,128)(2,1)S(1)} async-done(((bf16[16,16,128]{2,1,0:T(8,128)(2,1)}), bf16[16,16,128]{2,1,0:T(8,128)(2,1)S(1)}, u32[]{:S(2)}, u32[]{:S(2)}) %all-to-all-start) | async-done | bytes 65568 | tf_op jit(solution)/shard_map/all_to_all | solution.py:362
  19.5 1.0 %shard_map.47 = bf16[16,56,128]{2,1,0:T(8,128)(2,1)} custom-call(bf16[16,16,128]{2,1,0:T(8,128)(2,1)S(1)} %all-to-all-done.tall_ref, s32[1,320]{1,0:T(1,128)S(1)} %broadcast_in_dim.8.across_ref, s32[1,80]{1,0:T(1,128)S(1)} %xor.46.partner_ref), custom_call_target="tpu_custom_call" | custom-call | tf_op jit(solution)/shard_map/pallas_call | solution.py:146
  20.4 1.2 %collective-permute-start = (s32[4]{0:T(128)}, s32[4]{0:T(128)S(1)}, u32[]{:S(2)}, u32[]{:S(2)}) collective-permute-start(s32[4]{0:T(128)} %param.7), channel_id=1, source_target_pairs={{0,1},{1,0},{2,3},{3,2},{4,5},{5,4},{6,7},{7,6},{8,9},{9,8},{10,11... | collective-permute-start | bytes 56 | tf_op jit(solution)/shard_map/ppermute | solution.py:368
  21.7 6.5 %all-to-all-start.1 = ((bf16[16,56,128]{2,1,0:T(8,128)(2,1)}), bf16[16,56,128]{2,1,0:T(8,128)(2,1)S(1)}, u32[]{:S(2)}, u32[]{:S(2)}) async-start(bf16[16,56,128]{2,1,0:T(8,128)(2,1)} %shard_map.47), calls=%async_computation.1 | async-start | bytes 458752 | tf_op jit(solution)/shard_map/all_to_all | solution.py:366
  28.1 0.0 collective-permute-done
  28.1 0.7 fusion
  28.8 0.1 constant_dynamic-slice_fusion
  28.9 0.1 broadcast_in_dim.9
  29.0 6.9 %all-to-all-done.1.t_ref = bf16[16,56,128]{2,1,0:T(8,128)(2,1)S(1)} async-done(((bf16[16,56,128]{2,1,0:T(8,128)(2,1)}), bf16[16,56,128]{2,1,0:T(8,128)(2,1)S(1)}, u32[]{:S(2)}, u32[]{:S(2)}) %all-to-all-start.1) | async-done | bytes 229408 | tf_op jit(solution)/shard_map/all_to_all | solution.py:366
  35.9 0.0 collective-permute-done.1
  35.9 0.1 broadcast_in_dim.10.pair_ref
  35.9 16.0 %shard_map.48 = bf16[16,56,128]{2,1,0:T(8,128)(2,1)} custom-call(s32[4,128]{1,0:T(4,128)S(1)} %broadcast_in_dim.10.pair_ref, bf16[16,56,128]{2,1,0:T(8,128)(2,1)S(1)} %all-to-all-done.1.t_ref, bf16[2560,320]{1,0:T(8,128)(2,1)S(1)} %bitcast.6, bf16[2560,320]{1,0:T(8,128)(2,1)} %bitcast.7, s32[1,320]{1,0:T(1,128)S(1)} %broadcast_in_dim.8.across_ref), custom_call_target="tpu_custom_call" | custom-call | tf_op jit(solution)/shard_map/pallas_call | solution.py:321
  52.0 3.5 %all-to-all-start.2 = ((bf16[16,56,128]{2,1,0:T(8,128)(2,1)}), bf16[16,56,128]{2,1,0:T(8,128)(2,1)S(1)}, u32[]{:S(2)}, u32[]{:S(2)}) async-start(bf16[16,56,128]{2,1,0:T(8,128)(2,1)} %shard_map.48), calls=%async_computation.2 | async-start | bytes 458752 | tf_op jit(solution)/shard_map/all_to_all | solution.py:378
  55.6 0.8 dynamic_slice.15
  56.3 6.6 %all-to-all-done.2.pieces_ref = bf16[16,56,128]{2,1,0:T(8,128)(2,1)S(1)} async-done(((bf16[16,56,128]{2,1,0:T(8,128)(2,1)}), bf16[16,56,128]{2,1,0:T(8,128)(2,1)S(1)}, u32[]{:S(2)}, u32[]{:S(2)}) %all-to-all-start.2) | async-done | bytes 229408 | tf_op jit(solution)/shard_map/all_to_all | solution.py:378
  62.9 0.2 shard_map.49
  63.1 0.1 broadcast_in_dim.11.down_ref
  63.2 14.2 %all_to_all.20.finals_ref = f32[16,16,128]{2,1,0:T(8,128)S(1)} all-to-all(f32[16,16,128]{2,1,0:T(8,128)S(1)} %shard_map.49), channel_id=1, replica_groups=mesh['row'=16,'col'=8,'pair'=2] {'row'}, dimensions={0} | all-to-all | bytes 262144 | tf_op jit(solution)/shard_map/all_to_all | solution.py:384
  77.4 0.9 %shard_map.50 = f32[20,4,40]{2,1,0:T(4,128)} custom-call(f32[16,16,128]{2,1,0:T(8,128)S(1)} %all_to_all.20.finals_ref, s32[20,128]{1,0:T(8,128)S(1)} %broadcast_in_dim.11.down_ref, s32[2,80]{1,0:T(2,128)S(1)} %broadcast_xor_fusion.across_ref), custom_call_target="tpu_custom_call" | custom-call | tf_op jit(solution)/shard_map/pallas_call | solution.py:210
  (3 shorter events, 0.0 us)
Async XLA Ops:
  0.0 35.9 %collective-permute-start.1 = (bf16[8,320,320]{2,1,0:T(8,128)(2,1)}, bf16[8,320,320]{2,1,0:T(8,128)(2,1)S(1)}, u32[]{:S(2)}, u32[]{:S(2)}) collective-permute-start(bf16[8,320,320]{2,1,0:T(8,128)(2,1)} %param.5), channel_id=1, source_target_pairs={{0,16},{16,0},{32,48},{48,32},{64,80},{80,64},{96,112},{112,96},{1... | collective-permute-start | bytes 4915208 | tf_op jit(solution)/shard_map/ppermute | solution.py:354
  3.2 0.7 copy-start
  4.8 14.7 %all-to-all-start = ((bf16[16,16,128]{2,1,0:T(8,128)(2,1)}), bf16[16,16,128]{2,1,0:T(8,128)(2,1)S(1)}, u32[]{:S(2)}, u32[]{:S(2)}) async-start(bf16[16,16,128]{2,1,0:T(8,128)(2,1)} %shard_map.46), calls=%async_computation | async-start | bytes 131072 | tf_op jit(solution)/shard_map/all_to_all | solution.py:362
  20.4 7.7 %collective-permute-start = (s32[4]{0:T(128)}, s32[4]{0:T(128)S(1)}, u32[]{:S(2)}, u32[]{:S(2)}) collective-permute-start(s32[4]{0:T(128)} %param.7), channel_id=1, source_target_pairs={{0,1},{1,0},{2,3},{3,2},{4,5},{5,4},{6,7},{7,6},{8,9},{9,8},{10,11... | collective-permute-start | bytes 56 | tf_op jit(solution)/shard_map/ppermute | solution.py:368
  21.7 14.2 %all-to-all-start.1 = ((bf16[16,56,128]{2,1,0:T(8,128)(2,1)}), bf16[16,56,128]{2,1,0:T(8,128)(2,1)S(1)}, u32[]{:S(2)}, u32[]{:S(2)}) async-start(bf16[16,56,128]{2,1,0:T(8,128)(2,1)} %shard_map.47), calls=%async_computation.1 | async-start | bytes 458752 | tf_op jit(solution)/shard_map/all_to_all | solution.py:366
  52.0 10.9 %all-to-all-start.2 = ((bf16[16,56,128]{2,1,0:T(8,128)(2,1)}), bf16[16,56,128]{2,1,0:T(8,128)(2,1)S(1)}, u32[]{:S(2)}, u32[]{:S(2)}) async-start(bf16[16,56,128]{2,1,0:T(8,128)(2,1)} %shard_map.48), calls=%async_computation.2 | async-start | bytes 458752 | tf_op jit(solution)/shard_map/all_to_all | solution.py:378

commit v9 on v8

--- a/solution.py
+++ b/solution.py
@@ -57,19 +57,6 @@
     ]
     second = jnp.where(lane < LEFT, turn(first, -FOLD), jnp.concatenate(tail, axis=0))
     return first, second
-
-
-def unfold(x, tiles):
-    lane = lanes()
-    out = []
-    for t in range(tiles):
-        base = t * LANES
-        tile = None
-        for m in range(base // FOLD, -(-(base + LANES) // FOLD)):
-            moved = turn(x, m * FOLD - base)
-            tile = moved if tile is None else jnp.where(lane >= m * FOLD - base, moved, tile)
-        out.append(tile)
-    return out
 
 
 def fold(pieces):
@@ -107,26 +94,36 @@
             out_ref[m] = packed
 
 
-def fold_kernel(row_block, col_block, tall_ref, across_ref, partner_ref, out_ref):
+def fold_kernel(row_block, tall_ref, across_ref, partner_ref, out_ref):
+    groups, held, col_block, _ = out_ref.shape
     width = across_ref.shape[1]
-    lines = partner_ref.shape[1]
-    partner = jnp.broadcast_to(partner_ref[...], (SUB, lines)).T[:, :1]
-    lane = lanes()
-    filler = jnp.full((1, LANES - FOLD), -1, jnp.int32)
+    lines = held * col_block
+    tiles = -(-width // LANES)
+    filler = jnp.full((1, tiles * LANES - width), -1, jnp.int32)
+    labels = jnp.concatenate([across_ref[...], filler], axis=1)
+    partner = jnp.broadcast_to(partner_ref[...], (8, lines)).T[:, :1]
+    lane = lax.broadcasted_iota(jnp.int32, (1, LANES), 1)
     folded = [jnp.zeros((PACK, LANES), jnp.float32) for _ in range(lines // PACK)]
-    for m in range(width // FOLD):
-        labels = jnp.concatenate([across_ref[:, m * FOLD : (m + 1) * FOLD], filler], axis=1)
-        for k in range(FOLD // row_block):
-            low = k * row_block
-            here = jnp.where((lane >= low) & (lane < low + row_block), labels, -1)
-            piece = tall_ref[m * (FOLD // row_block) + k].astype(jnp.float32)
-            for g in range(lines // PACK):
-                fits = partner[g * PACK : (g + 1) * PACK] == here
-                folded[g] = folded[g] + jnp.where(fits, turn(piece, (k - g) * row_block), 0.0)
+    for r in range(tall_ref.shape[0]):
+        tile, low = r * row_block // LANES, r * row_block % LANES
+        here = jnp.where(
+            (lane >= low) & (lane < low + row_block), labels[:, tile * LANES : (tile + 1) * LANES], -1
+        )
+        over = low + row_block - LANES
+        if over > 0:
+            following = labels[:, (tile + 1) * LANES : (tile + 2) * LANES]
+            here = jnp.where(lane < over, following, here)
+        piece = tall_ref[r].astype(jnp.float32)
+        for g in range(lines // PACK):
+            shift = (r - g) * row_block % LANES
+            moved = pltpu.roll(piece, shift, 1) if shift else piece
+            fits = partner[g * PACK : (g + 1) * PACK] == here
+            folded[g] = folded[g] + jnp.where(fits, moved, 0.0)
     block = jnp.concatenate(folded, axis=0)
-    block = join(block[:col_block], block[col_block:]).astype(out_ref.dtype)
-    for m in range(out_ref.shape[0]):
-        out_ref[m] = block
+    for j in range(held):
+        part = block[j * col_block : (j + 1) * col_block].astype(out_ref.dtype)
+        for m in range(groups):
+            out_ref[m, j] = part
 
 
 def spread_call(amplitudes, rows):
@@ -140,12 +137,12 @@
     )(amplitudes)
 
 
-def fold_call(tall, across, partner, row_block, col_block, groups):
+def fold_call(tall, across, partner, row_block, shape):
     vmem = pl.BlockSpec(memory_space=pltpu.VMEM)
     close = functools.partial(pltpu.with_memory_space_constraint, memory_space=pltpu.VMEM)
     return pl.pallas_call(
-        functools.partial(fold_kernel, row_block, col_block),
-        out_shape=jax.ShapeDtypeStruct((groups, joined_rows(col_block), LANES), tall.dtype),
+        functools.partial(fold_kernel, row_block),
+        out_shape=jax.ShapeDtypeStruct(shape, tall.dtype),
         in_specs=[vmem] * 3,
         out_specs=vmem,
         compiler_params=pltpu.CompilerParams(vmem_limit_bytes=8 * 2**20),
@@ -246,14 +243,13 @@
     filler = jnp.full((1, tiles * LANES - width), -1, jnp.int32)
     down = jnp.broadcast_to(across_ref[...], (8, width)).T[:, :1]
     mixed = jnp.bitwise_xor(down, jnp.concatenate([across_ref[...], filler], axis=1))
-    for half in range(groups):
-        both = [part(t_ref[q * groups + half].astype(jnp.float32), block) for q in range(cols)]
-        for at in range(CORES):
-            p = half * CORES + at
-            rows = jnp.concatenate([pieces[at] for pieces in both], axis=0)
-            spread = jnp.concatenate(unfold(rows, tiles), axis=1)
-            spread = jnp.where(mixed == pair_ref[p : p + 1, :1], spread, 0.0)
-            amp[p * width : (p + 1) * width, :] = spread.astype(jnp.bfloat16)[:, :width]
+    for p in range(pairs):
+        half, at = p // CORES, p % CORES
+        rows = jnp.concatenate(
+            [t_ref[q * groups + half, at].astype(jnp.float32) for q in range(cols)], axis=0
+        )
+        spread = jnp.where(mixed == pair_ref[p : p + 1, :1], jnp.concatenate([rows] * tiles, axis=1), 0.0)
+        amp[p * width : (p + 1) * width, :] = spread.astype(jnp.bfloat16)[:, :width]
 
     for source, base in ((near_ref, 0), (stack, half_steps)):
         if base:
@@ -320,7 +316,9 @@
     close = functools.partial(pltpu.with_memory_space_constraint, memory_space=pltpu.VMEM)
     return pl.pallas_call(
         functools.partial(ladder_kernel, cols, group, 2 * LANES),
-        out_shape=pltpu.VMEM(gathered.shape, jnp.bfloat16),
+        out_shape=jax.ShapeDtypeStruct(
+            (gathered.shape[0], joined_rows(width // cols), LANES), jnp.bfloat16
+        ),
         in_specs=[vmem, vmem, vmem, anywhere, vmem],
         out_specs=vmem,
         scratch_shapes=[
@@ -361,7 +359,7 @@
     sent = spread_call(amplitudes, rows)
     tall = lax.all_to_all(sent, "row", 0, 0, tiled=True)
     groups = cols * lax.axis_size("pair")
-    block = fold_call(tall, across, partner, row_block, col_block, groups)
+    block = fold_call(tall, across, partner, row_block, (groups, held, col_block, LANES))
     block, late_vir, late_pair = lax.optimization_barrier((block, vir_irrep, pair_irrep))
     gathered = lax.all_to_all(block, plane, 0, 0, tiled=True)
 
@@ -377,7 +375,7 @@
 
     pieces = lax.all_to_all(partial_sums, plane, 0, 0, tiled=True)
     packed = pack_call(pieces, rows, row_block, col_block)
-    need = jnp.bitwise_xor(pair_irrep[:, None], col_labels[None, :]).reshape(CORES, inner)
+    need = jnp.bitwise_xor(late_pair[:, None], col_labels[None, :]).reshape(CORES, inner)
     packed, row_labels, need = lax.optimization_barrier(
         (packed, jnp.broadcast_to(row_labels[:, None], (row_block, LANES)), need)
     )

time: 78.8 us -> 79.7 us (1.011)
  waiting for transfers between devices: 18 us -> 19.8 us
  Pallas kernels: 19 us -> 18 us
    pallas_call x1, Pallas kernels: 16 us -> 15.1 us  [ladder_call(): pl.pallas_call(functools.partial(ladder_kernel, cols, group, 2 * LANES),...]
    all_to_all x1, waiting for transfers between devices: 4.47 us -> 5.36 us  [body(): tall = lax.all_to_all(sent, 'row', 0, 0, tiled=True)]
where the time goes in v9:
time: 79.7 us; the launch traced here: 79.1 us
  starting transfers between devices  21.3 us (27%)
  waiting for transfers between devices  19.8 us (25%)
  Pallas kernels  18 us (23%)
  blocking collectives  14.2 us (18%)
  local copies, waits for them, and re-layouts  5.04 us (6%)
    pallas_call x1, Pallas kernels, ladder_call(): pl.pallas_call(functools.partial(ladder_kernel, cols, group, 2 * LANES),...  15.1 us
    all_to_all x1, blocking collectives, body(): finals = lax.all_to_all(packed, 'row', 0, 0, tiled=True)  14.2 us
    all_to_all x1, waiting for transfers between devices, body(): pieces = lax.all_to_all(partial_sums, plane, 0, 0, tiled=True)  7.34 us
    all_to_all x1, waiting for transfers between devices, body(): gathered = lax.all_to_all(block, plane, 0, 0, tiled=True)  7.06 us
    all_to_all x1, starting transfers between devices, body(): tall = lax.all_to_all(sent, 'row', 0, 0, tiled=True)  6.88 us
    all_to_all x1, starting transfers between devices, body(): gathered = lax.all_to_all(block, plane, 0, 0, tiled=True)  6.46 us
    all_to_all x1, waiting for transfers between devices, body(): tall = lax.all_to_all(sent, 'row', 0, 0, tiled=True)  5.36 us
    all_to_all x1, starting transfers between devices, body(): pieces = lax.all_to_all(partial_sums, plane, 0, 0, tiled=True)  3.54 us
  transfers between devices with their start and end apart: 5, of which 3 were waited for; matrix products, arithmetic and copies ran while one was open for 6% of the time, Pallas kernels for 2%

profile of v9, /device:TPU:1, one launch (start us, length us, event | category | flops | bytes accessed | tf_op | source)
XLA Modules:
  0.0 79.1 jit_solution(1738508098804662828)
XLA Ops:
  0.0 3.2 %collective-permute-start.1 = (bf16[8,320,320]{2,1,0:T(8,128)(2,1)}, bf16[8,320,320]{2,1,0:T(8,128)(2,1)S(1)}, u32[]{:S(2)}, u32[]{:S(2)}) collective-permute-start(bf16[8,320,320]{2,1,0:T(8,128)(2,1)} %param.5), channel_id=1, source_target_pairs={{0,16},{16,0},{32,48},{48,32},{64,80},{80,64},{96,112},{112,96},{1... | collective-permute-start | bytes 4915208 | tf_op jit(solution)/shard_map/ppermute | solution.py:352
  3.2 0.0 copy-start
  3.2 0.7 copy-done
  3.9 0.9 %shard_map.46 = bf16[16,16,128]{2,1,0:T(8,128)(2,1)} custom-call(bf16[20,4,40]{2,1,0:T(4,128)(2,1)S(1)} %copy-done), custom_call_target="tpu_custom_call" | custom-call | tf_op jit(solution)/shard_map/pallas_call | solution.py:131
  4.8 6.9 %all-to-all-start = ((bf16[16,16,128]{2,1,0:T(8,128)(2,1)}), bf16[16,16,128]{2,1,0:T(8,128)(2,1)S(1)}, u32[]{:S(2)}, u32[]{:S(2)}) async-start(bf16[16,16,128]{2,1,0:T(8,128)(2,1)} %shard_map.46), calls=%async_computation | async-start | bytes 131072 | tf_op jit(solution)/shard_map/all_to_all | solution.py:360
  11.7 0.7 broadcast_in_dim.8.across_ref
  12.4 0.8 dynamic_slice.13
  13.1 0.7 dynamic_slice.12
  13.8 0.1 broadcast_xor_fusion.1
  13.9 0.1 xor.46.partner_ref
  14.0 0.1 xor.50
  14.1 5.4 %all-to-all-done.tall_ref = bf16[16,16,128]{2,1,0:T(8,128)(2,1)S(1)} async-done(((bf16[16,16,128]{2,1,0:T(8,128)(2,1)}), bf16[16,16,128]{2,1,0:T(8,128)(2,1)S(1)}, u32[]{:S(2)}, u32[]{:S(2)}) %all-to-all-start) | async-done | bytes 65568 | tf_op jit(solution)/shard_map/all_to_all | solution.py:360
  19.5 1.0 %shard_map.47 = bf16[16,2,40,128]{3,2,1,0:T(8,128)(2,1)} custom-call(bf16[16,16,128]{2,1,0:T(8,128)(2,1)S(1)} %all-to-all-done.tall_ref, s32[1,320]{1,0:T(1,128)S(1)} %broadcast_in_dim.8.across_ref, s32[1,80]{1,0:T(1,128)S(1)} %xor.46.partner_ref), custom_call_target="tpu_custom_call" | custom-call | tf_op jit(solution)/shard_map/pallas_call | solution.py:143
  20.4 1.2 %collective-permute-start = (s32[4]{0:T(128)}, s32[4]{0:T(128)S(1)}, u32[]{:S(2)}, u32[]{:S(2)}) collective-permute-start(s32[4]{0:T(128)} %param.7), channel_id=1, source_target_pairs={{0,1},{1,0},{2,3},{3,2},{4,5},{5,4},{6,7},{7,6},{8,9},{9,8},{10,11... | collective-permute-start | bytes 56 | tf_op jit(solution)/shard_map/ppermute | solution.py:366
  21.6 0.8 xor.47
  22.4 6.5 %all-to-all-start.1 = ((bf16[16,2,40,128]{3,2,1,0:T(8,128)(2,1)}), bf16[16,2,40,128]{3,2,1,0:T(8,128)(2,1)S(1)}, u32[]{:S(2)}, u32[]{:S(2)}) async-start(bf16[16,2,40,128]{3,2,1,0:T(8,128)(2,1)} %shard_map.47), calls=%async_computation.1 | async-start | bytes 655360 | tf_op jit(solution)/shard_map/all_to_all | solution.py:364
  28.9 0.1 xor.48
  29.0 0.1 xor.49
  29.0 0.8 dynamic_slice.15
  29.8 0.0 collective-permute-done
  29.8 0.7 fusion
  30.5 0.1 constant_dynamic-slice_fusion
  30.5 0.1 broadcast_in_dim.9
  30.6 7.1 %all-to-all-done.1.t_ref = bf16[16,2,40,128]{3,2,1,0:T(8,128)(2,1)S(1)} async-done(((bf16[16,2,40,128]{3,2,1,0:T(8,128)(2,1)}), bf16[16,2,40,128]{3,2,1,0:T(8,128)(2,1)S(1)}, u32[]{:S(2)}, u32[]{:S(2)}) %all-to-all-start.1) | async-done | bytes 327712 | tf_op jit(solution)/shard_map/all_to_all | solution.py:364
  37.7 0.0 collective-permute-done.1
  37.7 0.1 broadcast_in_dim.10.pair_ref
  37.8 15.1 %shard_map.48 = bf16[16,56,128]{2,1,0:T(8,128)(2,1)} custom-call(s32[4,128]{1,0:T(4,128)S(1)} %broadcast_in_dim.10.pair_ref, bf16[16,2,40,128]{3,2,1,0:T(8,128)(2,1)S(1)} %all-to-all-done.1.t_ref, bf16[2560,320]{1,0:T(8,128)(2,1)S(1)} %bitcast.6, bf16[2560,320]{1,0:T(8,128)(2,1)} %bitcast.7, s32[1,320]{1,0:T(1,128)S(1)} %broadcast_in_dim.8.across_ref), custom_call_target="tpu_custom_call" | custom-call | tf_op jit(solution)/shard_map/pallas_call | solution.py:317
  52.8 3.5 %all-to-all-start.2 = ((bf16[16,56,128]{2,1,0:T(8,128)(2,1)}), bf16[16,56,128]{2,1,0:T(8,128)(2,1)S(1)}, u32[]{:S(2)}, u32[]{:S(2)}) async-start(bf16[16,56,128]{2,1,0:T(8,128)(2,1)} %shard_map.48), calls=%async_computation.2 | async-start | bytes 458752 | tf_op jit(solution)/shard_map/all_to_all | solution.py:376
  56.4 7.3 %all-to-all-done.2.pieces_ref = bf16[16,56,128]{2,1,0:T(8,128)(2,1)S(1)} async-done(((bf16[16,56,128]{2,1,0:T(8,128)(2,1)}), bf16[16,56,128]{2,1,0:T(8,128)(2,1)S(1)}, u32[]{:S(2)}, u32[]{:S(2)}) %all-to-all-start.2) | async-done | bytes 229408 | tf_op jit(solution)/shard_map/all_to_all | solution.py:376
  63.7 0.2 shard_map.49
  63.9 0.1 broadcast_in_dim.11.down_ref
  64.0 14.2 %all_to_all.20.finals_ref = f32[16,16,128]{2,1,0:T(8,128)S(1)} all-to-all(f32[16,16,128]{2,1,0:T(8,128)S(1)} %shard_map.49), channel_id=1, replica_groups=mesh['row'=16,'col'=8,'pair'=2] {'row'}, dimensions={0} | all-to-all | bytes 262144 | tf_op jit(solution)/shard_map/all_to_all | solution.py:382
  78.2 0.9 %shard_map.50 = f32[20,4,40]{2,1,0:T(4,128)} custom-call(f32[16,16,128]{2,1,0:T(8,128)S(1)} %all_to_all.20.finals_ref, s32[20,128]{1,0:T(8,128)S(1)} %broadcast_in_dim.11.down_ref, s32[2,80]{1,0:T(2,128)S(1)} %broadcast_xor_fusion.across_ref), custom_call_target="tpu_custom_call" | custom-call | tf_op jit(solution)/shard_map/pallas_call | solution.py:207
  (3 shorter events, 0.0 us)
Async XLA Ops:
  0.0 37.7 %collective-permute-start.1 = (bf16[8,320,320]{2,1,0:T(8,128)(2,1)}, bf16[8,320,320]{2,1,0:T(8,128)(2,1)S(1)}, u32[]{:S(2)}, u32[]{:S(2)}) collective-permute-start(bf16[8,320,320]{2,1,0:T(8,128)(2,1)} %param.5), channel_id=1, source_target_pairs={{0,16},{16,0},{32,48},{48,32},{64,80},{80,64},{96,112},{112,96},{1... | collective-permute-start | bytes 4915208 | tf_op jit(solution)/shard_map/ppermute | solution.py:352
  3.2 0.7 copy-start
  4.8 14.7 %all-to-all-start = ((bf16[16,16,128]{2,1,0:T(8,128)(2,1)}), bf16[16,16,128]{2,1,0:T(8,128)(2,1)S(1)}, u32[]{:S(2)}, u32[]{:S(2)}) async-start(bf16[16,16,128]{2,1,0:T(8,128)(2,1)} %shard_map.46), calls=%async_computation | async-start | bytes 131072 | tf_op jit(solution)/shard_map/all_to_all | solution.py:360
  20.4 9.4 %collective-permute-start = (s32[4]{0:T(128)}, s32[4]{0:T(128)S(1)}, u32[]{:S(2)}, u32[]{:S(2)}) collective-permute-start(s32[4]{0:T(128)} %param.7), channel_id=1, source_target_pairs={{0,1},{1,0},{2,3},{3,2},{4,5},{5,4},{6,7},{7,6},{8,9},{9,8},{10,11... | collective-permute-start | bytes 56 | tf_op jit(solution)/shard_map/ppermute | solution.py:366
  22.4 15.3 %all-to-all-start.1 = ((bf16[16,2,40,128]{3,2,1,0:T(8,128)(2,1)}), bf16[16,2,40,128]{3,2,1,0:T(8,128)(2,1)S(1)}, u32[]{:S(2)}, u32[]{:S(2)}) async-start(bf16[16,2,40,128]{3,2,1,0:T(8,128)(2,1)} %shard_map.47), calls=%async_computation.1 | async-start | bytes 655360 | tf_op jit(solution)/shard_map/all_to_all | solution.py:364
  52.8 10.9 %all-to-all-start.2 = ((bf16[16,56,128]{2,1,0:T(8,128)(2,1)}), bf16[16,56,128]{2,1,0:T(8,128)(2,1)S(1)}, u32[]{:S(2)}, u32[]{:S(2)}) async-start(bf16[16,56,128]{2,1,0:T(8,128)(2,1)} %shard_map.48), calls=%async_computation.2 | async-start | bytes 458752 | tf_op jit(solution)/shard_map/all_to_all | solution.py:376

commit v10 on v8

--- a/solution.py
+++ b/solution.py
@@ -89,6 +89,21 @@
 
 
 PACK = 16
+
+
+def pick(row, index, size):
+    out = row[:, :size]
+    for k in range(1, row.shape[1] // size):
+        out = jnp.where(index == k, row[:, k * size : (k + 1) * size], out)
+    return out
+
+
+def split_labels(label_ref, width):
+    return label_ref[:, :width], label_ref[:, width:]
+
+
+def as_column(row):
+    return jnp.broadcast_to(row, (SUB, row.shape[1])).T[:, :1]
 
 
 def spread_kernel(amp_ref, out_ref):
@@ -107,15 +122,21 @@
             out_ref[m] = packed
 
 
-def fold_kernel(row_block, col_block, tall_ref, across_ref, partner_ref, out_ref):
-    width = across_ref.shape[1]
-    lines = partner_ref.shape[1]
-    partner = jnp.broadcast_to(partner_ref[...], (SUB, lines)).T[:, :1]
+def fold_kernel(row_block, col_block, tall_ref, label_ref, out_ref):
+    width = tall_ref.shape[0] * row_block
+    across, own_pairs = split_labels(label_ref, width)
+    held = own_pairs.shape[1] // CORES
+    lines = held * col_block
+    mine = pick(across, lax.axis_index("col"), col_block)
+    pairs = pick(own_pairs, lax.axis_index("row") % CORES, held)
+    partner = as_column(
+        jnp.concatenate([jnp.bitwise_xor(mine, pairs[:, j : j + 1]) for j in range(held)], axis=1)
+    )
     lane = lanes()
     filler = jnp.full((1, LANES - FOLD), -1, jnp.int32)
     folded = [jnp.zeros((PACK, LANES), jnp.float32) for _ in range(lines // PACK)]
     for m in range(width // FOLD):
-        labels = jnp.concatenate([across_ref[:, m * FOLD : (m + 1) * FOLD], filler], axis=1)
+        labels = jnp.concatenate([across[:, m * FOLD : (m + 1) * FOLD], filler], axis=1)
         for k in range(FOLD // row_block):
             low = k * row_block
             here = jnp.where((lane >= low) & (lane < low + row_block), labels, -1)
@@ -140,16 +161,16 @@
     )(amplitudes)
 
 
-def fold_call(tall, across, partner, row_block, col_block, groups):
+def fold_call(tall, labels, row_block, col_block, groups):
     vmem = pl.BlockSpec(memory_space=pltpu.VMEM)
     close = functools.partial(pltpu.with_memory_space_constraint, memory_space=pltpu.VMEM)
     return pl.pallas_call(
         functools.partial(fold_kernel, row_block, col_block),
         out_shape=jax.ShapeDtypeStruct((groups, joined_rows(col_block), LANES), tall.dtype),
-        in_specs=[vmem] * 3,
+        in_specs=[vmem] * 2,
         out_specs=vmem,
         compiler_params=pltpu.CompilerParams(vmem_limit_bytes=8 * 2**20),
-    )(close(tall), close(across), close(partner))
+    )(close(tall), close(labels))
 
 
 def pack_kernel(row_block, col_block, pieces_ref, out_ref):
@@ -170,10 +191,14 @@
             out_ref[r] = packed
 
 
-def unpack_kernel(finals_ref, down_ref, across_ref, out_ref):
+def unpack_kernel(finals_ref, label_ref, out_ref):
     row_block, pairs_here, col_block = out_ref.shape
     held = pairs_here // CORES
     lines = held * col_block
+    width = finals_ref.shape[0] * row_block
+    across, own_pairs = split_labels(label_ref, width)
+    down = as_column(pick(across, lax.axis_index("row"), row_block))
+    mine = pick(across, lax.axis_index("col"), col_block)
     for c in range(CORES):
         total = finals_ref[c]
         for z in range(CORES + c, finals_ref.shape[0], CORES):
@@ -185,11 +210,12 @@
             ],
             axis=0,
         )
-        spread = jnp.where(
-            down_ref[:, :1] == across_ref[c : c + 1, :lines], spread.T[:row_block], 0.0
-        )
+        spread = spread.T[:row_block]
         for j in range(held):
-            out_ref[:, c * held + j, :] = spread[:, j * col_block : (j + 1) * col_block]
+            at = c * held + j
+            wanted = jnp.bitwise_xor(mine, own_pairs[:, at : at + 1])
+            piece = spread[:, j * col_block : (j + 1) * col_block]
+            out_ref[:, at, :] = jnp.where(down == wanted, piece, 0.0)
 
 
 def pack_call(pieces, rows, row_block, col_block):
@@ -204,27 +230,27 @@
     )(close(pieces))
 
 
-def unpack_call(finals, down, across, shape):
+def unpack_call(finals, labels, shape):
     close = functools.partial(pltpu.with_memory_space_constraint, memory_space=pltpu.VMEM)
     vmem = pl.BlockSpec(memory_space=pltpu.VMEM)
     return pl.pallas_call(
         unpack_kernel,
         out_shape=jax.ShapeDtypeStruct(shape, jnp.float32),
-        in_specs=[vmem] * 3,
+        in_specs=[vmem] * 2,
         out_specs=vmem,
         compiler_params=pltpu.CompilerParams(vmem_limit_bytes=8 * 2**20),
-    )(close(finals), close(down), close(across))
+    )(close(finals), close(labels))
 
 
 def ladder_kernel(
     cols,
     group,
     lane_group,
-    pair_ref,
+    other_pair_ref,
     t_ref,
     near_ref,
     far_ref,
-    across_ref,
+    label_ref,
     out_ref,
     inner,
     amp,
@@ -233,9 +259,10 @@
     stack,
     arrived,
 ):
-    width = across_ref.shape[1]
-    half_depth = near_ref.shape[0]
-    groups, pairs = t_ref.shape[0] // cols, pair_ref.shape[0]
+    half_depth, width = near_ref.shape
+    across, own_pairs = split_labels(label_ref, width)
+    groups = t_ref.shape[0] // cols
+    pairs = own_pairs.shape[1] // CORES * groups
     tiles = -(-width // LANES)
     block = width // cols
     step = group * width
@@ -244,15 +271,22 @@
     fetch = pltpu.make_async_copy(far_ref, stack, arrived)
     fetch.start()
     filler = jnp.full((1, tiles * LANES - width), -1, jnp.int32)
-    down = jnp.broadcast_to(across_ref[...], (8, width)).T[:, :1]
-    mixed = jnp.bitwise_xor(down, jnp.concatenate([across_ref[...], filler], axis=1))
+    down = as_column(across)
+    mixed = jnp.bitwise_xor(down, jnp.concatenate([across, filler], axis=1))
+    core, place = lax.axis_index("row") % CORES, lax.axis_index("pair")
+    own_pairs = pick(own_pairs, core, pairs // groups)
+    other_pairs = pick(other_pair_ref[...], core, pairs // groups)
+    wanted = []
+    for half in range(groups):
+        chosen = jnp.where(place == half, own_pairs, other_pairs)
+        wanted += [chosen[:, j : j + 1] for j in range(pairs // groups)]
     for half in range(groups):
         both = [part(t_ref[q * groups + half].astype(jnp.float32), block) for q in range(cols)]
         for at in range(CORES):
             p = half * CORES + at
             rows = jnp.concatenate([pieces[at] for pieces in both], axis=0)
             spread = jnp.concatenate(unfold(rows, tiles), axis=1)
-            spread = jnp.where(mixed == pair_ref[p : p + 1, :1], spread, 0.0)
+            spread = jnp.where(mixed == wanted[p], spread, 0.0)
             amp[p * width : (p + 1) * width, :] = spread.astype(jnp.bfloat16)[:, :width]
 
     for source, base in ((near_ref, 0), (stack, half_steps)):
@@ -296,7 +330,7 @@
         for at in range(CORES):
             p = half * CORES + at
             ladder = jnp.concatenate([ladders[:, p * width : (p + 1) * width], blank], axis=1)
-            ladder = jnp.where(mixed == pair_ref[p : p + 1, :1], ladder, 0.0)
+            ladder = jnp.where(mixed == wanted[p], ladder, 0.0)
             tall = ladder[:FOLD]
             for start in range(FOLD, width, FOLD):
                 tall = tall + ladder[start : start + FOLD]
@@ -310,9 +344,9 @@
             out_ref[q * groups + half] = join(both[0][span], both[1][span]).astype(out_ref.dtype)
 
 
-def ladder_call(gathered, near, far, across, pair_labels, cols):
+def ladder_call(gathered, near, far, labels, other_pairs, cols):
     count, width, _ = near.shape
-    pairs = pair_labels.shape[0]
+    pairs = other_pairs.shape[1]
     group = 4
     depth, lanes = 2 * count * width, pairs * width
     vmem = pl.BlockSpec(memory_space=pltpu.VMEM)
@@ -333,56 +367,36 @@
         ],
         compiler_params=pltpu.CompilerParams(vmem_limit_bytes=40 * 2**20),
     )(
-        close(jnp.broadcast_to(pair_labels[:, None], (pairs, LANES))),
+        close(other_pairs),
         close(gathered),
         close(near.reshape(count * width, width)),
         pltpu.with_memory_space_constraint(far.reshape(count * width, width), pltpu.HBM),
-        close(across),
+        close(labels),
     )
 
 
 def body(amplitudes, factors, vir_irrep, pair_irrep):
-    row_block, pairs_here, col_block = amplitudes.shape
+    row_block, _, col_block = amplitudes.shape
     width = vir_irrep.shape[0]
     rows, cols = width // row_block, width // col_block
-    held = pairs_here // CORES
-    inner = held * col_block
     plane = ("col", "pair")
-    core = lax.axis_index("row") % CORES
     swap = [(k, k ^ 1) for k in range(rows)]
+    labels = jnp.concatenate([vir_irrep, pair_irrep])[None, :]
 
     other_factors = lax.ppermute(factors, "row", swap)
-
-    col_labels = lax.dynamic_slice_in_dim(vir_irrep, lax.axis_index("col") * col_block, col_block)
-    pairs_held = lax.dynamic_slice_in_dim(pair_irrep, core * held, held)
-    partner = jnp.bitwise_xor(pairs_held[:, None], col_labels[None, :]).reshape(1, inner)
-    across = vir_irrep[None, :]
+    other_pairs = lax.ppermute(pair_irrep[None, :], "pair", [(0, 1), (1, 0)])
 
     sent = spread_call(amplitudes, rows)
     tall = lax.all_to_all(sent, "row", 0, 0, tiled=True)
+    tall, other_pairs = lax.optimization_barrier((tall, other_pairs))
     groups = cols * lax.axis_size("pair")
-    block = fold_call(tall, across, partner, row_block, col_block, groups)
-    block, late_vir, late_pair = lax.optimization_barrier((block, vir_irrep, pair_irrep))
+    block = fold_call(tall, labels, row_block, col_block, groups)
     gathered = lax.all_to_all(block, plane, 0, 0, tiled=True)
-
-    other_pairs = lax.ppermute(late_pair, "pair", [(0, 1), (1, 0)])
-    first = lax.axis_index("pair") == 0
-    pair_labels = jnp.stack(
-        [jnp.where(first, late_pair, other_pairs), jnp.where(first, other_pairs, late_pair)]
-    )
-    pair_labels = lax.dynamic_slice_in_dim(pair_labels, core * held, held, axis=1).reshape(-1)
-    row_labels = lax.dynamic_slice_in_dim(late_vir, lax.axis_index("row") * row_block, row_block)
-
-    partial_sums = ladder_call(gathered, other_factors, factors, across, pair_labels, cols)
-
+    partial_sums = ladder_call(gathered, other_factors, factors, labels, other_pairs, cols)
     pieces = lax.all_to_all(partial_sums, plane, 0, 0, tiled=True)
     packed = pack_call(pieces, rows, row_block, col_block)
-    need = jnp.bitwise_xor(pair_irrep[:, None], col_labels[None, :]).reshape(CORES, inner)
-    packed, row_labels, need = lax.optimization_barrier(
-        (packed, jnp.broadcast_to(row_labels[:, None], (row_block, LANES)), need)
-    )
     finals = lax.all_to_all(packed, "row", 0, 0, tiled=True)
-    return unpack_call(finals, row_labels, need, amplitudes.shape)
+    return unpack_call(finals, labels, amplitudes.shape)
 
 
 def solution(mesh):

time: 78.8 us -> 76.1 us (0.966)
  blocking collectives: 14.2 us -> 38.6 us
  waiting for transfers between devices: 18 us -> 5.79 us
  starting transfers between devices: 21.3 us -> 11.3 us
  local copies, waits for them, and re-layouts: 5.01 us -> 0.73 us
    all_to_all x0 -> x2, blocking collectives: none -> 24.6 us  [the longest x1 14.6 us: body(): gathered = lax.all_to_all(block, plane, 0, 0, tiled=True)]
    all_to_all x2 -> x0, waiting for transfers between devices: 13.5 us -> none  [the longest x1 6.91 us: body(): gathered = lax.all_to_all(block, plane, 0, 0, tiled=True)]
    all_to_all x2 -> x0, starting transfers between devices: 10 us -> none  [the longest x1 6.46 us: body(): gathered = lax.all_to_all(block, plane, 0, 0, tiled=True)]
    dynamic_slice x4 -> x0, local copies, waits for them, and re-layouts: 2.32 us -> none  [the longest x1 0.76 us: body(): lax.dynamic_slice_in_dim(late_vir, lax.axis_index('row') * row_block, row...]
    xor x6 -> x0, local copies, waits for them, and re-layouts: 1.06 us -> none  [the longest x4 0.97 us: body(): jnp.bitwise_xor(pair_irrep[:, None], col_labels[None, :])]
    broadcast_in_dim x4 -> x1, local copies, waits for them, and re-layouts: 0.91 us -> 0.01 us  [body(): labels = jnp.concatenate([vir_irrep, pair_irrep])[None, :]]
  transfers between devices with their start and end apart: 5 -> 3, of which waited for: 3 -> 2; matrix products, arithmetic and copies ran while one was open for 6% -> 1% of each run, Pallas kernels for 2% -> 2%
where the time goes in v10:
time: 76.1 us; the launch traced here: 75.8 us
  blocking collectives  38.6 us (51%)
  Pallas kernels  18.5 us (24%)
  starting transfers between devices  11.3 us (15%)
  waiting for transfers between devices  5.79 us (8%)
  other arithmetic  0.77 us (1%)
    pallas_call x1, Pallas kernels, ladder_call(): pl.pallas_call(functools.partial(ladder_kernel, cols, group, 2 * LANES),...  15.6 us
    all_to_all x1, blocking collectives, body(): gathered = lax.all_to_all(block, plane, 0, 0, tiled=True)  14.6 us
    all_to_all x1, blocking collectives, body(): finals = lax.all_to_all(packed, 'row', 0, 0, tiled=True)  14 us
    all_to_all x1, blocking collectives, body(): pieces = lax.all_to_all(partial_sums, plane, 0, 0, tiled=True)  10.1 us
    all_to_all x1, starting transfers between devices, body(): tall = lax.all_to_all(sent, 'row', 0, 0, tiled=True)  6.88 us
    all_to_all x1, waiting for transfers between devices, body(): tall = lax.all_to_all(sent, 'row', 0, 0, tiled=True)  5.22 us
    ppermute x1, starting transfers between devices, body(): other_factors = lax.ppermute(factors, 'row', swap)  3.2 us
  transfers between devices with their start and end apart: 3, of which 2 were waited for; matrix products, arithmetic and copies ran while one was open for 1% of the time, Pallas kernels for 2%

profile of v10, /device:TPU:1, one launch (start us, length us, event | category | flops | bytes accessed | tf_op | source)
XLA Modules:
  0.0 75.8 jit_solution(18322113711794027958)
XLA Ops:
  0.0 3.2 %collective-permute-start.1 = (bf16[8,320,320]{2,1,0:T(8,128)(2,1)}, bf16[8,320,320]{2,1,0:T(8,128)(2,1)S(1)}, u32[]{:S(2)}, u32[]{:S(2)}) collective-permute-start(bf16[8,320,320]{2,1,0:T(8,128)(2,1)} %param.5), channel_id=1, source_target_pairs={{0,16},{16,0},{32,48},{48,32},{64,80},{80,64},{96,112},{112,96},{1... | collective-permute-start | bytes 4915208 | tf_op jit(solution)/shard_map/ppermute | solution.py:386
  3.2 0.0 copy-start
  3.2 0.7 copy-done
  3.9 0.9 %shard_map.46 = bf16[16,16,128]{2,1,0:T(8,128)(2,1)} custom-call(bf16[20,4,40]{2,1,0:T(4,128)(2,1)S(1)} %copy-done), custom_call_target="tpu_custom_call" | custom-call | tf_op jit(solution)/shard_map/pallas_call | solution.py:155
  4.8 6.9 %all-to-all-start = ((bf16[16,16,128]{2,1,0:T(8,128)(2,1)}), bf16[16,16,128]{2,1,0:T(8,128)(2,1)S(1)}, u32[]{:S(2)}, u32[]{:S(2)}) async-start(bf16[16,16,128]{2,1,0:T(8,128)(2,1)} %shard_map.46), calls=%async_computation | async-start | bytes 131072 | tf_op jit(solution)/shard_map/all_to_all | solution.py:390
  11.7 1.2 %collective-permute-start = (s32[1,4]{1,0:T(1,128)}, s32[1,4]{1,0:T(1,128)S(1)}, u32[]{:S(2)}, u32[]{:S(2)}) collective-permute-start(s32[1,4]{1,0:T(1,128)} %bitcast.5), channel_id=1, source_target_pairs={{0,1},{1,0},{2,3},{3,2},{4,5},{5,4},{6,7},{7,6},{8,9},{9,8},{10,11... | collective-permute-start | bytes 56 | tf_op jit(solution)/shard_map/ppermute | solution.py:387
  12.9 0.8 %pad_add_fusion = s32[324]{0:T(512)S(1)} fusion(s32[4]{0:T(128)} %param.7, s32[320]{0:T(512)} %param.6), kind=kLoop, calls=%fused_computation | loop fusion | flops 324 | bytes 2592 | tf_op jit(solution)/shard_map/concatenate | solution.py:384
  13.7 0.6 collective-permute-done.other_pair_ref
  14.2 5.2 %all-to-all-done.tall_ref = bf16[16,16,128]{2,1,0:T(8,128)(2,1)S(1)} async-done(((bf16[16,16,128]{2,1,0:T(8,128)(2,1)}), bf16[16,16,128]{2,1,0:T(8,128)(2,1)S(1)}, u32[]{:S(2)}, u32[]{:S(2)}) %all-to-all-start) | async-done | bytes 65568 | tf_op jit(solution)/shard_map/all_to_all | solution.py:390
  19.5 0.6 shard_map.47
  20.1 14.6 %all_to_all.20.t_ref = bf16[16,56,128]{2,1,0:T(8,128)(2,1)S(1)} all-to-all(bf16[16,56,128]{2,1,0:T(8,128)(2,1)S(1)} %shard_map.47), channel_id=1, replica_groups=mesh['row'=16,'col'=8,'pair'=2] {'col','pair'}, dimensions={0} | all-to-all | bytes 458752 | tf_op jit(solution)/shard_map/all_to_all | solution.py:394
  34.7 0.0 collective-permute-done.1
  34.7 15.6 %shard_map.48 = bf16[16,56,128]{2,1,0:T(8,128)(2,1)S(1)} custom-call(s32[1,4]{1,0:T(1,128)S(1)} %collective-permute-done.other_pair_ref, bf16[16,56,128]{2,1,0:T(8,128)(2,1)S(1)} %all_to_all.20.t_ref, bf16[2560,320]{1,0:T(8,128)(2,1)S(1)} %bitcast.3, bf16[2560,320]{1,0:T(8,128)(2,1)} %bitcast.4, s32[1,324]{1,0:T(1,128)S(1)} %broadcast_in_dim.7.label_ref), custom_call_target="tpu_custom_call" | custom-call | tf_op jit(solution)/shard_map/pallas_call | solution.py:355
  50.3 10.1 %all_to_all.21.pieces_ref = bf16[16,56,128]{2,1,0:T(8,128)(2,1)S(1)} all-to-all(bf16[16,56,128]{2,1,0:T(8,128)(2,1)S(1)} %shard_map.48), channel_id=1, replica_groups=mesh['row'=16,'col'=8,'pair'=2] {'col','pair'}, dimensions={0} | all-to-all | bytes 458752 | tf_op jit(solution)/shard_map/all_to_all | solution.py:396
  60.3 0.2 shard_map.49
  60.5 14.0 %all_to_all.22.finals_ref = f32[16,16,128]{2,1,0:T(8,128)S(1)} all-to-all(f32[16,16,128]{2,1,0:T(8,128)S(1)} %shard_map.49), channel_id=1, replica_groups=mesh['row'=16,'col'=8,'pair'=2] {'row'}, dimensions={0} | all-to-all | bytes 262144 | tf_op jit(solution)/shard_map/all_to_all | solution.py:398
  74.5 1.3 %shard_map.50 = f32[20,4,40]{2,1,0:T(4,128)} custom-call(f32[16,16,128]{2,1,0:T(8,128)S(1)} %all_to_all.22.finals_ref, s32[1,324]{1,0:T(1,128)S(1)} %broadcast_in_dim.7.label_ref), custom_call_target="tpu_custom_call" | custom-call | tf_op jit(solution)/shard_map/pallas_call | solution.py:236
  (1 shorter events, 0.0 us)
Async XLA Ops:
  0.0 34.7 %collective-permute-start.1 = (bf16[8,320,320]{2,1,0:T(8,128)(2,1)}, bf16[8,320,320]{2,1,0:T(8,128)(2,1)S(1)}, u32[]{:S(2)}, u32[]{:S(2)}) collective-permute-start(bf16[8,320,320]{2,1,0:T(8,128)(2,1)} %param.5), channel_id=1, source_target_pairs={{0,16},{16,0},{32,48},{48,32},{64,80},{80,64},{96,112},{112,96},{1... | collective-permute-start | bytes 4915208 | tf_op jit(solution)/shard_map/ppermute | solution.py:386
  3.2 0.7 copy-start
  4.8 14.7 %all-to-all-start = ((bf16[16,16,128]{2,1,0:T(8,128)(2,1)}), bf16[16,16,128]{2,1,0:T(8,128)(2,1)S(1)}, u32[]{:S(2)}, u32[]{:S(2)}) async-start(bf16[16,16,128]{2,1,0:T(8,128)(2,1)} %shard_map.46), calls=%async_computation | async-start | bytes 131072 | tf_op jit(solution)/shard_map/all_to_all | solution.py:390
  11.7 2.6 %collective-permute-start = (s32[1,4]{1,0:T(1,128)}, s32[1,4]{1,0:T(1,128)S(1)}, u32[]{:S(2)}, u32[]{:S(2)}) collective-permute-start(s32[1,4]{1,0:T(1,128)} %bitcast.5), channel_id=1, source_target_pairs={{0,1},{1,0},{2,3},{3,2},{4,5},{5,4},{6,7},{7,6},{8,9},{9,8},{10,11... | collective-permute-start | bytes 56 | tf_op jit(solution)/shard_map/ppermute | solution.py:387
